TPU v7x, 512 devices: a whole 4x4x16 slice. The times are simulated.
512 devices in a mesh: chain: 128 (over z, y, core), seg: 4 (over x).
Axes of the slice: x: 4, y: 4, z: 16, core: 2. Of those that a mesh axis runs over, the one named last changes fastest.
Arguments:
- band_tiles: bfloat16 [128, 1024, 7, 1024], P('chain', None, None, 'seg'), may hold values from -0.009765625 to 0.009765625
- widths: int32 [128], P('chain'), may hold values from 2 to 6, as said below
- warm_start: float32 [131072, 256], P(('chain', 'seg')), may hold values from -4 to 4
- scores: float32 [131072, 64], P(('chain', 'seg')), may hold values from -6 to 6
- penalty: float32 [256], replicated, may hold values from 0.05 to 0.5
Outputs:
- fitted_effects: float32 [131072, 256], P(('chain', 'seg'))
Inputs may be any that keep to these rules, and one draw needn't show every extreme that they name: `widths`: each block uses between 2 and 6 forward tiles; both 2 and 6 occur in every draw.
All inputs are finite; a program needn't handle non-finite values.
Results may differ from a plain program's by a relative error of at most 0.00085.
Values may be sent and summed in bfloat16 or wider, within the bound.
No kernel may reach another device: no remote copies, remote signals or barrier semaphores. Data moves between devices by JAX's collectives and lax.ppermute only.
A program may use at most 64 MiB of HBM per device.

v0:
```python
import jax
import jax.numpy as jnp
from jax import lax
from jax.sharding import PartitionSpec as P

ITERS = 2


step_size = 0.8


def shifted(value, axis, by):
    length = lax.axis_size(axis)
    pairs = [(i, i + by) for i in range(length) if 0 <= i + by < length]
    return lax.ppermute(value, axis, pairs)


def soft_limit(values, limit):
    return jnp.sign(values) * jnp.maximum(jnp.abs(values) - limit, 0.0)


def per_device(band_tiles, widths, warm_start, scores, penalty):
    local_tiles = band_tiles[0]
    block_len = local_tiles.shape[0]
    depth = local_tiles.shape[1]
    strip_len = local_tiles.shape[2]
    flat_tiles = local_tiles.reshape(block_len, depth * strip_len)
    columns = warm_start.shape[1]
    path_len = columns // scores.shape[1]
    target = jnp.tile(scores, (1, path_len))
    offsets = jnp.arange(depth, dtype=jnp.int32)
    live_flags = offsets <= widths[0]
    live_half = live_flags.astype(jnp.bfloat16)
    live_full = live_flags.astype(jnp.float32)
    estimate = warm_start
    for iteration in range(ITERS):
        current = estimate.astype(jnp.bfloat16)
        whole_block = lax.all_gather(current, "seg", axis=0, tiled=True)
        ahead_list = [current] + [
            shifted(current, "chain", -shift_by) for shift_by in range(1, depth)
        ]
        stacked = (jnp.stack(ahead_list) * live_half[:, None, None]).reshape(
            depth * strip_len, columns
        )

        def forward_term(start_row, count, stacked=stacked):
            return jnp.dot(flat_tiles, stacked, preferred_element_type=jnp.float32)

        forward = lax.psum_scatter(
            forward_term(jnp.int32(0), strip_len * lax.axis_size("seg")).astype(jnp.bfloat16),
            "seg",
            scatter_dimension=0,
            tiled=True,
        ).astype(jnp.float32)
        outgoing = lax.dot_general(
            flat_tiles, whole_block, (((0,), (0,)), ((), ())), preferred_element_type=jnp.float32
        )
        outgoing = outgoing.reshape(depth, strip_len, columns) * live_full[:, None, None]
        backward = outgoing[0]
        for shift_by in range(1, depth):
            backward = backward + shifted(
                outgoing[shift_by].astype(jnp.bfloat16), "chain", shift_by
            ).astype(jnp.float32)
        stepped = estimate - step_size * (estimate + (forward + backward) - target)
        estimate = soft_limit(stepped, step_size * penalty)
    return estimate


def solution(mesh):
    in_specs = (
        P("chain", None, None, "seg"),
        P("chain"),
        P(("chain", "seg"), None),
        P(("chain", "seg"), None),
        P(),
    )
    out_specs = P(("chain", "seg"), None)
    return jax.shard_map(
        per_device, mesh=mesh, in_specs=in_specs, out_specs=out_specs, check_vma=False
    )
```

profile of v0, /device:TPU:65, one launch (start us, length us, event | category | flops | bytes accessed | tf_op | source)
XLA Modules:
  0.0 180.1 jit_solution(8785533673903158669)
XLA Ops:
  6.5 1.1 copy.18
  7.7 2.7 %collective-permute-start.5 = (bf16[256,256]{0,1:T(8,128)(2,1)S(1)}, bf16[256,256]{0,1:T(8,128)(2,1)S(1)}, u32[]{:S(2)}, u32[]{:S(2)}) collective-permute-start(bf16[256,256]{0,1:T(8,128)(2,1)S(1)} %get-tuple-element.10), channel_id=1, source_target_pairs={{24,0},{28,4},{32,8},{36,12},{40,16},{44,20},{48,24},{52,28},{56,3... | collective-permute-start | bytes 393224 | tf_op jit(solution)/shard_map/ppermute | solution.py:15
  10.4 4.9 %collective-permute-start.4 = (bf16[256,256]{0,1:T(8,128)(2,1)S(1)}, bf16[256,256]{0,1:T(8,128)(2,1)S(1)}, u32[]{:S(2)}, u32[]{:S(2)}) collective-permute-start(bf16[256,256]{0,1:T(8,128)(2,1)S(1)} %get-tuple-element.10), channel_id=1, source_target_pairs={{20,0},{24,4},{28,8},{32,12},{36,16},{40,20},{44,24},{48,28},{52,3... | collective-permute-start | bytes 393224 | tf_op jit(solution)/shard_map/ppermute | solution.py:15
  15.3 2.3 %collective-permute-start.3 = (bf16[256,256]{0,1:T(8,128)(2,1)S(1)}, bf16[256,256]{0,1:T(8,128)(2,1)S(1)}, u32[]{:S(2)}, u32[]{:S(2)}) collective-permute-start(bf16[256,256]{0,1:T(8,128)(2,1)S(1)} %get-tuple-element.10), channel_id=1, source_target_pairs={{16,0},{20,4},{24,8},{28,12},{32,16},{36,20},{40,24},{44,28},{48,3... | collective-permute-start | bytes 393224 | tf_op jit(solution)/shard_map/ppermute | solution.py:15
  17.6 2.9 %collective-permute-start.2 = (bf16[256,256]{0,1:T(8,128)(2,1)S(1)}, bf16[256,256]{0,1:T(8,128)(2,1)S(1)}, u32[]{:S(2)}, u32[]{:S(2)}) collective-permute-start(bf16[256,256]{0,1:T(8,128)(2,1)S(1)} %get-tuple-element.10), channel_id=1, source_target_pairs={{12,0},{16,4},{20,8},{24,12},{28,16},{32,20},{36,24},{40,28},{44,3... | collective-permute-start | bytes 393224 | tf_op jit(solution)/shard_map/ppermute | solution.py:15
  20.5 2.0 %collective-permute-start = (bf16[256,256]{0,1:T(8,128)(2,1)S(1)}, bf16[256,256]{0,1:T(8,128)(2,1)S(1)}, u32[]{:S(2)}, u32[]{:S(2)}) collective-permute-start(bf16[256,256]{0,1:T(8,128)(2,1)S(1)} %get-tuple-element.10), channel_id=1, source_target_pairs={{4,0},{8,4},{12,8},{16,12},{20,16},{24,20},{28,24},{32,28},{36,32}... | collective-permute-start | bytes 393224 | tf_op jit(solution)/shard_map/ppermute | solution.py:15
  22.5 10.2 %all_gather.6 = bf16[1024,256]{0,1:T(8,128)(2,1)S(1)} all-gather(bf16[256,256]{0,1:T(8,128)(2,1)S(1)} %get-tuple-element.10), channel_id=1, replica_groups=mesh['chain'=128,'seg'=4] {'seg'}, dimensions={0}, use_global_device_ids=true | all-gather | bytes 655360 | tf_op jit(solution)/shard_map/all_gather | solution.py:38
  33.4 6.1 %copy.14 = bf16[1,1024,7,256]{1,3,2,0:T(8,128)(2,1)} copy(bf16[1,1024,7,256]{3,1,2,0:T(8,128)(2,1)} %param.5) | data formatting | bytes 7340032 | tf_op args[0]
  39.5 8.1 %collective-permute-start.1 = (bf16[256,256]{0,1:T(8,128)(2,1)S(1)}, bf16[256,256]{0,1:T(8,128)(2,1)S(1)}, u32[]{:S(2)}, u32[]{:S(2)}) collective-permute-start(bf16[256,256]{0,1:T(8,128)(2,1)S(1)} %get-tuple-element.10), channel_id=1, source_target_pairs={{8,0},{12,4},{16,8},{20,12},{24,16},{28,20},{32,24},{36,28},{40,32... | collective-permute-start | bytes 393224 | tf_op jit(solution)/shard_map/ppermute | solution.py:15
  47.7 2.9 %collective-permute-done.1 = bf16[256,256]{0,1:T(8,128)(2,1)S(1)} collective-permute-done((bf16[256,256]{0,1:T(8,128)(2,1)S(1)}, bf16[256,256]{0,1:T(8,128)(2,1)S(1)}, u32[]{:S(2)}, u32[]{:S(2)}) %collective-permute-start.1) | collective-permute-done | bytes 131104 | tf_op jit(solution)/shard_map/ppermute | solution.py:15
  50.6 0.0 collective-permute-done.2
  50.6 0.0 collective-permute-done.3
  50.7 0.1 broadcast_multiply_fusion.2
  50.8 0.6 copy.13
  51.4 4.0 %fusion.5 = bf16[1024,256]{0,1:T(8,128)(2,1)} fusion(bf16[1792,256]{1,0:T(8,128)(2,1)S(1)} %bitcast.149, bf16[1024,1792]{0,1:T(8,128)(2,1)} %bitcast.145), kind=kOutput, calls=%fused_computation.6 | convolution fusion | flops 939786240 | bytes 5111808 | tf_op jit(solution)/shard_map/dot_general | solution.py:47
  55.4 0.0 reduce-scatter.3.cloned.1.call-update
  55.4 0.0 reduce-scatter.5.cloned.1.call-start
  55.5 0.0 copy-start.1
  55.5 0.0 copy-start
  55.5 3.2 %fusion.29 = (bf16[7,256,256]{1,2,0:T(8,128)(2,1)S(1)}, f32[7,256,256]{1,2,0:T(8,128)S(1)}) fusion(f32[7]{0:T(128)S(1)} %compare_convert_fusion, bf16[1024,256]{0,1:T(8,128)(2,1)S(1)} %all_gather.6, bf16[1,1024,7,256]{1,3,2,0:T(8,128)(2,1)} %copy.14), kind=kOutput, calls=%fused_computation.68 | convolution fusion | flops 940441600 | bytes 6946844 | tf_op jit(solution)/shard_map/dot_general | solution.py:55
  58.8 0.1 slice_bitcast_fusion.13
  58.8 7.5 %collective-permute-start.6 = (bf16[256,256]{0,1:T(8,128)(2,1)S(1)}, bf16[256,256]{0,1:T(8,128)(2,1)S(1)}, u32[]{:S(2)}, u32[]{:S(2)}) collective-permute-start(bf16[256,256]{0,1:T(8,128)(2,1)S(1)} %get-tuple-element.17), channel_id=1, source_target_pairs={{0,4},{4,8},{8,12},{12,16},{16,20},{20,24},{24,28},{28,32},{32,36}... | collective-permute-start | bytes 393224 | tf_op jit(solution)/shard_map/ppermute | solution.py:15
  66.3 1.9 %collective-permute-start.11 = (bf16[256,256]{0,1:T(8,128)(2,1)S(1)}, bf16[256,256]{0,1:T(8,128)(2,1)S(1)}, u32[]{:S(2)}, u32[]{:S(2)}) collective-permute-start(bf16[256,256]{0,1:T(8,128)(2,1)S(1)} %get-tuple-element.18), channel_id=1, source_target_pairs={{0,24},{4,28},{8,32},{12,36},{16,40},{20,44},{24,48},{28,52},{32,5... | collective-permute-start | bytes 393224 | tf_op jit(solution)/shard_map/ppermute | solution.py:15
  68.2 1.9 %collective-permute-start.10 = (bf16[256,256]{0,1:T(8,128)(2,1)S(1)}, bf16[256,256]{0,1:T(8,128)(2,1)S(1)}, u32[]{:S(2)}, u32[]{:S(2)}) collective-permute-start(bf16[256,256]{0,1:T(8,128)(2,1)S(1)} %get-tuple-element.19), channel_id=1, source_target_pairs={{0,20},{4,24},{8,28},{12,32},{16,36},{20,40},{24,44},{28,48},{32,5... | collective-permute-start | bytes 393224 | tf_op jit(solution)/shard_map/ppermute | solution.py:15
  70.2 4.1 %collective-permute-start.9 = (bf16[256,256]{0,1:T(8,128)(2,1)S(1)}, bf16[256,256]{0,1:T(8,128)(2,1)S(1)}, u32[]{:S(2)}, u32[]{:S(2)}) collective-permute-start(bf16[256,256]{0,1:T(8,128)(2,1)S(1)} %get-tuple-element.20), channel_id=1, source_target_pairs={{0,16},{4,20},{8,24},{12,28},{16,32},{20,36},{24,40},{28,44},{32,4... | collective-permute-start | bytes 393224 | tf_op jit(solution)/shard_map/ppermute | solution.py:15
  74.3 5.4 %collective-permute-start.8 = (bf16[256,256]{0,1:T(8,128)(2,1)S(1)}, bf16[256,256]{0,1:T(8,128)(2,1)S(1)}, u32[]{:S(2)}, u32[]{:S(2)}) collective-permute-start(bf16[256,256]{0,1:T(8,128)(2,1)S(1)} %get-tuple-element.21), channel_id=1, source_target_pairs={{0,12},{4,16},{8,20},{12,24},{16,28},{20,32},{24,36},{28,40},{32,4... | collective-permute-start | bytes 393224 | tf_op jit(solution)/shard_map/ppermute | solution.py:15
  79.6 4.1 %collective-permute-start.7 = (bf16[256,256]{0,1:T(8,128)(2,1)S(1)}, bf16[256,256]{0,1:T(8,128)(2,1)S(1)}, u32[]{:S(2)}, u32[]{:S(2)}) collective-permute-start(bf16[256,256]{0,1:T(8,128)(2,1)S(1)} %get-tuple-element.22), channel_id=1, source_target_pairs={{0,8},{4,12},{8,16},{12,20},{16,24},{20,28},{24,32},{28,36},{32,40... | collective-permute-start | bytes 393224 | tf_op jit(solution)/shard_map/ppermute | solution.py:15
  83.8 0.0 collective-permute-done.11
  83.8 0.0 collective-permute-done.9
  83.8 1.5 collective-permute-done.8
  85.3 3.4 %collective-permute-done.7 = bf16[256,256]{0,1:T(8,128)(2,1)S(1)} collective-permute-done((bf16[256,256]{0,1:T(8,128)(2,1)S(1)}, bf16[256,256]{0,1:T(8,128)(2,1)S(1)}, u32[]{:S(2)}, u32[]{:S(2)}) %collective-permute-start.7) | collective-permute-done | bytes 131104 | tf_op jit(solution)/shard_map/ppermute | solution.py:15
  88.7 1.2 bitcast_dynamic-update-slice_fusion.6
  89.9 2.6 %collective-permute-start.17 = (bf16[256,256]{0,1:T(8,128)(2,1)S(1)}, bf16[256,256]{0,1:T(8,128)(2,1)S(1)}, u32[]{:S(2)}, u32[]{:S(2)}) collective-permute-start(bf16[256,256]{0,1:T(8,128)(2,1)S(1)} %get-tuple-element.6), channel_id=1, source_target_pairs={{24,0},{28,4},{32,8},{36,12},{40,16},{44,20},{48,24},{52,28},{56,3... | collective-permute-start | bytes 393224 | tf_op jit(solution)/shard_map/ppermute | solution.py:15
  92.6 7.3 %collective-permute-start.16 = (bf16[256,256]{0,1:T(8,128)(2,1)S(1)}, bf16[256,256]{0,1:T(8,128)(2,1)S(1)}, u32[]{:S(2)}, u32[]{:S(2)}) collective-permute-start(bf16[256,256]{0,1:T(8,128)(2,1)S(1)} %get-tuple-element.6), channel_id=1, source_target_pairs={{20,0},{24,4},{28,8},{32,12},{36,16},{40,20},{44,24},{48,28},{52,3... | collective-permute-start | bytes 393224 | tf_op jit(solution)/shard_map/ppermute | solution.py:15
  99.9 2.5 %collective-permute-start.15 = (bf16[256,256]{0,1:T(8,128)(2,1)S(1)}, bf16[256,256]{0,1:T(8,128)(2,1)S(1)}, u32[]{:S(2)}, u32[]{:S(2)}) collective-permute-start(bf16[256,256]{0,1:T(8,128)(2,1)S(1)} %get-tuple-element.6), channel_id=1, source_target_pairs={{16,0},{20,4},{24,8},{28,12},{32,16},{36,20},{40,24},{44,28},{48,3... | collective-permute-start | bytes 393224 | tf_op jit(solution)/shard_map/ppermute | solution.py:15
  102.4 2.9 %collective-permute-start.14 = (bf16[256,256]{0,1:T(8,128)(2,1)S(1)}, bf16[256,256]{0,1:T(8,128)(2,1)S(1)}, u32[]{:S(2)}, u32[]{:S(2)}) collective-permute-start(bf16[256,256]{0,1:T(8,128)(2,1)S(1)} %get-tuple-element.6), channel_id=1, source_target_pairs={{12,0},{16,4},{20,8},{24,12},{28,16},{32,20},{36,24},{40,28},{44,3... | collective-permute-start | bytes 393224 | tf_op jit(solution)/shard_map/ppermute | solution.py:15
  105.3 2.0 %collective-permute-start.12 = (bf16[256,256]{0,1:T(8,128)(2,1)S(1)}, bf16[256,256]{0,1:T(8,128)(2,1)S(1)}, u32[]{:S(2)}, u32[]{:S(2)}) collective-permute-start(bf16[256,256]{0,1:T(8,128)(2,1)S(1)} %get-tuple-element.6), channel_id=1, source_target_pairs={{4,0},{8,4},{12,8},{16,12},{20,16},{24,20},{28,24},{32,28},{36,32}... | collective-permute-start | bytes 393224 | tf_op jit(solution)/shard_map/ppermute | solution.py:15
  107.3 9.9 %all_gather.7 = bf16[1024,256]{0,1:T(8,128)(2,1)S(1)} all-gather(bf16[256,256]{0,1:T(8,128)(2,1)S(1)} %get-tuple-element.6), channel_id=1, replica_groups=mesh['chain'=128,'seg'=4] {'seg'}, dimensions={0}, use_global_device_ids=true | all-gather | bytes 655360 | tf_op jit(solution)/shard_map/all_gather | solution.py:38
  117.2 0.0 collective-permute-done.12
  117.2 3.2 %collective-permute-start.13 = (bf16[256,256]{0,1:T(8,128)(2,1)S(1)}, bf16[256,256]{0,1:T(8,128)(2,1)S(1)}, u32[]{:S(2)}, u32[]{:S(2)}) collective-permute-start(bf16[256,256]{0,1:T(8,128)(2,1)S(1)} %get-tuple-element.6), channel_id=1, source_target_pairs={{8,0},{12,4},{16,8},{20,12},{24,16},{28,20},{32,24},{36,28},{40,32... | collective-permute-start | bytes 393224 | tf_op jit(solution)/shard_map/ppermute | solution.py:15
  120.5 2.5 %collective-permute-done.13 = bf16[256,256]{0,1:T(8,128)(2,1)S(1)} collective-permute-done((bf16[256,256]{0,1:T(8,128)(2,1)S(1)}, bf16[256,256]{0,1:T(8,128)(2,1)S(1)}, u32[]{:S(2)}, u32[]{:S(2)}) %collective-permute-start.13) | collective-permute-done | bytes 131104 | tf_op jit(solution)/shard_map/ppermute | solution.py:15
  123.0 0.0 collective-permute-done.15
  123.0 0.0 collective-permute-done.16
  123.1 0.1 broadcast_multiply_fusion.1
  123.2 0.6 copy.19
  123.8 4.0 %fusion.6 = bf16[1024,256]{0,1:T(8,128)(2,1)} fusion(bf16[1792,256]{1,0:T(8,128)(2,1)S(1)} %bitcast.150, bf16[1024,1792]{0,1:T(8,128)(2,1)} %bitcast.146), kind=kOutput, calls=%fused_computation.7 | convolution fusion | flops 939786240 | bytes 5111808 | tf_op jit(solution)/shard_map/dot_general | solution.py:47
  127.8 0.0 reduce-scatter.5.cloned.1.call-update
  127.8 3.2 %convolution_bitcast_fusion = f32[1792,256]{0,1:T(8,128)S(1)} fusion(bf16[1024,256]{0,1:T(8,128)(2,1)S(1)} %all_gather.7, bf16[1024,1792]{0,1:T(8,128)(2,1)} %bitcast.147), kind=kOutput, calls=%fused_computation.2 | convolution fusion | flops 939524096 | bytes 6029312 | tf_op jit(solution)/shard_map/dot_general | solution.py:55
  131.0 1.7 copy.20
  132.7 1.8 %copy.21 = f32[7,256,256]{1,2,0:T(8,128)S(1)} copy(f32[7,256,256]{2,1,0:T(8,128)} %bitcast.148) | data formatting | bytes 3670016 | tf_op jit(solution)/shard_map/reshape | solution.py:58
  134.6 1.6 fusion.28
  136.1 0.1 slice_bitcast_fusion.7
  136.2 8.0 %collective-permute-start.18 = (bf16[256,256]{0,1:T(8,128)(2,1)S(1)}, bf16[256,256]{0,1:T(8,128)(2,1)S(1)}, u32[]{:S(2)}, u32[]{:S(2)}) collective-permute-start(bf16[256,256]{0,1:T(8,128)(2,1)S(1)} %get-tuple-element.11), channel_id=1, source_target_pairs={{0,4},{4,8},{8,12},{12,16},{16,20},{20,24},{24,28},{28,32},{32,36}... | collective-permute-start | bytes 393224 | tf_op jit(solution)/shard_map/ppermute | solution.py:15
  144.2 5.8 %collective-permute-start.23 = (bf16[256,256]{0,1:T(8,128)(2,1)S(1)}, bf16[256,256]{0,1:T(8,128)(2,1)S(1)}, u32[]{:S(2)}, u32[]{:S(2)}) collective-permute-start(bf16[256,256]{0,1:T(8,128)(2,1)S(1)} %get-tuple-element.12), channel_id=1, source_target_pairs={{0,24},{4,28},{8,32},{12,36},{16,40},{20,44},{24,48},{28,52},{32,5... | collective-permute-start | bytes 393224 | tf_op jit(solution)/shard_map/ppermute | solution.py:15
  150.0 1.9 %collective-permute-start.22 = (bf16[256,256]{0,1:T(8,128)(2,1)S(1)}, bf16[256,256]{0,1:T(8,128)(2,1)S(1)}, u32[]{:S(2)}, u32[]{:S(2)}) collective-permute-start(bf16[256,256]{0,1:T(8,128)(2,1)S(1)} %get-tuple-element.13), channel_id=1, source_target_pairs={{0,20},{4,24},{8,28},{12,32},{16,36},{20,40},{24,44},{28,48},{32,5... | collective-permute-start | bytes 393224 | tf_op jit(solution)/shard_map/ppermute | solution.py:15
  151.9 4.9 %collective-permute-start.21 = (bf16[256,256]{0,1:T(8,128)(2,1)S(1)}, bf16[256,256]{0,1:T(8,128)(2,1)S(1)}, u32[]{:S(2)}, u32[]{:S(2)}) collective-permute-start(bf16[256,256]{0,1:T(8,128)(2,1)S(1)} %get-tuple-element.14), channel_id=1, source_target_pairs={{0,16},{4,20},{8,24},{12,28},{16,32},{20,36},{24,40},{28,44},{32,4... | collective-permute-start | bytes 393224 | tf_op jit(solution)/shard_map/ppermute | solution.py:15
  156.8 5.6 %collective-permute-start.20 = (bf16[256,256]{0,1:T(8,128)(2,1)S(1)}, bf16[256,256]{0,1:T(8,128)(2,1)S(1)}, u32[]{:S(2)}, u32[]{:S(2)}) collective-permute-start(bf16[256,256]{0,1:T(8,128)(2,1)S(1)} %get-tuple-element.15), channel_id=1, source_target_pairs={{0,12},{4,16},{8,20},{12,24},{16,28},{20,32},{24,36},{28,40},{32,4... | collective-permute-start | bytes 393224 | tf_op jit(solution)/shard_map/ppermute | solution.py:15
  162.5 0.0 collective-permute-done.18
  162.5 3.8 %collective-permute-start.19 = (bf16[256,256]{0,1:T(8,128)(2,1)S(1)}, bf16[256,256]{0,1:T(8,128)(2,1)S(1)}, u32[]{:S(2)}, u32[]{:S(2)}) collective-permute-start(bf16[256,256]{0,1:T(8,128)(2,1)S(1)} %get-tuple-element.16), channel_id=1, source_target_pairs={{0,8},{4,12},{8,16},{12,20},{16,24},{20,28},{24,32},{28,36},{32,40... | collective-permute-start | bytes 393224 | tf_op jit(solution)/shard_map/ppermute | solution.py:15
  166.2 0.0 collective-permute-done.22
  166.3 1.9 %collective-permute-done.20 = bf16[256,256]{0,1:T(8,128)(2,1)S(1)} collective-permute-done((bf16[256,256]{0,1:T(8,128)(2,1)S(1)}, bf16[256,256]{0,1:T(8,128)(2,1)S(1)}, u32[]{:S(2)}, u32[]{:S(2)}) %collective-permute-start.20) | collective-permute-done | bytes 131104 | tf_op jit(solution)/shard_map/ppermute | solution.py:15
  168.1 3.1 %collective-permute-done.19 = bf16[256,256]{0,1:T(8,128)(2,1)S(1)} collective-permute-done((bf16[256,256]{0,1:T(8,128)(2,1)S(1)}, bf16[256,256]{0,1:T(8,128)(2,1)S(1)}, u32[]{:S(2)}, u32[]{:S(2)}) %collective-permute-start.19) | collective-permute-done | bytes 131104 | tf_op jit(solution)/shard_map/ppermute | solution.py:15
  171.2 1.2 maximum_multiply_fusion
  172.5 0.8 copy.22
  (30 shorter events, 0.2 us)
Async XLA Ops:
  6.5 82.2 %reduce-scatter.3.cloned.1.call-start = ((), (), s32[]{:S(2)}) async-start(), calls=%async_computation.2 | async-start | bytes 655360 | tf_op jit(solution)/shard_map/reduce_scatter | solution.py:49
  7.7 43.0 %collective-permute-start.5 = (bf16[256,256]{0,1:T(8,128)(2,1)S(1)}, bf16[256,256]{0,1:T(8,128)(2,1)S(1)}, u32[]{:S(2)}, u32[]{:S(2)}) collective-permute-start(bf16[256,256]{0,1:T(8,128)(2,1)S(1)} %get-tuple-element.10), channel_id=1, source_target_pairs={{24,0},{28,4},{32,8},{36,12},{40,16},{44,20},{48,24},{52,28},{56,3... | collective-permute-start | bytes 393224 | tf_op jit(solution)/shard_map/ppermute | solution.py:15
  10.4 40.2 %collective-permute-start.4 = (bf16[256,256]{0,1:T(8,128)(2,1)S(1)}, bf16[256,256]{0,1:T(8,128)(2,1)S(1)}, u32[]{:S(2)}, u32[]{:S(2)}) collective-permute-start(bf16[256,256]{0,1:T(8,128)(2,1)S(1)} %get-tuple-element.10), channel_id=1, source_target_pairs={{20,0},{24,4},{28,8},{32,12},{36,16},{40,20},{44,24},{48,28},{52,3... | collective-permute-start | bytes 393224 | tf_op jit(solution)/shard_map/ppermute | solution.py:15
  15.3 35.3 %collective-permute-start.3 = (bf16[256,256]{0,1:T(8,128)(2,1)S(1)}, bf16[256,256]{0,1:T(8,128)(2,1)S(1)}, u32[]{:S(2)}, u32[]{:S(2)}) collective-permute-start(bf16[256,256]{0,1:T(8,128)(2,1)S(1)} %get-tuple-element.10), channel_id=1, source_target_pairs={{16,0},{20,4},{24,8},{28,12},{32,16},{36,20},{40,24},{44,28},{48,3... | collective-permute-start | bytes 393224 | tf_op jit(solution)/shard_map/ppermute | solution.py:15
  17.6 33.0 %collective-permute-start.2 = (bf16[256,256]{0,1:T(8,128)(2,1)S(1)}, bf16[256,256]{0,1:T(8,128)(2,1)S(1)}, u32[]{:S(2)}, u32[]{:S(2)}) collective-permute-start(bf16[256,256]{0,1:T(8,128)(2,1)S(1)} %get-tuple-element.10), channel_id=1, source_target_pairs={{12,0},{16,4},{20,8},{24,12},{28,16},{32,20},{36,24},{40,28},{44,3... | collective-permute-start | bytes 393224 | tf_op jit(solution)/shard_map/ppermute | solution.py:15
  20.5 19.0 %collective-permute-start = (bf16[256,256]{0,1:T(8,128)(2,1)S(1)}, bf16[256,256]{0,1:T(8,128)(2,1)S(1)}, u32[]{:S(2)}, u32[]{:S(2)}) collective-permute-start(bf16[256,256]{0,1:T(8,128)(2,1)S(1)} %get-tuple-element.10), channel_id=1, source_target_pairs={{4,0},{8,4},{12,8},{16,12},{20,16},{24,20},{28,24},{32,28},{36,32}... | collective-permute-start | bytes 393224 | tf_op jit(solution)/shard_map/ppermute | solution.py:15
  39.5 11.0 %collective-permute-start.1 = (bf16[256,256]{0,1:T(8,128)(2,1)S(1)}, bf16[256,256]{0,1:T(8,128)(2,1)S(1)}, u32[]{:S(2)}, u32[]{:S(2)}) collective-permute-start(bf16[256,256]{0,1:T(8,128)(2,1)S(1)} %get-tuple-element.10), channel_id=1, source_target_pairs={{8,0},{12,4},{16,8},{20,12},{24,16},{28,20},{32,24},{36,28},{40,32... | collective-permute-start | bytes 393224 | tf_op jit(solution)/shard_map/ppermute | solution.py:15
  55.4 115.8 %reduce-scatter.5.cloned.1.call-start = ((), (), s32[]{:S(2)}) async-start(), calls=%async_computation.3 | async-start | bytes 655360 | tf_op jit(solution)/shard_map/reduce_scatter | solution.py:49
  55.5 28.3 %copy-start.1 = (f32[256]{0:T(256)S(1)}, f32[256]{0:T(256)}, u32[]{:S(2)}) copy-start(f32[256]{0:T(256)} %param.9) | copy-start | bytes 3076
  55.5 33.2 %copy-start = (f32[256,64]{0,1:T(8,128)S(1)}, f32[256,64]{0,1:T(8,128)}, u32[]{:S(2)}) copy-start(f32[256,64]{0,1:T(8,128)} %param.8) | copy-start | bytes 196612
  58.8 20.8 %collective-permute-start.6 = (bf16[256,256]{0,1:T(8,128)(2,1)S(1)}, bf16[256,256]{0,1:T(8,128)(2,1)S(1)}, u32[]{:S(2)}, u32[]{:S(2)}) collective-permute-start(bf16[256,256]{0,1:T(8,128)(2,1)S(1)} %get-tuple-element.17), channel_id=1, source_target_pairs={{0,4},{4,8},{8,12},{12,16},{16,20},{20,24},{24,28},{28,32},{32,36}... | collective-permute-start | bytes 393224 | tf_op jit(solution)/shard_map/ppermute | solution.py:15
  66.3 17.5 %collective-permute-start.11 = (bf16[256,256]{0,1:T(8,128)(2,1)S(1)}, bf16[256,256]{0,1:T(8,128)(2,1)S(1)}, u32[]{:S(2)}, u32[]{:S(2)}) collective-permute-start(bf16[256,256]{0,1:T(8,128)(2,1)S(1)} %get-tuple-element.18), channel_id=1, source_target_pairs={{0,24},{4,28},{8,32},{12,36},{16,40},{20,44},{24,48},{28,52},{32,5... | collective-permute-start | bytes 393224 | tf_op jit(solution)/shard_map/ppermute | solution.py:15
  68.2 15.6 %collective-permute-start.10 = (bf16[256,256]{0,1:T(8,128)(2,1)S(1)}, bf16[256,256]{0,1:T(8,128)(2,1)S(1)}, u32[]{:S(2)}, u32[]{:S(2)}) collective-permute-start(bf16[256,256]{0,1:T(8,128)(2,1)S(1)} %get-tuple-element.19), channel_id=1, source_target_pairs={{0,20},{4,24},{8,28},{12,32},{16,36},{20,40},{24,44},{28,48},{32,5... | collective-permute-start | bytes 393224 | tf_op jit(solution)/shard_map/ppermute | solution.py:15
  70.2 13.6 %collective-permute-start.9 = (bf16[256,256]{0,1:T(8,128)(2,1)S(1)}, bf16[256,256]{0,1:T(8,128)(2,1)S(1)}, u32[]{:S(2)}, u32[]{:S(2)}) collective-permute-start(bf16[256,256]{0,1:T(8,128)(2,1)S(1)} %get-tuple-element.20), channel_id=1, source_target_pairs={{0,16},{4,20},{8,24},{12,28},{16,32},{20,36},{24,40},{28,44},{32,4... | collective-permute-start | bytes 393224 | tf_op jit(solution)/shard_map/ppermute | solution.py:15
  74.3 11.0 %collective-permute-start.8 = (bf16[256,256]{0,1:T(8,128)(2,1)S(1)}, bf16[256,256]{0,1:T(8,128)(2,1)S(1)}, u32[]{:S(2)}, u32[]{:S(2)}) collective-permute-start(bf16[256,256]{0,1:T(8,128)(2,1)S(1)} %get-tuple-element.21), channel_id=1, source_target_pairs={{0,12},{4,16},{8,20},{12,24},{16,28},{20,32},{24,36},{28,40},{32,4... | collective-permute-start | bytes 393224 | tf_op jit(solution)/shard_map/ppermute | solution.py:15
  79.6 9.1 %collective-permute-start.7 = (bf16[256,256]{0,1:T(8,128)(2,1)S(1)}, bf16[256,256]{0,1:T(8,128)(2,1)S(1)}, u32[]{:S(2)}, u32[]{:S(2)}) collective-permute-start(bf16[256,256]{0,1:T(8,128)(2,1)S(1)} %get-tuple-element.22), channel_id=1, source_target_pairs={{0,8},{4,12},{8,16},{12,20},{16,24},{20,28},{24,32},{28,36},{32,40... | collective-permute-start | bytes 393224 | tf_op jit(solution)/shard_map/ppermute | solution.py:15
  89.9 33.1 %collective-permute-start.17 = (bf16[256,256]{0,1:T(8,128)(2,1)S(1)}, bf16[256,256]{0,1:T(8,128)(2,1)S(1)}, u32[]{:S(2)}, u32[]{:S(2)}) collective-permute-start(bf16[256,256]{0,1:T(8,128)(2,1)S(1)} %get-tuple-element.6), channel_id=1, source_target_pairs={{24,0},{28,4},{32,8},{36,12},{40,16},{44,20},{48,24},{52,28},{56,3... | collective-permute-start | bytes 393224 | tf_op jit(solution)/shard_map/ppermute | solution.py:15
  92.6 30.5 %collective-permute-start.16 = (bf16[256,256]{0,1:T(8,128)(2,1)S(1)}, bf16[256,256]{0,1:T(8,128)(2,1)S(1)}, u32[]{:S(2)}, u32[]{:S(2)}) collective-permute-start(bf16[256,256]{0,1:T(8,128)(2,1)S(1)} %get-tuple-element.6), channel_id=1, source_target_pairs={{20,0},{24,4},{28,8},{32,12},{36,16},{40,20},{44,24},{48,28},{52,3... | collective-permute-start | bytes 393224 | tf_op jit(solution)/shard_map/ppermute | solution.py:15
  99.9 23.1 %collective-permute-start.15 = (bf16[256,256]{0,1:T(8,128)(2,1)S(1)}, bf16[256,256]{0,1:T(8,128)(2,1)S(1)}, u32[]{:S(2)}, u32[]{:S(2)}) collective-permute-start(bf16[256,256]{0,1:T(8,128)(2,1)S(1)} %get-tuple-element.6), channel_id=1, source_target_pairs={{16,0},{20,4},{24,8},{28,12},{32,16},{36,20},{40,24},{44,28},{48,3... | collective-permute-start | bytes 393224 | tf_op jit(solution)/shard_map/ppermute | solution.py:15
  102.4 20.6 %collective-permute-start.14 = (bf16[256,256]{0,1:T(8,128)(2,1)S(1)}, bf16[256,256]{0,1:T(8,128)(2,1)S(1)}, u32[]{:S(2)}, u32[]{:S(2)}) collective-permute-start(bf16[256,256]{0,1:T(8,128)(2,1)S(1)} %get-tuple-element.6), channel_id=1, source_target_pairs={{12,0},{16,4},{20,8},{24,12},{28,16},{32,20},{36,24},{40,28},{44,3... | collective-permute-start | bytes 393224 | tf_op jit(solution)/shard_map/ppermute | solution.py:15
  105.3 11.9 %collective-permute-start.12 = (bf16[256,256]{0,1:T(8,128)(2,1)S(1)}, bf16[256,256]{0,1:T(8,128)(2,1)S(1)}, u32[]{:S(2)}, u32[]{:S(2)}) collective-permute-start(bf16[256,256]{0,1:T(8,128)(2,1)S(1)} %get-tuple-element.6), channel_id=1, source_target_pairs={{4,0},{8,4},{12,8},{16,12},{20,16},{24,20},{28,24},{32,28},{36,32}... | collective-permute-start | bytes 393224 | tf_op jit(solution)/shard_map/ppermute | solution.py:15
  117.2 5.7 %collective-permute-start.13 = (bf16[256,256]{0,1:T(8,128)(2,1)S(1)}, bf16[256,256]{0,1:T(8,128)(2,1)S(1)}, u32[]{:S(2)}, u32[]{:S(2)}) collective-permute-start(bf16[256,256]{0,1:T(8,128)(2,1)S(1)} %get-tuple-element.6), channel_id=1, source_target_pairs={{8,0},{12,4},{16,8},{20,12},{24,16},{28,20},{32,24},{36,28},{40,32... | collective-permute-start | bytes 393224 | tf_op jit(solution)/shard_map/ppermute | solution.py:15
  136.2 26.3 %collective-permute-start.18 = (bf16[256,256]{0,1:T(8,128)(2,1)S(1)}, bf16[256,256]{0,1:T(8,128)(2,1)S(1)}, u32[]{:S(2)}, u32[]{:S(2)}) collective-permute-start(bf16[256,256]{0,1:T(8,128)(2,1)S(1)} %get-tuple-element.11), channel_id=1, source_target_pairs={{0,4},{4,8},{8,12},{12,16},{16,20},{20,24},{24,28},{28,32},{32,36}... | collective-permute-start | bytes 393224 | tf_op jit(solution)/shard_map/ppermute | solution.py:15
  144.2 22.0 %collective-permute-start.23 = (bf16[256,256]{0,1:T(8,128)(2,1)S(1)}, bf16[256,256]{0,1:T(8,128)(2,1)S(1)}, u32[]{:S(2)}, u32[]{:S(2)}) collective-permute-start(bf16[256,256]{0,1:T(8,128)(2,1)S(1)} %get-tuple-element.12), channel_id=1, source_target_pairs={{0,24},{4,28},{8,32},{12,36},{16,40},{20,44},{24,48},{28,52},{32,5... | collective-permute-start | bytes 393224 | tf_op jit(solution)/shard_map/ppermute | solution.py:15
  150.0 16.3 %collective-permute-start.22 = (bf16[256,256]{0,1:T(8,128)(2,1)S(1)}, bf16[256,256]{0,1:T(8,128)(2,1)S(1)}, u32[]{:S(2)}, u32[]{:S(2)}) collective-permute-start(bf16[256,256]{0,1:T(8,128)(2,1)S(1)} %get-tuple-element.13), channel_id=1, source_target_pairs={{0,20},{4,24},{8,28},{12,32},{16,36},{20,40},{24,44},{28,48},{32,5... | collective-permute-start | bytes 393224 | tf_op jit(solution)/shard_map/ppermute | solution.py:15
  151.9 14.3 %collective-permute-start.21 = (bf16[256,256]{0,1:T(8,128)(2,1)S(1)}, bf16[256,256]{0,1:T(8,128)(2,1)S(1)}, u32[]{:S(2)}, u32[]{:S(2)}) collective-permute-start(bf16[256,256]{0,1:T(8,128)(2,1)S(1)} %get-tuple-element.14), channel_id=1, source_target_pairs={{0,16},{4,20},{8,24},{12,28},{16,32},{20,36},{24,40},{28,44},{32,4... | collective-permute-start | bytes 393224 | tf_op jit(solution)/shard_map/ppermute | solution.py:15
  156.8 11.3 %collective-permute-start.20 = (bf16[256,256]{0,1:T(8,128)(2,1)S(1)}, bf16[256,256]{0,1:T(8,128)(2,1)S(1)}, u32[]{:S(2)}, u32[]{:S(2)}) collective-permute-start(bf16[256,256]{0,1:T(8,128)(2,1)S(1)} %get-tuple-element.15), channel_id=1, source_target_pairs={{0,12},{4,16},{8,20},{12,24},{16,28},{20,32},{24,36},{28,40},{32,4... | collective-permute-start | bytes 393224 | tf_op jit(solution)/shard_map/ppermute | solution.py:15
  162.5 8.7 %collective-permute-start.19 = (bf16[256,256]{0,1:T(8,128)(2,1)S(1)}, bf16[256,256]{0,1:T(8,128)(2,1)S(1)}, u32[]{:S(2)}, u32[]{:S(2)}) collective-permute-start(bf16[256,256]{0,1:T(8,128)(2,1)S(1)} %get-tuple-element.16), channel_id=1, source_target_pairs={{0,8},{4,12},{8,16},{12,20},{16,24},{20,28},{24,32},{28,36},{32,40... | collective-permute-start | bytes 393224 | tf_op jit(solution)/shard_map/ppermute | solution.py:15
Sparse Core Ops, SparseCore 0:
  55.6 32.8 reduce-scatter.2
  128.0 33.7 reduce-scatter.4
where the time goes:
time: 181 us; the launch traced here: 180 us
  starting transfers between devices  98.5 us (54%)
  blocking collectives  20.1 us (11%)
  waiting for transfers between devices  15.3 us (8%)
  between operations  14.6 us (8%)
  matrix products  14.4 us (8%)
  local copies, waits for them, and re-layouts  13 us (7%)
  other arithmetic  4.26 us (2%)
    ppermute x24, starting transfers between devices, shifted(): return lax.ppermute(value, axis, pairs)  98.4 us
    all_gather x2, blocking collectives, per_device(): whole_block = lax.all_gather(current, 'seg', axis=0, tiled=True)  20.1 us
    ppermute x24, waiting for transfers between devices, shifted(): return lax.ppermute(value, axis, pairs)  15.3 us
    dot_general x2, matrix products, forward_term(): return jnp.dot(flat_tiles, stacked, preferred_element_type=jnp.float32)  7.95 us
    unnamed x16, local copies, waits for them, and re-layouts  7.27 us
    dot_general x2, matrix products, per_device(): lax.dot_general(flat_tiles, whole_block, (((0,), (0,)), ((), ())), prefer...  6.41 us
  transfers between devices with their start and end apart: 26, of which 6 were waited for; matrix products, arithmetic and copies ran while one was open for 10% of the time, Pallas kernels for 0%

commit v1 on v0

v1 whole, which is shorter than its diff:
```python
import functools

import jax
import jax.numpy as jnp
from jax import lax
from jax.experimental import pallas as pl
from jax.experimental.pallas import tpu as pltpu
from jax.sharding import PartitionSpec as P

ITERS = 2


step_size = 0.8

VMEM = pltpu.VMEM
F32 = jnp.float32
BF16 = jnp.bfloat16


def spec(space=None):
    return pl.BlockSpec(memory_space=VMEM if space is None else space)


def shifted(value, by):
    length = lax.axis_size("chain")
    pairs = [(i, i + by) for i in range(length) if 0 <= i + by < length]
    return lax.ppermute(value, "chain", pairs)


def swapped(value):
    length = lax.axis_size("chain")
    return lax.ppermute(value, "chain", [(i, i ^ 1) for i in range(length)])


def soft_limit(values, limit):
    return jnp.maximum(values - limit, 0.0) + jnp.minimum(values + limit, 0.0)


def begin_kernel(warm_ref, est_ref, cur_ref, copies_ref):
    est = warm_ref[...].T
    est_ref[...] = est
    cur = est.astype(BF16)
    cur_ref[...] = cur
    for s in range(copies_ref.shape[0]):
        copies_ref[s] = cur


def load_tiles(tiles_ref, held, sems):
    copies = [
        pltpu.make_async_copy(tiles_ref.at[j], held.at[j], sems.at[j])
        for j in range(held.shape[0])
    ]
    for copy in copies:
        copy.start()
    return copies


def backward_kernel(widths_ref, tiles_ref, block_ref, first_ref, rest_ref, held, sems):
    copies = load_tiles(tiles_ref, held, sems)
    n_seg, _, strip = block_ref.shape
    for j, copy in enumerate(copies):
        copy.wait()
        total = None
        for s in range(n_seg):
            term = jnp.dot(
                block_ref[s],
                held[j, pl.ds(s * strip, strip), :],
                preferred_element_type=F32,
            )
            total = term if total is None else total + term
        total = jnp.where(j <= widths_ref[0], total, 0.0)
        if j == 0:
            first_ref[...] = total
        else:
            rest_ref[j - 1] = total.astype(BF16)


def forward_kernel(
    widths_ref, tiles_ref, cur_ref, swap_ref, r1_ref, r2_ref, r3_ref, out_ref, held, total, sems
):
    copies = load_tiles(tiles_ref, held, sems)
    n_seg = out_ref.shape[0]
    strip = out_ref.shape[2]
    ahead = [
        lambda: cur_ref[...],
        lambda: swap_ref[0],
        lambda: r1_ref[...],
        lambda: swap_ref[1],
        lambda: r2_ref[...],
        lambda: swap_ref[2],
        lambda: r3_ref[...],
    ]
    for j, copy in enumerate(copies):
        copy.wait()
        value = ahead[j]()
        value = jnp.where(j <= widths_ref[0], value, jnp.zeros_like(value))
        for s in range(n_seg):
            term = lax.dot_general(
                value,
                held[j, pl.ds(s * strip, strip), :],
                (((1,), (1,)), ((), ())),
                preferred_element_type=F32,
            )
            if j == 0:
                total[s] = term
            elif j < len(copies) - 1:
                total[s] += term
            else:
                out_ref[s] = (total[s] + term).astype(BF16)


def new_estimate(odd_ref, est_ref, first_ref, pair_ref, seg_ref, b1_ref, b2_ref, b3_ref, scores_ref, pen_ref):
    coupled = first_ref[...]
    pair = pair_ref[0].astype(F32)
    coupled = coupled + jnp.where(odd_ref[0] == 1, pair, 0.0)
    for s in range(seg_ref.shape[0]):
        coupled = coupled + seg_ref[s].astype(F32)
    for ref in (b1_ref, b2_ref, b3_ref):
        coupled = coupled + ref[...].astype(F32)
    est = est_ref[...]
    columns, traits = est.shape[0], scores_ref.shape[0]
    target = jnp.concatenate([scores_ref[...]] * (columns // traits), axis=0)
    stepped = est - step_size * (est + coupled - target)
    return soft_limit(stepped, pen_ref[...])


def update_kernel(*refs):
    new_ref, cur_ref, copies_ref = refs[-3:]
    est = new_estimate(*refs[:-3])
    new_ref[...] = est
    cur = est.astype(BF16)
    cur_ref[...] = cur
    for s in range(copies_ref.shape[0]):
        copies_ref[s] = cur


def final_kernel(*refs):
    refs[-1][...] = new_estimate(*refs[:-1]).T


def per_device(band_tiles, widths, warm_start, scores, penalty):
    n_seg = lax.axis_size("seg")
    tiles = jnp.transpose(band_tiles[0], (1, 0, 2))
    depth, block_len, strip = tiles.shape
    columns = warm_start.shape[1]
    scores_t = scores.T
    pen = jnp.broadcast_to((step_size * penalty)[:, None], (columns, strip))
    odd = lax.rem(lax.axis_index("chain"), 2).astype(jnp.int32)
    is_odd = odd == 1
    odd_arr = odd.reshape((1,))
    vec_f32 = jax.ShapeDtypeStruct((columns, strip), F32)
    vec_bf16 = jax.ShapeDtypeStruct((columns, strip), BF16)
    seg_bf16 = jax.ShapeDtypeStruct((n_seg, columns, strip), BF16)
    smem = spec(pltpu.SMEM)
    hbm = spec(pl.ANY)
    flops = 2 * depth * block_len * strip * columns
    mat_cost = pl.CostEstimate(
        flops=flops, bytes_accessed=depth * block_len * strip * 2, transcendentals=0
    )
    small_cost = pl.CostEstimate(
        flops=20 * columns * strip, bytes_accessed=12 * columns * strip, transcendentals=0
    )
    tile_scratch = [VMEM((depth, block_len, strip), BF16)]
    tile_sems = [pltpu.SemaphoreType.DMA((depth,))]

    begin = pl.pallas_call(
        begin_kernel,
        out_shape=(vec_f32, vec_bf16, seg_bf16),
        in_specs=[spec()],
        out_specs=(spec(),) * 3,
        cost_estimate=small_cost,
        compiler_params=pltpu.CompilerParams(vmem_limit_bytes=4 << 20),
        name="begin",
    )
    backward = pl.pallas_call(
        backward_kernel,
        out_shape=(vec_f32, jax.ShapeDtypeStruct((depth - 1, columns, strip), BF16)),
        in_specs=[smem, hbm, spec()],
        out_specs=(spec(),) * 2,
        scratch_shapes=tile_scratch + tile_sems,
        cost_estimate=mat_cost,
        compiler_params=pltpu.CompilerParams(vmem_limit_bytes=10 << 20),
        name="backward",
    )
    forward = pl.pallas_call(
        forward_kernel,
        out_shape=seg_bf16,
        in_specs=[smem, hbm] + [spec()] * 5,
        out_specs=spec(),
        scratch_shapes=tile_scratch + [VMEM((n_seg, columns, strip), F32)] + tile_sems,
        cost_estimate=mat_cost,
        compiler_params=pltpu.CompilerParams(vmem_limit_bytes=10 << 20),
        name="forward",
    )
    update = pl.pallas_call(
        update_kernel,
        out_shape=(vec_f32, vec_bf16, seg_bf16),
        in_specs=[smem] + [spec()] * 9,
        out_specs=(spec(),) * 3,
        cost_estimate=small_cost,
        compiler_params=pltpu.CompilerParams(vmem_limit_bytes=8 << 20),
        name="update",
    )
    final = pl.pallas_call(
        final_kernel,
        out_shape=jax.ShapeDtypeStruct((strip, columns), F32),
        in_specs=[smem] + [spec()] * 9,
        out_specs=spec(),
        cost_estimate=small_cost,
        compiler_params=pltpu.CompilerParams(vmem_limit_bytes=8 << 20),
        name="final",
    )

    estimate, current, copies = begin(warm_start)
    for iteration in range(ITERS):
        block = lax.all_to_all(copies, "seg", 0, 0)
        r3, r2, r1 = (shifted(current, -2 * k) for k in (3, 2, 1))
        first, rest = backward(widths, tiles, block)
        lent = jnp.stack(
            [
                jnp.where(is_odd, current, r1),
                jnp.where(is_odd, r1, r2),
                jnp.where(is_odd, r2, r3),
                rest[0],
                rest[2],
                rest[4],
            ]
        )
        got = swapped(lent)
        add_1 = jnp.where(is_odd, got[4], got[3]).astype(F32)
        add_2 = jnp.where(is_odd, got[5], got[4]).astype(F32)
        add_3 = jnp.where(is_odd, jnp.zeros_like(got[5]), got[5]).astype(F32)
        t1 = (rest[1].astype(F32) + add_1).astype(BF16)
        t2 = (rest[3].astype(F32) + add_2).astype(BF16)
        t3 = (rest[5].astype(F32) + add_3).astype(BF16)
        partial = forward(widths, tiles, current, got, r1, r2, r3)
        summed = lax.all_to_all(partial, "seg", 0, 0)
        b3, b2, b1 = shifted(t3, 6), shifted(t2, 4), shifted(t1, 2)
        operands = (odd_arr, estimate, first, got[3:4], summed, b1, b2, b3, scores_t, pen)
        if iteration < ITERS - 1:
            estimate, current, copies = update(*operands)
        else:
            return final(*operands)


def solution(mesh):
    in_specs = (
        P("chain", None, None, "seg"),
        P("chain"),
        P(("chain", "seg"), None),
        P(("chain", "seg"), None),
        P(),
    )
    out_specs = P(("chain", "seg"), None)
    return jax.shard_map(
        per_device, mesh=mesh, in_specs=in_specs, out_specs=out_specs, check_vma=False
    )
```

time: 181 us -> 126 us (0.70)
  the two profiles are of different devices: /device:TPU:65 before, /device:TPU:386 now
where the time goes in v1:
time: 126 us; the launch traced here: 125 us
  starting transfers between devices  65.7 us (52%)
  waiting for transfers between devices  29.8 us (24%)
  Pallas kernels  14.8 us (12%)
  local copies, waits for them, and re-layouts  9.15 us (7%)
  other arithmetic  4.33 us (3%)
    ppermute x12, starting transfers between devices, shifted(): return lax.ppermute(value, 'chain', pairs)  42.3 us
    ppermute x12, waiting for transfers between devices, shifted(): return lax.ppermute(value, 'chain', pairs)  16.6 us
    all_to_all x2, starting transfers between devices, per_device(): summed = lax.all_to_all(partial, 'seg', 0, 0)  9.82 us
    all_to_all x2, starting transfers between devices, per_device(): block = lax.all_to_all(copies, 'seg', 0, 0)  9.65 us
    all_to_all x2, waiting for transfers between devices, per_device(): block = lax.all_to_all(copies, 'seg', 0, 0)  8.29 us
    unnamed x18, local copies, waits for them, and re-layouts  7.7 us
    pallas_call x2, Pallas kernels, per_device(): first, rest = backward(widths, tiles, block)  6.28 us
    pallas_call x2, Pallas kernels, per_device(): partial = forward(widths, tiles, current, got, r1, r2, r3)  5.51 us
  transfers between devices with their start and end apart: 18, of which 9 were waited for; matrix products, arithmetic and copies ran while one was open for 3% of the time, Pallas kernels for 0%

profile of v1, /device:TPU:386, one launch (start us, length us, event | category | flops | bytes accessed | tf_op | source)
XLA Modules:
  0.0 124.7 jit_solution(9997698630577544467)
XLA Ops:
  0.0 0.9 copy-done.5
  1.0 1.0 begin.1
  1.9 6.6 %collective-permute-start = (bf16[256,256]{1,0:T(8,128)(2,1)S(1)}, bf16[256,256]{1,0:T(8,128)(2,1)S(1)}, u32[]{:S(2)}, u32[]{:S(2)}) collective-permute-start(bf16[256,256]{1,0:T(8,128)(2,1)S(1)} %get-tuple-element.18.cur_ref), channel_id=1, source_target_pairs={{8,0},{12,4},{16,8},{20,12},{24,16},{28,20},{32,24},{36,28},{40,32... | collective-permute-start | bytes 393224 | tf_op jit(solution)/shard_map/ppermute | solution.py:27
  8.5 1.9 %collective-permute-start.2 = (bf16[256,256]{1,0:T(8,128)(2,1)S(1)}, bf16[256,256]{1,0:T(8,128)(2,1)S(1)}, u32[]{:S(2)}, u32[]{:S(2)}) collective-permute-start(bf16[256,256]{1,0:T(8,128)(2,1)S(1)} %get-tuple-element.18.cur_ref), channel_id=1, source_target_pairs={{24,0},{28,4},{32,8},{36,12},{40,16},{44,20},{48,24},{52,28},{56,3... | collective-permute-start | bytes 393224 | tf_op jit(solution)/shard_map/ppermute | solution.py:27
  10.4 4.5 %collective-permute-start.1 = (bf16[256,256]{1,0:T(8,128)(2,1)S(1)}, bf16[256,256]{1,0:T(8,128)(2,1)S(1)}, u32[]{:S(2)}, u32[]{:S(2)}) collective-permute-start(bf16[256,256]{1,0:T(8,128)(2,1)S(1)} %get-tuple-element.18.cur_ref), channel_id=1, source_target_pairs={{16,0},{20,4},{24,8},{28,12},{32,16},{36,20},{40,24},{44,28},{48,3... | collective-permute-start | bytes 393224 | tf_op jit(solution)/shard_map/ppermute | solution.py:27
  15.0 4.8 %all-to-all-start = ((bf16[4,256,256]{2,1,0:T(8,128)(2,1)}), bf16[4,256,256]{2,1,0:T(8,128)(2,1)S(1)}, u32[]{:S(2)}, u32[]{:S(2)}) async-start(bf16[4,256,256]{2,1,0:T(8,128)(2,1)} %get-tuple-element.16), calls=%async_computation | async-start | bytes 1048576 | tf_op jit(solution)/shard_map/all_to_all | solution.py:216
  20.5 0.0 collective-permute-done.r1_ref
  20.5 0.7 bitcast_dynamic-update-slice_fusion.5
  21.2 0.0 collective-permute-done.1.r2_ref
  21.2 0.7 bitcast_dynamic-update-slice_fusion.4
  21.9 0.0 collective-permute-done.2.r3_ref
  21.9 0.7 bitcast_dynamic-update-slice_fusion.3
  22.5 4.5 %all-to-all-done.block_ref = bf16[4,256,256]{2,1,0:T(8,128)(2,1)S(1)} async-done(((bf16[4,256,256]{2,1,0:T(8,128)(2,1)}), bf16[4,256,256]{2,1,0:T(8,128)(2,1)S(1)}, u32[]{:S(2)}, u32[]{:S(2)}) %all-to-all-start) | async-done | bytes 524320 | tf_op jit(solution)/shard_map/all_to_all | solution.py:216
  27.0 2.0 %copy-done = bf16[1,1024,7,256]{3,1,2,0:T(8,128)(2,1)S(1)} copy-done((bf16[1,1024,7,256]{3,1,2,0:T(8,128)(2,1)S(1)}, bf16[1,1024,7,256]{3,1,2,0:T(8,128)(2,1)}, u32[]{:S(2)}) %copy-start) | copy-done | bytes 3670040
  29.0 3.1 %backward.2 = (f32[256,256]{1,0:T(8,128)S(1)}, bf16[6,256,256]{2,1,0:T(8,128)(2,1)S(1)}) custom-call(s32[1]{0:T(128)S(6)} %copy.16.widths_ref, bf16[7,1024,256]{2,1,0:T(8,128)(2,1)S(1)} %bitcast.29, bf16[4,256,256]{2,1,0:T(8,128)(2,1)S(1)} %all-to-all-done.block_ref), custom_call_target="tpu_custom_call" | custom-call | flops 939524096 | bytes 3670016 | tf_op jit(solution)/shard_map/backward/pallas_call | solution.py:218
  32.2 0.7 slice_dynamic-update-slice_fusion.5
  32.9 0.7 slice_dynamic-update-slice_fusion.4
  33.5 0.7 slice_dynamic-update-slice_fusion.3
  34.2 2.0 %collective-permute-start.3 = (bf16[6,256,256]{2,1,0:T(8,128)(2,1)}, bf16[6,256,256]{2,1,0:T(8,128)(2,1)S(1)}, u32[]{:S(2)}, u32[]{:S(2)}) collective-permute-start(bf16[6,256,256]{2,1,0:T(8,128)(2,1)} %slice_dynamic-update-slice_fusion.3), channel_id=1, source_target_pairs={{0,4},{4,0},{8,12},{12,8},{16,20},{20,16},{24,28},{28,24},{32,36},... | collective-permute-start | bytes 2359304 | tf_op jit(solution)/shard_map/ppermute | solution.py:32
  36.2 2.5 %collective-permute-done.3.swap_ref = bf16[6,256,256]{2,1,0:T(8,128)(2,1)S(1)} collective-permute-done((bf16[6,256,256]{2,1,0:T(8,128)(2,1)}, bf16[6,256,256]{2,1,0:T(8,128)(2,1)S(1)}, u32[]{:S(2)}, u32[]{:S(2)}) %collective-permute-start.3) | collective-permute-done | bytes 786464 | tf_op jit(solution)/shard_map/ppermute | solution.py:32
  38.7 0.0 copy-done.1
  38.7 2.8 %forward.2 = bf16[4,256,256]{2,1,0:T(8,128)(2,1)} custom-call(s32[1]{0:T(128)S(6)} %copy.16.widths_ref, bf16[7,1024,256]{2,1,0:T(8,128)(2,1)S(1)} %bitcast.30, bf16[256,256]{1,0:T(8,128)(2,1)S(1)} %get-tuple-element.18.cur_ref, bf16[6,256,256]{2,1,0:T(8,128)(2,1)S(1)} %collective-permute-done.3.swap_ref, bf16[256,256]{1,0:T(8,128)(2,1)S(1)} %collective-permute-done.r1_ref, ...), custom_call_target="tpu_custom_call" | custom-call | flops 939524096 | bytes 3670016 | tf_op jit(solution)/shard_map/forward/pallas_call | solution.py:236
  41.5 4.9 %all-to-all-start.1 = ((bf16[4,256,256]{2,1,0:T(8,128)(2,1)}), bf16[4,256,256]{2,1,0:T(8,128)(2,1)S(1)}, u32[]{:S(2)}, u32[]{:S(2)}) async-start(bf16[4,256,256]{2,1,0:T(8,128)(2,1)} %forward.2), calls=%async_computation.1 | async-start | bytes 1048576 | tf_op jit(solution)/shard_map/all_to_all | solution.py:237
  46.4 0.1 fusion.2
  46.5 2.8 %collective-permute-start.6 = (bf16[256,256]{1,0:T(8,128)(2,1)S(1)}, bf16[256,256]{1,0:T(8,128)(2,1)S(1)}, u32[]{:S(2)}, u32[]{:S(2)}) collective-permute-start(bf16[256,256]{1,0:T(8,128)(2,1)S(1)} %get-tuple-element.28), channel_id=1, source_target_pairs={{0,24},{4,28},{8,32},{12,36},{16,40},{20,44},{24,48},{28,52},{32,5... | collective-permute-start | bytes 393224 | tf_op jit(solution)/shard_map/ppermute | solution.py:27
  49.3 5.4 %collective-permute-start.5 = (bf16[256,256]{1,0:T(8,128)(2,1)S(1)}, bf16[256,256]{1,0:T(8,128)(2,1)S(1)}, u32[]{:S(2)}, u32[]{:S(2)}) collective-permute-start(bf16[256,256]{1,0:T(8,128)(2,1)S(1)} %get-tuple-element.29), channel_id=1, source_target_pairs={{0,16},{4,20},{8,24},{12,28},{16,32},{20,36},{24,40},{28,44},{32,4... | collective-permute-start | bytes 393224 | tf_op jit(solution)/shard_map/ppermute | solution.py:27
  54.8 1.9 %collective-permute-start.4 = (bf16[256,256]{1,0:T(8,128)(2,1)S(1)}, bf16[256,256]{1,0:T(8,128)(2,1)S(1)}, u32[]{:S(2)}, u32[]{:S(2)}) collective-permute-start(bf16[256,256]{1,0:T(8,128)(2,1)S(1)} %get-tuple-element.30), channel_id=1, source_target_pairs={{0,8},{4,12},{8,16},{12,20},{16,24},{20,28},{24,32},{28,36},{32,40... | collective-permute-start | bytes 393224 | tf_op jit(solution)/shard_map/ppermute | solution.py:27
  56.7 0.0 collective-permute-done.6.refs_7_
  56.7 3.9 %collective-permute-done.5.refs_6_ = bf16[256,256]{1,0:T(8,128)(2,1)S(1)} collective-permute-done((bf16[256,256]{1,0:T(8,128)(2,1)S(1)}, bf16[256,256]{1,0:T(8,128)(2,1)S(1)}, u32[]{:S(2)}, u32[]{:S(2)}) %collective-permute-start.5) | collective-permute-done | bytes 131104 | tf_op jit(solution)/shard_map/ppermute | solution.py:27
  60.6 4.3 %collective-permute-done.4.refs_5_ = bf16[256,256]{1,0:T(8,128)(2,1)S(1)} collective-permute-done((bf16[256,256]{1,0:T(8,128)(2,1)S(1)}, bf16[256,256]{1,0:T(8,128)(2,1)S(1)}, u32[]{:S(2)}, u32[]{:S(2)}) %collective-permute-start.4) | collective-permute-done | bytes 131104 | tf_op jit(solution)/shard_map/ppermute | solution.py:27
  64.9 0.0 all-to-all-done.1.refs_4_
  64.9 0.1 broadcast_in_dim.2.refs_9_
  65.0 0.0 copy-done.4
  65.1 1.1 update.1
  66.1 1.9 %collective-permute-start.7 = (bf16[256,256]{1,0:T(8,128)(2,1)S(1)}, bf16[256,256]{1,0:T(8,128)(2,1)S(1)}, u32[]{:S(2)}, u32[]{:S(2)}) collective-permute-start(bf16[256,256]{1,0:T(8,128)(2,1)S(1)} %get-tuple-element.23.cur_ref), channel_id=1, source_target_pairs={{8,0},{12,4},{16,8},{20,12},{24,16},{28,20},{32,24},{36,28},{40,32... | collective-permute-start | bytes 393224 | tf_op jit(solution)/shard_map/ppermute | solution.py:27
  68.0 4.4 %collective-permute-start.9 = (bf16[256,256]{1,0:T(8,128)(2,1)S(1)}, bf16[256,256]{1,0:T(8,128)(2,1)S(1)}, u32[]{:S(2)}, u32[]{:S(2)}) collective-permute-start(bf16[256,256]{1,0:T(8,128)(2,1)S(1)} %get-tuple-element.23.cur_ref), channel_id=1, source_target_pairs={{24,0},{28,4},{32,8},{36,12},{40,16},{44,20},{48,24},{52,28},{56,3... | collective-permute-start | bytes 393224 | tf_op jit(solution)/shard_map/ppermute | solution.py:27
  72.4 1.9 %collective-permute-start.8 = (bf16[256,256]{1,0:T(8,128)(2,1)S(1)}, bf16[256,256]{1,0:T(8,128)(2,1)S(1)}, u32[]{:S(2)}, u32[]{:S(2)}) collective-permute-start(bf16[256,256]{1,0:T(8,128)(2,1)S(1)} %get-tuple-element.23.cur_ref), channel_id=1, source_target_pairs={{16,0},{20,4},{24,8},{28,12},{32,16},{36,20},{40,24},{44,28},{48,3... | collective-permute-start | bytes 393224 | tf_op jit(solution)/shard_map/ppermute | solution.py:27
  74.3 4.8 %all-to-all-start.2 = ((bf16[4,256,256]{2,1,0:T(8,128)(2,1)}), bf16[4,256,256]{2,1,0:T(8,128)(2,1)S(1)}, u32[]{:S(2)}, u32[]{:S(2)}) async-start(bf16[4,256,256]{2,1,0:T(8,128)(2,1)} %get-tuple-element.21), calls=%async_computation.2 | async-start | bytes 1048576 | tf_op jit(solution)/shard_map/all_to_all | solution.py:216
  79.1 0.0 collective-permute-done.7.r1_ref
  79.1 0.7 bitcast_dynamic-update-slice_fusion.2
  79.8 0.9 collective-permute-done.8.r2_ref
  80.8 0.7 bitcast_dynamic-update-slice_fusion.1
  81.4 0.0 collective-permute-done.9.r3_ref
  81.5 0.7 bitcast_dynamic-update-slice_fusion
  82.1 3.8 %all-to-all-done.2.block_ref = bf16[4,256,256]{2,1,0:T(8,128)(2,1)S(1)} async-done(((bf16[4,256,256]{2,1,0:T(8,128)(2,1)}), bf16[4,256,256]{2,1,0:T(8,128)(2,1)S(1)}, u32[]{:S(2)}, u32[]{:S(2)}) %all-to-all-start.2) | async-done | bytes 524320 | tf_op jit(solution)/shard_map/all_to_all | solution.py:216
  86.0 2.0 %copy-done.2 = bf16[1,1024,7,256]{3,1,2,0:T(8,128)(2,1)S(1)} copy-done((bf16[1,1024,7,256]{3,1,2,0:T(8,128)(2,1)S(1)}, bf16[1,1024,7,256]{3,1,2,0:T(8,128)(2,1)}, u32[]{:S(2)}) %copy-start.2) | copy-done | bytes 3670040
  88.0 3.1 %backward.3 = (f32[256,256]{1,0:T(8,128)S(1)}, bf16[6,256,256]{2,1,0:T(8,128)(2,1)S(1)}) custom-call(s32[1]{0:T(128)S(6)} %copy.16.widths_ref, bf16[7,1024,256]{2,1,0:T(8,128)(2,1)S(1)} %bitcast.31, bf16[4,256,256]{2,1,0:T(8,128)(2,1)S(1)} %all-to-all-done.2.block_ref), custom_call_target="tpu_custom_call" | custom-call | flops 939524096 | bytes 3670016 | tf_op jit(solution)/shard_map/backward/pallas_call | solution.py:218
  91.1 0.7 slice_dynamic-update-slice_fusion.2
  91.8 0.7 slice_dynamic-update-slice_fusion.1
  92.5 0.7 slice_dynamic-update-slice_fusion
  93.1 1.9 %collective-permute-start.10 = (bf16[6,256,256]{2,1,0:T(8,128)(2,1)}, bf16[6,256,256]{2,1,0:T(8,128)(2,1)S(1)}, u32[]{:S(2)}, u32[]{:S(2)}) collective-permute-start(bf16[6,256,256]{2,1,0:T(8,128)(2,1)} %slice_dynamic-update-slice_fusion), channel_id=1, source_target_pairs={{0,4},{4,0},{8,12},{12,8},{16,20},{20,16},{24,28},{28,24},{32,36},... | collective-permute-start | bytes 2359304 | tf_op jit(solution)/shard_map/ppermute | solution.py:32
  95.1 2.5 %collective-permute-done.10.swap_ref = bf16[6,256,256]{2,1,0:T(8,128)(2,1)S(1)} collective-permute-done((bf16[6,256,256]{2,1,0:T(8,128)(2,1)}, bf16[6,256,256]{2,1,0:T(8,128)(2,1)S(1)}, u32[]{:S(2)}, u32[]{:S(2)}) %collective-permute-start.10) | collective-permute-done | bytes 786464 | tf_op jit(solution)/shard_map/ppermute | solution.py:32
  97.5 0.0 copy-done.3
  97.5 2.8 %forward.3 = bf16[4,256,256]{2,1,0:T(8,128)(2,1)} custom-call(s32[1]{0:T(128)S(6)} %copy.16.widths_ref, bf16[7,1024,256]{2,1,0:T(8,128)(2,1)S(1)} %bitcast.32, bf16[256,256]{1,0:T(8,128)(2,1)S(1)} %get-tuple-element.23.cur_ref, bf16[6,256,256]{2,1,0:T(8,128)(2,1)S(1)} %collective-permute-done.10.swap_ref, ...), custom_call_target="tpu_custom_call" | custom-call | flops 939524096 | bytes 3670016 | tf_op jit(solution)/shard_map/forward/pallas_call | solution.py:236
  100.3 4.9 %all-to-all-start.3 = ((bf16[4,256,256]{2,1,0:T(8,128)(2,1)}), bf16[4,256,256]{2,1,0:T(8,128)(2,1)S(1)}, u32[]{:S(2)}, u32[]{:S(2)}) async-start(bf16[4,256,256]{2,1,0:T(8,128)(2,1)} %forward.3), calls=%async_computation.3 | async-start | bytes 1048576 | tf_op jit(solution)/shard_map/all_to_all | solution.py:237
  105.2 0.1 fusion.5
  105.3 4.0 %collective-permute-start.13 = (bf16[256,256]{1,0:T(8,128)(2,1)S(1)}, bf16[256,256]{1,0:T(8,128)(2,1)S(1)}, u32[]{:S(2)}, u32[]{:S(2)}) collective-permute-start(bf16[256,256]{1,0:T(8,128)(2,1)S(1)} %get-tuple-element.25), channel_id=1, source_target_pairs={{0,24},{4,28},{8,32},{12,36},{16,40},{20,44},{24,48},{28,52},{32,5... | collective-permute-start | bytes 393224 | tf_op jit(solution)/shard_map/ppermute | solution.py:27
  109.3 4.3 %collective-permute-start.12 = (bf16[256,256]{1,0:T(8,128)(2,1)S(1)}, bf16[256,256]{1,0:T(8,128)(2,1)S(1)}, u32[]{:S(2)}, u32[]{:S(2)}) collective-permute-start(bf16[256,256]{1,0:T(8,128)(2,1)S(1)} %get-tuple-element.26), channel_id=1, source_target_pairs={{0,16},{4,20},{8,24},{12,28},{16,32},{20,36},{24,40},{28,44},{32,4... | collective-permute-start | bytes 393224 | tf_op jit(solution)/shard_map/ppermute | solution.py:27
  113.6 2.7 %collective-permute-start.11 = (bf16[256,256]{1,0:T(8,128)(2,1)S(1)}, bf16[256,256]{1,0:T(8,128)(2,1)S(1)}, u32[]{:S(2)}, u32[]{:S(2)}) collective-permute-start(bf16[256,256]{1,0:T(8,128)(2,1)S(1)} %get-tuple-element.27), channel_id=1, source_target_pairs={{0,8},{4,12},{8,16},{12,20},{16,24},{20,28},{24,32},{28,36},{32,40... | collective-permute-start | bytes 393224 | tf_op jit(solution)/shard_map/ppermute | solution.py:27
  116.3 0.0 collective-permute-done.13.refs_7_
  116.3 3.6 %collective-permute-done.12.refs_6_ = bf16[256,256]{1,0:T(8,128)(2,1)S(1)} collective-permute-done((bf16[256,256]{1,0:T(8,128)(2,1)S(1)}, bf16[256,256]{1,0:T(8,128)(2,1)S(1)}, u32[]{:S(2)}, u32[]{:S(2)}) %collective-permute-start.12) | collective-permute-done | bytes 131104 | tf_op jit(solution)/shard_map/ppermute | solution.py:27
  119.9 3.9 %collective-permute-done.11.refs_5_ = bf16[256,256]{1,0:T(8,128)(2,1)S(1)} collective-permute-done((bf16[256,256]{1,0:T(8,128)(2,1)S(1)}, bf16[256,256]{1,0:T(8,128)(2,1)S(1)}, u32[]{:S(2)}, u32[]{:S(2)}) %collective-permute-start.11) | collective-permute-done | bytes 131104 | tf_op jit(solution)/shard_map/ppermute | solution.py:27
  123.7 0.0 all-to-all-done.3.refs_4_
  123.7 1.0 final.1
  (11 shorter events, 0.0 us)
Async XLA Ops:
  0.0 0.9 copy-start.5
  1.9 18.5 %collective-permute-start = (bf16[256,256]{1,0:T(8,128)(2,1)S(1)}, bf16[256,256]{1,0:T(8,128)(2,1)S(1)}, u32[]{:S(2)}, u32[]{:S(2)}) collective-permute-start(bf16[256,256]{1,0:T(8,128)(2,1)S(1)} %get-tuple-element.18.cur_ref), channel_id=1, source_target_pairs={{8,0},{12,4},{16,8},{20,12},{24,16},{28,20},{32,24},{36,28},{40,32... | collective-permute-start | bytes 393224 | tf_op jit(solution)/shard_map/ppermute | solution.py:27
  8.5 13.3 %collective-permute-start.2 = (bf16[256,256]{1,0:T(8,128)(2,1)S(1)}, bf16[256,256]{1,0:T(8,128)(2,1)S(1)}, u32[]{:S(2)}, u32[]{:S(2)}) collective-permute-start(bf16[256,256]{1,0:T(8,128)(2,1)S(1)} %get-tuple-element.18.cur_ref), channel_id=1, source_target_pairs={{24,0},{28,4},{32,8},{36,12},{40,16},{44,20},{48,24},{52,28},{56,3... | collective-permute-start | bytes 393224 | tf_op jit(solution)/shard_map/ppermute | solution.py:27
  10.4 10.7 %collective-permute-start.1 = (bf16[256,256]{1,0:T(8,128)(2,1)S(1)}, bf16[256,256]{1,0:T(8,128)(2,1)S(1)}, u32[]{:S(2)}, u32[]{:S(2)}) collective-permute-start(bf16[256,256]{1,0:T(8,128)(2,1)S(1)} %get-tuple-element.18.cur_ref), channel_id=1, source_target_pairs={{16,0},{20,4},{24,8},{28,12},{32,16},{36,20},{40,24},{44,28},{48,3... | collective-permute-start | bytes 393224 | tf_op jit(solution)/shard_map/ppermute | solution.py:27
  15.0 12.0 %all-to-all-start = ((bf16[4,256,256]{2,1,0:T(8,128)(2,1)}), bf16[4,256,256]{2,1,0:T(8,128)(2,1)S(1)}, u32[]{:S(2)}, u32[]{:S(2)}) async-start(bf16[4,256,256]{2,1,0:T(8,128)(2,1)} %get-tuple-element.16), calls=%async_computation | async-start | bytes 1048576 | tf_op jit(solution)/shard_map/all_to_all | solution.py:216
  27.0 2.0 %copy-start = (bf16[1,1024,7,256]{3,1,2,0:T(8,128)(2,1)S(1)}, bf16[1,1024,7,256]{3,1,2,0:T(8,128)(2,1)}, u32[]{:S(2)}) copy-start(bf16[1,1024,7,256]{3,1,2,0:T(8,128)(2,1)} %param.5) | copy-start | bytes 11010052
  29.0 9.7 %copy-start.1 = (bf16[1,1024,7,256]{3,1,2,0:T(8,128)(2,1)S(1)}, bf16[1,1024,7,256]{3,1,2,0:T(8,128)(2,1)}, u32[]{:S(2)}) copy-start(bf16[1,1024,7,256]{3,1,2,0:T(8,128)(2,1)} %param.5) | copy-start | bytes 11010052
  34.2 22.5 %copy-start.6 = (f32[256]{0:T(256)S(1)}, f32[256]{0:T(256)}, u32[]{:S(2)}) copy-start(f32[256]{0:T(256)} %param.9) | copy-start | bytes 3076
  34.2 30.9 %copy-start.4 = (f32[256,64]{0,1:T(8,128)S(1)}, f32[256,64]{0,1:T(8,128)}, u32[]{:S(2)}) copy-start(f32[256,64]{0,1:T(8,128)} %param.8) | copy-start | bytes 196612
  34.2 4.5 %collective-permute-start.3 = (bf16[6,256,256]{2,1,0:T(8,128)(2,1)}, bf16[6,256,256]{2,1,0:T(8,128)(2,1)S(1)}, u32[]{:S(2)}, u32[]{:S(2)}) collective-permute-start(bf16[6,256,256]{2,1,0:T(8,128)(2,1)} %slice_dynamic-update-slice_fusion.3), channel_id=1, source_target_pairs={{0,4},{4,0},{8,12},{12,8},{16,20},{20,16},{24,28},{28,24},{32,36},... | collective-permute-start | bytes 2359304 | tf_op jit(solution)/shard_map/ppermute | solution.py:32
  41.5 23.5 %all-to-all-start.1 = ((bf16[4,256,256]{2,1,0:T(8,128)(2,1)}), bf16[4,256,256]{2,1,0:T(8,128)(2,1)S(1)}, u32[]{:S(2)}, u32[]{:S(2)}) async-start(bf16[4,256,256]{2,1,0:T(8,128)(2,1)} %forward.2), calls=%async_computation.1 | async-start | bytes 1048576 | tf_op jit(solution)/shard_map/all_to_all | solution.py:237
  46.5 10.2 %collective-permute-start.6 = (bf16[256,256]{1,0:T(8,128)(2,1)S(1)}, bf16[256,256]{1,0:T(8,128)(2,1)S(1)}, u32[]{:S(2)}, u32[]{:S(2)}) collective-permute-start(bf16[256,256]{1,0:T(8,128)(2,1)S(1)} %get-tuple-element.28), channel_id=1, source_target_pairs={{0,24},{4,28},{8,32},{12,36},{16,40},{20,44},{24,48},{28,52},{32,5... | collective-permute-start | bytes 393224 | tf_op jit(solution)/shard_map/ppermute | solution.py:27
  49.3 11.3 %collective-permute-start.5 = (bf16[256,256]{1,0:T(8,128)(2,1)S(1)}, bf16[256,256]{1,0:T(8,128)(2,1)S(1)}, u32[]{:S(2)}, u32[]{:S(2)}) collective-permute-start(bf16[256,256]{1,0:T(8,128)(2,1)S(1)} %get-tuple-element.29), channel_id=1, source_target_pairs={{0,16},{4,20},{8,24},{12,28},{16,32},{20,36},{24,40},{28,44},{32,4... | collective-permute-start | bytes 393224 | tf_op jit(solution)/shard_map/ppermute | solution.py:27
  54.8 10.2 %collective-permute-start.4 = (bf16[256,256]{1,0:T(8,128)(2,1)S(1)}, bf16[256,256]{1,0:T(8,128)(2,1)S(1)}, u32[]{:S(2)}, u32[]{:S(2)}) collective-permute-start(bf16[256,256]{1,0:T(8,128)(2,1)S(1)} %get-tuple-element.30), channel_id=1, source_target_pairs={{0,8},{4,12},{8,16},{12,20},{16,24},{20,28},{24,32},{28,36},{32,40... | collective-permute-start | bytes 393224 | tf_op jit(solution)/shard_map/ppermute | solution.py:27
  66.1 13.0 %collective-permute-start.7 = (bf16[256,256]{1,0:T(8,128)(2,1)S(1)}, bf16[256,256]{1,0:T(8,128)(2,1)S(1)}, u32[]{:S(2)}, u32[]{:S(2)}) collective-permute-start(bf16[256,256]{1,0:T(8,128)(2,1)S(1)} %get-tuple-element.23.cur_ref), channel_id=1, source_target_pairs={{8,0},{12,4},{16,8},{20,12},{24,16},{28,20},{32,24},{36,28},{40,32... | collective-permute-start | bytes 393224 | tf_op jit(solution)/shard_map/ppermute | solution.py:27
  68.0 13.4 %collective-permute-start.9 = (bf16[256,256]{1,0:T(8,128)(2,1)S(1)}, bf16[256,256]{1,0:T(8,128)(2,1)S(1)}, u32[]{:S(2)}, u32[]{:S(2)}) collective-permute-start(bf16[256,256]{1,0:T(8,128)(2,1)S(1)} %get-tuple-element.23.cur_ref), channel_id=1, source_target_pairs={{24,0},{28,4},{32,8},{36,12},{40,16},{44,20},{48,24},{52,28},{56,3... | collective-permute-start | bytes 393224 | tf_op jit(solution)/shard_map/ppermute | solution.py:27
  72.4 8.4 %collective-permute-start.8 = (bf16[256,256]{1,0:T(8,128)(2,1)S(1)}, bf16[256,256]{1,0:T(8,128)(2,1)S(1)}, u32[]{:S(2)}, u32[]{:S(2)}) collective-permute-start(bf16[256,256]{1,0:T(8,128)(2,1)S(1)} %get-tuple-element.23.cur_ref), channel_id=1, source_target_pairs={{16,0},{20,4},{24,8},{28,12},{32,16},{36,20},{40,24},{44,28},{48,3... | collective-permute-start | bytes 393224 | tf_op jit(solution)/shard_map/ppermute | solution.py:27
  74.3 11.6 %all-to-all-start.2 = ((bf16[4,256,256]{2,1,0:T(8,128)(2,1)}), bf16[4,256,256]{2,1,0:T(8,128)(2,1)S(1)}, u32[]{:S(2)}, u32[]{:S(2)}) async-start(bf16[4,256,256]{2,1,0:T(8,128)(2,1)} %get-tuple-element.21), calls=%async_computation.2 | async-start | bytes 1048576 | tf_op jit(solution)/shard_map/all_to_all | solution.py:216
  86.0 2.0 %copy-start.2 = (bf16[1,1024,7,256]{3,1,2,0:T(8,128)(2,1)S(1)}, bf16[1,1024,7,256]{3,1,2,0:T(8,128)(2,1)}, u32[]{:S(2)}) copy-start(bf16[1,1024,7,256]{3,1,2,0:T(8,128)(2,1)} %param.5) | copy-start | bytes 11010052
  88.0 9.5 %copy-start.3 = (bf16[1,1024,7,256]{3,1,2,0:T(8,128)(2,1)S(1)}, bf16[1,1024,7,256]{3,1,2,0:T(8,128)(2,1)}, u32[]{:S(2)}) copy-start(bf16[1,1024,7,256]{3,1,2,0:T(8,128)(2,1)} %param.5) | copy-start | bytes 11010052
  93.1 4.4 %collective-permute-start.10 = (bf16[6,256,256]{2,1,0:T(8,128)(2,1)}, bf16[6,256,256]{2,1,0:T(8,128)(2,1)S(1)}, u32[]{:S(2)}, u32[]{:S(2)}) collective-permute-start(bf16[6,256,256]{2,1,0:T(8,128)(2,1)} %slice_dynamic-update-slice_fusion), channel_id=1, source_target_pairs={{0,4},{4,0},{8,12},{12,8},{16,20},{20,16},{24,28},{28,24},{32,36},... | collective-permute-start | bytes 2359304 | tf_op jit(solution)/shard_map/ppermute | solution.py:32
  100.3 23.5 %all-to-all-start.3 = ((bf16[4,256,256]{2,1,0:T(8,128)(2,1)}), bf16[4,256,256]{2,1,0:T(8,128)(2,1)S(1)}, u32[]{:S(2)}, u32[]{:S(2)}) async-start(bf16[4,256,256]{2,1,0:T(8,128)(2,1)} %forward.3), calls=%async_computation.3 | async-start | bytes 1048576 | tf_op jit(solution)/shard_map/all_to_all | solution.py:237
  105.3 11.0 %collective-permute-start.13 = (bf16[256,256]{1,0:T(8,128)(2,1)S(1)}, bf16[256,256]{1,0:T(8,128)(2,1)S(1)}, u32[]{:S(2)}, u32[]{:S(2)}) collective-permute-start(bf16[256,256]{1,0:T(8,128)(2,1)S(1)} %get-tuple-element.25), channel_id=1, source_target_pairs={{0,24},{4,28},{8,32},{12,36},{16,40},{20,44},{24,48},{28,52},{32,5... | collective-permute-start | bytes 393224 | tf_op jit(solution)/shard_map/ppermute | solution.py:27
  109.3 10.6 %collective-permute-start.12 = (bf16[256,256]{1,0:T(8,128)(2,1)S(1)}, bf16[256,256]{1,0:T(8,128)(2,1)S(1)}, u32[]{:S(2)}, u32[]{:S(2)}) collective-permute-start(bf16[256,256]{1,0:T(8,128)(2,1)S(1)} %get-tuple-element.26), channel_id=1, source_target_pairs={{0,16},{4,20},{8,24},{12,28},{16,32},{20,36},{24,40},{28,44},{32,4... | collective-permute-start | bytes 393224 | tf_op jit(solution)/shard_map/ppermute | solution.py:27
  113.6 10.2 %collective-permute-start.11 = (bf16[256,256]{1,0:T(8,128)(2,1)S(1)}, bf16[256,256]{1,0:T(8,128)(2,1)S(1)}, u32[]{:S(2)}, u32[]{:S(2)}) collective-permute-start(bf16[256,256]{1,0:T(8,128)(2,1)S(1)} %get-tuple-element.27), channel_id=1, source_target_pairs={{0,8},{4,12},{8,16},{12,20},{16,24},{20,28},{24,32},{28,36},{32,40... | collective-permute-start | bytes 393224 | tf_op jit(solution)/shard_map/ppermute | solution.py:27

commit v2 on v0

v2 whole, which is shorter than its diff:
```python
import jax
import jax.numpy as jnp
from jax import lax
from jax.experimental import pallas as pl
from jax.experimental.pallas import tpu as pltpu
from jax.sharding import PartitionSpec as P


ITERS = 2


step_size = 0.8

VMEM = pltpu.VMEM
HBM = pltpu.HBM
F32 = jnp.float32
BF16 = jnp.bfloat16


def spec(space=None):
    return pl.BlockSpec(memory_space=VMEM if space is None else space)


def shifted(value, by):
    length = lax.axis_size("chain")
    pairs = [(i, i + by) for i in range(length) if 0 <= i + by < length]
    return lax.ppermute(value, "chain", pairs)


def swapped(value):
    length = lax.axis_size("chain")
    return lax.ppermute(value, "chain", [(i, i ^ 1) for i in range(length)])


def soft_limit(values, limit):
    return jnp.maximum(values - limit, 0.0) + jnp.minimum(values + limit, 0.0)


def begin_kernel(warm_ref, est_ref, cur_ref, copies_ref):
    est = warm_ref[...].T
    est_ref[...] = est
    cur = est.astype(BF16)
    cur_ref[...] = cur
    for s in range(copies_ref.shape[0]):
        copies_ref[s] = cur


def pair_kernel(cur_ref, far_ref, out_ref):
    out_ref[0] = cur_ref[...]
    out_ref[1] = far_ref[...]


def backward_body(widths_ref, held, block_ref, first_ref, even_ref, lent_ref, wait):
    block = jnp.concatenate([block_ref[s] for s in range(block_ref.shape[0])], axis=1)
    for j in range(held.shape[0]):
        wait(j)
        total = jnp.dot(block, held[j], preferred_element_type=F32)
        total = jnp.where(j <= widths_ref[0], total, 0.0)
        if j == 0:
            first_ref[...] = total
        elif j % 2 == 0:
            even_ref[j // 2 - 1] = total.astype(BF16)
        else:
            lent_ref[3 + j // 2] = total.astype(BF16)


def backward_load_kernel(widths_ref, tiles_ref, block_ref, first_ref, even_ref, lent_ref, held, sems):
    copies = [
        pltpu.make_async_copy(tiles_ref.at[j], held.at[j], sems.at[j])
        for j in range(held.shape[0])
    ]
    for copy in copies:
        copy.start()
    backward_body(
        widths_ref, held, block_ref, first_ref, even_ref, lent_ref, lambda j: copies[j].wait()
    )


def backward_kernel(widths_ref, held, block_ref, first_ref, even_ref, lent_ref):
    backward_body(widths_ref, held, block_ref, first_ref, even_ref, lent_ref, lambda j: None)


def lend_kernel(odd_ref, lent_ref, cur_ref, near_ref, far_ref, out_ref):
    del lent_ref

    @pl.when(odd_ref[0] == 1)
    def _():
        out_ref[0] = cur_ref[...]
        out_ref[1] = near_ref[0]
        out_ref[2] = far_ref[...]

    @pl.when(odd_ref[0] == 0)
    def _():
        out_ref[0] = near_ref[0]
        out_ref[1] = far_ref[...]
        out_ref[2] = near_ref[1]


def forward_product(widths_ref, held, values, offsets, s):
    strip = held.shape[2]
    left = jnp.concatenate(
        [jnp.where(j <= widths_ref[0], v, jnp.zeros_like(v)) for j, v in zip(offsets, values)],
        axis=1,
    )
    right = jnp.concatenate([held[j, pl.ds(s * strip, strip), :] for j in offsets], axis=1)
    return lax.dot_general(left, right, (((1,), (1,)), ((), ())), preferred_element_type=F32)


def forward_even_kernel(widths_ref, held, cur_ref, near_ref, far_ref, total_ref):
    values = [cur_ref[...], near_ref[0], far_ref[...], near_ref[1]]
    for s in range(total_ref.shape[0]):
        total_ref[s] = forward_product(widths_ref, held, values, (0, 2, 4, 6), s)


def forward_odd_kernel(widths_ref, held, got_ref, total_ref, out_ref):
    values = [got_ref[0], got_ref[1], got_ref[2]]
    for s in range(out_ref.shape[0]):
        term = forward_product(widths_ref, held, values, (1, 3, 5), s)
        out_ref[s] = (total_ref[s] + term).astype(BF16)


def combine_kernel(odd_ref, even_ref, got_ref, pair_ref, mid_ref):
    def add(k, other):
        return (even_ref[k].astype(F32) + other.astype(F32)).astype(BF16)

    @pl.when(odd_ref[0] == 1)
    def _():
        pair_ref[0] = add(0, got_ref[4])
        mid_ref[...] = add(1, got_ref[5])
        pair_ref[1] = even_ref[2]

    @pl.when(odd_ref[0] == 0)
    def _():
        pair_ref[0] = add(0, got_ref[3])
        mid_ref[...] = add(1, got_ref[4])
        pair_ref[1] = add(2, got_ref[5])


def relay_kernel(mid_ref, near_ref, out_ref):
    out_ref[...] = (mid_ref[...].astype(F32) + near_ref[1].astype(F32)).astype(BF16)


def new_estimate(odd_ref, est_ref, first_ref, got_ref, seg_ref, near_ref, far_ref, scores_ref, pen_ref):
    coupled = first_ref[...]
    coupled = coupled + jnp.where(odd_ref[0] == 1, got_ref[3].astype(F32), 0.0)
    for s in range(seg_ref.shape[0]):
        coupled = coupled + seg_ref[s].astype(F32)
    coupled = coupled + near_ref[0].astype(F32)
    coupled = coupled + far_ref[...].astype(F32)
    est = est_ref[...]
    columns, traits = est.shape[0], scores_ref.shape[0]
    target = jnp.concatenate([scores_ref[...]] * (columns // traits), axis=0)
    stepped = est - step_size * (est + coupled - target)
    return soft_limit(stepped, pen_ref[...])


def update_kernel(*refs):
    new_ref, cur_ref, copies_ref = refs[-3:]
    est = new_estimate(*refs[:-3])
    new_ref[...] = est
    cur = est.astype(BF16)
    cur_ref[...] = cur
    for s in range(copies_ref.shape[0]):
        copies_ref[s] = cur


def final_kernel(*refs):
    refs[-1][...] = new_estimate(*refs[:-1]).T


def call(kernel, out_shape, n_in, scalars, flops, nbytes, mib, tiles_in=None, **more):
    ins = [spec(pltpu.SMEM)] * scalars + [spec()] * (n_in - scalars)
    if tiles_in is not None:
        ins[tiles_in] = spec(HBM)
    outs = jax.tree.map(lambda _: spec(), out_shape)
    return pl.pallas_call(
        kernel,
        out_shape=out_shape,
        in_specs=ins,
        out_specs=outs,
        cost_estimate=pl.CostEstimate(flops=flops, bytes_accessed=nbytes, transcendentals=0),
        compiler_params=pltpu.CompilerParams(vmem_limit_bytes=mib << 20),
        **more,
    )


def per_device(band_tiles, widths, warm_start, scores, penalty):
    n_seg = lax.axis_size("seg")
    tiles = pltpu.with_memory_space_constraint(jnp.transpose(band_tiles[0], (1, 0, 2)), HBM)
    depth, block_len, strip = tiles.shape
    columns = warm_start.shape[1]
    scores_t = scores.T
    pen = jnp.broadcast_to((step_size * penalty)[:, None], (columns, strip))
    odd = lax.rem(lax.axis_index("chain"), 2).astype(jnp.int32).reshape((1,))

    def shape(dtype, *lead):
        return jax.ShapeDtypeStruct((*lead, columns, strip), dtype)

    flops = 2 * depth * block_len * strip * columns
    tile_bytes = depth * block_len * strip * 2
    one = columns * strip
    begin = call(begin_kernel, (shape(F32), shape(BF16), shape(BF16, n_seg)), 1, 0, one, 8 * one, 4)
    pair = call(pair_kernel, shape(BF16, 2), 2, 0, one, 8 * one, 2)
    products = (shape(F32), shape(BF16, 3), shape(BF16, 6))
    backward_load = call(
        backward_load_kernel,
        (*products, VMEM(tiles.shape, BF16)),
        3,
        1,
        flops,
        tile_bytes,
        8,
        tiles_in=1,
        scratch_shapes=[pltpu.SemaphoreType.DMA((depth,))],
    )
    backward = call(backward_kernel, products, 3, 1, flops, tile_bytes, 8)
    lend = call(lend_kernel, shape(BF16, 6), 5, 1, one, 12 * one, 4, input_output_aliases={1: 0})
    forward_even = call(forward_even_kernel, shape(F32, n_seg), 5, 1, flops * 4 // 7, tile_bytes, 8)
    forward_odd = call(forward_odd_kernel, shape(BF16, n_seg), 4, 1, flops * 3 // 7, tile_bytes, 8)
    combine = call(combine_kernel, (shape(BF16, 2), shape(BF16)), 3, 1, one, 18 * one, 4)
    relay = call(relay_kernel, shape(BF16), 2, 0, one, 6 * one, 2)
    update = call(update_kernel, (shape(F32), shape(BF16), shape(BF16, n_seg)), 9, 1, one, 12 * one, 8)
    final = call(final_kernel, jax.ShapeDtypeStruct((strip, columns), F32), 9, 1, one, 12 * one, 8)

    estimate, current, copies = begin(warm_start)
    for iteration in range(ITERS):
        far = shifted(current, -4)
        block = lax.all_to_all(copies, "seg", 0, 0)
        near = shifted(pair(current, far), -2)
        if iteration == 0:
            first, even, lent, held = backward_load(widths, tiles, block)
        else:
            first, even, lent = backward(widths, held, block)
        got = swapped(lend(odd, lent, current, near, far))
        total = forward_even(widths, held, current, near, far)
        back_pair, mid = combine(odd, even, got)
        back_near = shifted(back_pair, 2)
        partial = forward_odd(widths, held, got, total)
        summed = lax.all_to_all(partial, "seg", 0, 0)
        back_far = shifted(relay(mid, back_near), 4)
        operands = (odd, estimate, first, got, summed, back_near, back_far, scores_t, pen)
        if iteration < ITERS - 1:
            estimate, current, copies = update(*operands)
        else:
            return final(*operands)


def solution(mesh):
    in_specs = (
        P("chain", None, None, "seg"),
        P("chain"),
        P(("chain", "seg"), None),
        P(("chain", "seg"), None),
        P(),
    )
    out_specs = P(("chain", "seg"), None)
    return jax.shard_map(
        per_device, mesh=mesh, in_specs=in_specs, out_specs=out_specs, check_vma=False
    )
```

time: 181 us -> 109 us (0.60)
  the two profiles are of different devices: /device:TPU:65 before, /device:TPU:386 now
where the time goes in v2:
time: 109 us
  starting transfers between devices  50.9 us (47%)
  waiting for transfers between devices  41.3 us (38%)
  Pallas kernels  12.7 us (12%)
  local copies, waits for them, and re-layouts  3.09 us (3%)
    ppermute x8, waiting for transfers between devices, shifted(): return lax.ppermute(value, 'chain', pairs)  34.9 us
    ppermute x8, starting transfers between devices, shifted(): return lax.ppermute(value, 'chain', pairs)  27.8 us
    all_to_all x2, starting transfers between devices, per_device(): block = lax.all_to_all(copies, 'seg', 0, 0)  9.62 us
    all_to_all x2, starting transfers between devices, per_device(): summed = lax.all_to_all(partial, 'seg', 0, 0)  9.59 us
    pallas_call x1, Pallas kernels, per_device(): first, even, lent, held = backward_load(widths, tiles, block)  3.94 us
    ppermute x2, starting transfers between devices, swapped(): return lax.ppermute(value, 'chain', [(i, i ^ 1) for i in range(length)])  3.84 us
    ppermute x2, waiting for transfers between devices, swapped(): return lax.ppermute(value, 'chain', [(i, i ^ 1) for i in range(length)])  3.76 us
    unnamed x10, local copies, waits for them, and re-layouts  3 us
  transfers between devices with their start and end apart: 14, of which 11 were waited for; matrix products, arithmetic and copies ran while one was open for 0% of the time, Pallas kernels for 9%

profile of v2, /device:TPU:386, one launch (start us, length us, event | category | flops | bytes accessed | tf_op | source)
XLA Modules:
  0.0 108.8 jit_solution(18316044556330805246)
XLA Ops:
  0.0 0.0 copy-start.3
  0.0 0.9 copy-done.3
  1.0 1.0 shard_map.55
  1.9 4.8 %all-to-all-start = ((bf16[4,256,256]{2,1,0:T(8,128)(2,1)}), bf16[4,256,256]{2,1,0:T(8,128)(2,1)S(1)}, u32[]{:S(2)}, u32[]{:S(2)}) async-start(bf16[4,256,256]{2,1,0:T(8,128)(2,1)} %get-tuple-element.23), calls=%async_computation | async-start | bytes 1048576 | tf_op jit(solution)/shard_map/all_to_all | solution.py:228
  6.8 6.7 %collective-permute-start = (bf16[256,256]{1,0:T(8,128)(2,1)S(1)}, bf16[256,256]{1,0:T(8,128)(2,1)S(1)}, u32[]{:S(2)}, u32[]{:S(2)}) collective-permute-start(bf16[256,256]{1,0:T(8,128)(2,1)S(1)} %get-tuple-element.26.cur_ref), channel_id=1, source_target_pairs={{16,0},{20,4},{24,8},{28,12},{32,16},{36,20},{40,24},{44,28},{48,3... | collective-permute-start | bytes 393224 | tf_op jit(solution)/shard_map/ppermute | solution.py:27
  13.5 2.5 %collective-permute-done.far_ref = bf16[256,256]{1,0:T(8,128)(2,1)S(1)} collective-permute-done((bf16[256,256]{1,0:T(8,128)(2,1)S(1)}, bf16[256,256]{1,0:T(8,128)(2,1)S(1)}, u32[]{:S(2)}, u32[]{:S(2)}) %collective-permute-start) | collective-permute-done | bytes 131104 | tf_op jit(solution)/shard_map/ppermute | solution.py:27
  16.0 7.8 %collective-permute-start.1 = (bf16[2,256,256]{2,1,0:T(8,128)(2,1)S(1)}, bf16[2,256,256]{2,1,0:T(8,128)(2,1)S(1)}, u32[]{:S(2)}, u32[]{:S(2)}) collective-permute-start(bf16[2,256,256]{2,1,0:T(8,128)(2,1)S(1)} %shard_map.57), channel_id=1, source_target_pairs={{8,0},{12,4},{16,8},{20,12},{24,16},{28,20},{32,24},{36,28},{40,32... | collective-permute-start | bytes 786440 | tf_op jit(solution)/shard_map/ppermute | solution.py:27
  24.5 0.0 all-to-all-done.block_ref
  24.5 3.9 %shard_map.56 = (f32[256,256]{1,0:T(8,128)S(1)}, bf16[3,256,256]{2,1,0:T(8,128)(2,1)S(1)}, bf16[6,256,256]{2,1,0:T(8,128)(2,1)S(1)}, bf16[7,1024,256]{2,1,0:T(8,128)(2,1)S(1)}) custom-call(s32[1]{0:T(128)S(6)} %copy.10.widths_ref, bf16[7,1024,256]{2,1,0:T(8,128)(2,1)} %bitcast.7, bf16[4,256,256]{2,1,0:T(8,128)(2,1)S(1)} %all-to-all-done.block_ref), custom_call_target="tpu_custom_call" | custom-call | flops 939524096 | bytes 3670016 | tf_op jit(solution)/shard_map/pallas_call | solution.py:231
  28.4 0.0 copy-start
  28.4 0.0 collective-permute-done.1.near_ref
  28.5 1.9 %collective-permute-start.2 = (bf16[6,256,256]{2,1,0:T(8,128)(2,1)S(1)}, bf16[6,256,256]{2,1,0:T(8,128)(2,1)S(1)}, u32[]{:S(2)}, u32[]{:S(2)}) collective-permute-start(bf16[6,256,256]{2,1,0:T(8,128)(2,1)S(1)} %shard_map.58), channel_id=1, source_target_pairs={{0,4},{4,0},{8,12},{12,8},{16,20},{20,16},{24,28},{28,24},{32,36},... | collective-permute-start | bytes 2359304 | tf_op jit(solution)/shard_map/ppermute | solution.py:32
  30.4 2.3 %collective-permute-done.2.got_ref.refs_3_ = bf16[6,256,256]{2,1,0:T(8,128)(2,1)S(1)} collective-permute-done((bf16[6,256,256]{2,1,0:T(8,128)(2,1)S(1)}, bf16[6,256,256]{2,1,0:T(8,128)(2,1)S(1)}, u32[]{:S(2)}, u32[]{:S(2)}) %collective-permute-start.2) | collective-permute-done | bytes 786464 | tf_op jit(solution)/shard_map/ppermute | solution.py:32
  32.7 0.1 shard_map.61
  32.8 1.9 %collective-permute-start.3 = (bf16[2,256,256]{2,1,0:T(8,128)(2,1)S(1)}, bf16[2,256,256]{2,1,0:T(8,128)(2,1)S(1)}, u32[]{:S(2)}, u32[]{:S(2)}) collective-permute-start(bf16[2,256,256]{2,1,0:T(8,128)(2,1)S(1)} %get-tuple-element.29), channel_id=1, source_target_pairs={{0,8},{4,12},{8,16},{12,20},{16,24},{20,28},{24,32},{28,36},{32,40... | collective-permute-start | bytes 786440 | tf_op jit(solution)/shard_map/ppermute | solution.py:27
  34.7 0.7 shard_map.59.total_ref
  35.4 0.0 copy-done
  35.5 0.0 copy-start.4
  35.5 0.0 copy-start.2
  35.5 1.4 %shard_map.60 = bf16[4,256,256]{2,1,0:T(8,128)(2,1)} custom-call(s32[1]{0:T(128)S(6)} %copy.10.widths_ref, bf16[7,1024,256]{2,1,0:T(8,128)(2,1)S(1)} %get-tuple-element.27.held, bf16[6,256,256]{2,1,0:T(8,128)(2,1)S(1)} %collective-permute-done.2.got_ref.refs_3_, f32[4,256,256]{2,1,0:T(8,128)S(1)} %shard_map.59.total_ref), custom_call_target="tpu_custom_call" | custom-call | flops 402653184 | bytes 3670016 | tf_op jit(solution)/shard_map/pallas_call | solution.py:238
  36.9 4.8 %all-to-all-start.1 = ((bf16[4,256,256]{2,1,0:T(8,128)(2,1)}), bf16[4,256,256]{2,1,0:T(8,128)(2,1)S(1)}, u32[]{:S(2)}, u32[]{:S(2)}) async-start(bf16[4,256,256]{2,1,0:T(8,128)(2,1)} %shard_map.60), calls=%async_computation.1 | async-start | bytes 1048576 | tf_op jit(solution)/shard_map/all_to_all | solution.py:239
  41.7 4.6 %collective-permute-done.3.near_ref.refs_5_ = bf16[2,256,256]{2,1,0:T(8,128)(2,1)S(1)} collective-permute-done((bf16[2,256,256]{2,1,0:T(8,128)(2,1)S(1)}, bf16[2,256,256]{2,1,0:T(8,128)(2,1)S(1)}, u32[]{:S(2)}, u32[]{:S(2)}) %collective-permute-start.3) | collective-permute-done | bytes 262176 | tf_op jit(solution)/shard_map/ppermute | solution.py:27
  46.4 1.9 %collective-permute-start.4 = (bf16[256,256]{1,0:T(8,128)(2,1)S(1)}, bf16[256,256]{1,0:T(8,128)(2,1)S(1)}, u32[]{:S(2)}, u32[]{:S(2)}) collective-permute-start(bf16[256,256]{1,0:T(8,128)(2,1)S(1)} %shard_map.62), channel_id=1, source_target_pairs={{0,16},{4,20},{8,24},{12,28},{16,32},{20,36},{24,40},{28,44},{32,4... | collective-permute-start | bytes 393224 | tf_op jit(solution)/shard_map/ppermute | solution.py:27
  48.3 0.0 copy-done.4
  48.3 1.7 %all-to-all-done.1.refs_4_ = bf16[4,256,256]{2,1,0:T(8,128)(2,1)S(1)} async-done(((bf16[4,256,256]{2,1,0:T(8,128)(2,1)}), bf16[4,256,256]{2,1,0:T(8,128)(2,1)S(1)}, u32[]{:S(2)}, u32[]{:S(2)}) %all-to-all-start.1) | async-done | bytes 524320 | tf_op jit(solution)/shard_map/all_to_all | solution.py:239
  50.0 6.9 %collective-permute-done.4.refs_6_ = bf16[256,256]{1,0:T(8,128)(2,1)S(1)} collective-permute-done((bf16[256,256]{1,0:T(8,128)(2,1)S(1)}, bf16[256,256]{1,0:T(8,128)(2,1)S(1)}, u32[]{:S(2)}, u32[]{:S(2)}) %collective-permute-start.4) | collective-permute-done | bytes 131104 | tf_op jit(solution)/shard_map/ppermute | solution.py:27
  56.8 0.1 broadcast_in_dim.2.refs_8_
  56.9 0.0 copy-done.2
  56.9 1.0 shard_map.63
  57.9 4.8 %all-to-all-start.2 = ((bf16[4,256,256]{2,1,0:T(8,128)(2,1)}), bf16[4,256,256]{2,1,0:T(8,128)(2,1)S(1)}, u32[]{:S(2)}, u32[]{:S(2)}) async-start(bf16[4,256,256]{2,1,0:T(8,128)(2,1)} %get-tuple-element.32), calls=%async_computation.2 | async-start | bytes 1048576 | tf_op jit(solution)/shard_map/all_to_all | solution.py:228
  62.7 1.9 %collective-permute-start.5 = (bf16[256,256]{1,0:T(8,128)(2,1)S(1)}, bf16[256,256]{1,0:T(8,128)(2,1)S(1)}, u32[]{:S(2)}, u32[]{:S(2)}) collective-permute-start(bf16[256,256]{1,0:T(8,128)(2,1)S(1)} %get-tuple-element.35.cur_ref), channel_id=1, source_target_pairs={{16,0},{20,4},{24,8},{28,12},{32,16},{36,20},{40,24},{44,28},{48,3... | collective-permute-start | bytes 393224 | tf_op jit(solution)/shard_map/ppermute | solution.py:27
  64.7 6.4 %collective-permute-done.5.far_ref = bf16[256,256]{1,0:T(8,128)(2,1)S(1)} collective-permute-done((bf16[256,256]{1,0:T(8,128)(2,1)S(1)}, bf16[256,256]{1,0:T(8,128)(2,1)S(1)}, u32[]{:S(2)}, u32[]{:S(2)}) %collective-permute-start.5) | collective-permute-done | bytes 131104 | tf_op jit(solution)/shard_map/ppermute | solution.py:27
  71.1 3.7 %collective-permute-start.6 = (bf16[2,256,256]{2,1,0:T(8,128)(2,1)S(1)}, bf16[2,256,256]{2,1,0:T(8,128)(2,1)S(1)}, u32[]{:S(2)}, u32[]{:S(2)}) collective-permute-start(bf16[2,256,256]{2,1,0:T(8,128)(2,1)S(1)} %shard_map.65), channel_id=1, source_target_pairs={{8,0},{12,4},{16,8},{20,12},{24,16},{28,20},{32,24},{36,28},{40,32... | collective-permute-start | bytes 786440 | tf_op jit(solution)/shard_map/ppermute | solution.py:27
  74.8 0.0 all-to-all-done.2.block_ref
  74.8 0.0 copy-start.1
  74.9 2.0 %copy-done.1 = bf16[7,1024,256]{2,1,0:T(8,128)(2,1)S(1)} copy-done((bf16[7,1024,256]{2,1,0:T(8,128)(2,1)S(1)}, bf16[7,1024,256]{2,1,0:T(8,128)(2,1)}, u32[]{:S(2)}) %copy-start.1) | copy-done | bytes 3670040
  76.9 1.1 %shard_map.64 = (f32[256,256]{1,0:T(8,128)S(1)}, bf16[3,256,256]{2,1,0:T(8,128)(2,1)S(1)}, bf16[6,256,256]{2,1,0:T(8,128)(2,1)S(1)}) custom-call(s32[1]{0:T(128)S(6)} %copy.10.widths_ref, bf16[7,1024,256]{2,1,0:T(8,128)(2,1)S(1)} %copy-done.1, bf16[4,256,256]{2,1,0:T(8,128)(2,1)S(1)} %all-to-all-done.2.block_ref), custom_call_target="tpu_custom_call" | custom-call | flops 939524096 | bytes 3670016 | tf_op jit(solution)/shard_map/pallas_call | solution.py:233
  78.0 1.4 %collective-permute-done.6.near_ref = bf16[2,256,256]{2,1,0:T(8,128)(2,1)S(1)} collective-permute-done((bf16[2,256,256]{2,1,0:T(8,128)(2,1)S(1)}, bf16[2,256,256]{2,1,0:T(8,128)(2,1)S(1)}, u32[]{:S(2)}, u32[]{:S(2)}) %collective-permute-start.6) | collective-permute-done | bytes 262176 | tf_op jit(solution)/shard_map/ppermute | solution.py:27
  79.4 1.9 %collective-permute-start.7 = (bf16[6,256,256]{2,1,0:T(8,128)(2,1)S(1)}, bf16[6,256,256]{2,1,0:T(8,128)(2,1)S(1)}, u32[]{:S(2)}, u32[]{:S(2)}) collective-permute-start(bf16[6,256,256]{2,1,0:T(8,128)(2,1)S(1)} %shard_map.66), channel_id=1, source_target_pairs={{0,4},{4,0},{8,12},{12,8},{16,20},{20,16},{24,28},{28,24},{32,36},... | collective-permute-start | bytes 2359304 | tf_op jit(solution)/shard_map/ppermute | solution.py:32
  81.3 0.7 shard_map.67.total_ref
  82.1 1.5 %collective-permute-done.7.got_ref.refs_3_ = bf16[6,256,256]{2,1,0:T(8,128)(2,1)S(1)} collective-permute-done((bf16[6,256,256]{2,1,0:T(8,128)(2,1)S(1)}, bf16[6,256,256]{2,1,0:T(8,128)(2,1)S(1)}, u32[]{:S(2)}, u32[]{:S(2)}) %collective-permute-start.7) | collective-permute-done | bytes 786464 | tf_op jit(solution)/shard_map/ppermute | solution.py:32
  83.6 0.1 shard_map.69
  83.7 1.9 %collective-permute-start.8 = (bf16[2,256,256]{2,1,0:T(8,128)(2,1)S(1)}, bf16[2,256,256]{2,1,0:T(8,128)(2,1)S(1)}, u32[]{:S(2)}, u32[]{:S(2)}) collective-permute-start(bf16[2,256,256]{2,1,0:T(8,128)(2,1)S(1)} %get-tuple-element.37), channel_id=1, source_target_pairs={{0,8},{4,12},{8,16},{12,20},{16,24},{20,28},{24,32},{28,36},{32,40... | collective-permute-start | bytes 786440 | tf_op jit(solution)/shard_map/ppermute | solution.py:27
  85.6 1.4 %shard_map.68 = bf16[4,256,256]{2,1,0:T(8,128)(2,1)} custom-call(s32[1]{0:T(128)S(6)} %copy.10.widths_ref, bf16[7,1024,256]{2,1,0:T(8,128)(2,1)S(1)} %copy-done.1, bf16[6,256,256]{2,1,0:T(8,128)(2,1)S(1)} %collective-permute-done.7.got_ref.refs_3_, f32[4,256,256]{2,1,0:T(8,128)S(1)} %shard_map.67.total_ref), custom_call_target="tpu_custom_call" | custom-call | flops 402653184 | bytes 3670016 | tf_op jit(solution)/shard_map/pallas_call | solution.py:238
  87.0 4.8 %all-to-all-start.3 = ((bf16[4,256,256]{2,1,0:T(8,128)(2,1)}), bf16[4,256,256]{2,1,0:T(8,128)(2,1)S(1)}, u32[]{:S(2)}, u32[]{:S(2)}) async-start(bf16[4,256,256]{2,1,0:T(8,128)(2,1)} %shard_map.68), calls=%async_computation.3 | async-start | bytes 1048576 | tf_op jit(solution)/shard_map/all_to_all | solution.py:239
  91.8 5.5 %collective-permute-done.8.near_ref.refs_5_ = bf16[2,256,256]{2,1,0:T(8,128)(2,1)S(1)} collective-permute-done((bf16[2,256,256]{2,1,0:T(8,128)(2,1)S(1)}, bf16[2,256,256]{2,1,0:T(8,128)(2,1)S(1)}, u32[]{:S(2)}, u32[]{:S(2)}) %collective-permute-start.8) | collective-permute-done | bytes 262176 | tf_op jit(solution)/shard_map/ppermute | solution.py:27
  97.3 1.9 %collective-permute-start.9 = (bf16[256,256]{1,0:T(8,128)(2,1)S(1)}, bf16[256,256]{1,0:T(8,128)(2,1)S(1)}, u32[]{:S(2)}, u32[]{:S(2)}) collective-permute-start(bf16[256,256]{1,0:T(8,128)(2,1)S(1)} %shard_map.70), channel_id=1, source_target_pairs={{0,16},{4,20},{8,24},{12,28},{16,32},{20,36},{24,40},{28,44},{32,4... | collective-permute-start | bytes 393224 | tf_op jit(solution)/shard_map/ppermute | solution.py:27
  99.3 0.9 all-to-all-done.3.refs_4_
  100.1 7.7 %collective-permute-done.9.refs_6_ = bf16[256,256]{1,0:T(8,128)(2,1)S(1)} collective-permute-done((bf16[256,256]{1,0:T(8,128)(2,1)S(1)}, bf16[256,256]{1,0:T(8,128)(2,1)S(1)}, u32[]{:S(2)}, u32[]{:S(2)}) %collective-permute-start.9) | collective-permute-done | bytes 131104 | tf_op jit(solution)/shard_map/ppermute | solution.py:27
  107.8 1.0 shard_map.71
  (7 shorter events, 0.2 us)
Async XLA Ops:
  0.0 0.9 copy-start.3
  1.9 22.6 %all-to-all-start = ((bf16[4,256,256]{2,1,0:T(8,128)(2,1)}), bf16[4,256,256]{2,1,0:T(8,128)(2,1)S(1)}, u32[]{:S(2)}, u32[]{:S(2)}) async-start(bf16[4,256,256]{2,1,0:T(8,128)(2,1)} %get-tuple-element.23), calls=%async_computation | async-start | bytes 1048576 | tf_op jit(solution)/shard_map/all_to_all | solution.py:228
  6.8 9.3 %collective-permute-start = (bf16[256,256]{1,0:T(8,128)(2,1)S(1)}, bf16[256,256]{1,0:T(8,128)(2,1)S(1)}, u32[]{:S(2)}, u32[]{:S(2)}) collective-permute-start(bf16[256,256]{1,0:T(8,128)(2,1)S(1)} %get-tuple-element.26.cur_ref), channel_id=1, source_target_pairs={{16,0},{20,4},{24,8},{28,12},{32,16},{36,20},{40,24},{44,28},{48,3... | collective-permute-start | bytes 393224 | tf_op jit(solution)/shard_map/ppermute | solution.py:27
  16.0 12.4 %collective-permute-start.1 = (bf16[2,256,256]{2,1,0:T(8,128)(2,1)S(1)}, bf16[2,256,256]{2,1,0:T(8,128)(2,1)S(1)}, u32[]{:S(2)}, u32[]{:S(2)}) collective-permute-start(bf16[2,256,256]{2,1,0:T(8,128)(2,1)S(1)} %shard_map.57), channel_id=1, source_target_pairs={{8,0},{12,4},{16,8},{20,12},{24,16},{28,20},{32,24},{36,28},{40,32... | collective-permute-start | bytes 786440 | tf_op jit(solution)/shard_map/ppermute | solution.py:27
  28.4 7.0 %copy-start = (bf16[7,1024,256]{2,1,0:T(8,128)(2,1)}, bf16[7,1024,256]{2,1,0:T(8,128)(2,1)S(1)}, u32[]{:S(2)}) copy-start(bf16[7,1024,256]{2,1,0:T(8,128)(2,1)S(1)} %get-tuple-element.27.held) | copy-start | bytes 11010052
  28.5 4.2 %collective-permute-start.2 = (bf16[6,256,256]{2,1,0:T(8,128)(2,1)S(1)}, bf16[6,256,256]{2,1,0:T(8,128)(2,1)S(1)}, u32[]{:S(2)}, u32[]{:S(2)}) collective-permute-start(bf16[6,256,256]{2,1,0:T(8,128)(2,1)S(1)} %shard_map.58), channel_id=1, source_target_pairs={{0,4},{4,0},{8,12},{12,8},{16,20},{20,16},{24,28},{28,24},{32,36},... | collective-permute-start | bytes 2359304 | tf_op jit(solution)/shard_map/ppermute | solution.py:32
  32.8 13.5 %collective-permute-start.3 = (bf16[2,256,256]{2,1,0:T(8,128)(2,1)S(1)}, bf16[2,256,256]{2,1,0:T(8,128)(2,1)S(1)}, u32[]{:S(2)}, u32[]{:S(2)}) collective-permute-start(bf16[2,256,256]{2,1,0:T(8,128)(2,1)S(1)} %get-tuple-element.29), channel_id=1, source_target_pairs={{0,8},{4,12},{8,16},{12,20},{16,24},{20,28},{24,32},{28,36},{32,40... | collective-permute-start | bytes 786440 | tf_op jit(solution)/shard_map/ppermute | solution.py:27
  35.5 12.8 %copy-start.4 = (f32[256]{0:T(256)S(1)}, f32[256]{0:T(256)}, u32[]{:S(2)}) copy-start(f32[256]{0:T(256)} %param.9) | copy-start | bytes 3076
  35.5 21.5 %copy-start.2 = (f32[256,64]{0,1:T(8,128)S(1)}, f32[256,64]{0,1:T(8,128)}, u32[]{:S(2)}) copy-start(f32[256,64]{0,1:T(8,128)} %param.8) | copy-start | bytes 196612
  36.9 13.1 %all-to-all-start.1 = ((bf16[4,256,256]{2,1,0:T(8,128)(2,1)}), bf16[4,256,256]{2,1,0:T(8,128)(2,1)S(1)}, u32[]{:S(2)}, u32[]{:S(2)}) async-start(bf16[4,256,256]{2,1,0:T(8,128)(2,1)} %shard_map.60), calls=%async_computation.1 | async-start | bytes 1048576 | tf_op jit(solution)/shard_map/all_to_all | solution.py:239
  46.4 10.5 %collective-permute-start.4 = (bf16[256,256]{1,0:T(8,128)(2,1)S(1)}, bf16[256,256]{1,0:T(8,128)(2,1)S(1)}, u32[]{:S(2)}, u32[]{:S(2)}) collective-permute-start(bf16[256,256]{1,0:T(8,128)(2,1)S(1)} %shard_map.62), channel_id=1, source_target_pairs={{0,16},{4,20},{8,24},{12,28},{16,32},{20,36},{24,40},{28,44},{32,4... | collective-permute-start | bytes 393224 | tf_op jit(solution)/shard_map/ppermute | solution.py:27
  57.9 16.9 %all-to-all-start.2 = ((bf16[4,256,256]{2,1,0:T(8,128)(2,1)}), bf16[4,256,256]{2,1,0:T(8,128)(2,1)S(1)}, u32[]{:S(2)}, u32[]{:S(2)}) async-start(bf16[4,256,256]{2,1,0:T(8,128)(2,1)} %get-tuple-element.32), calls=%async_computation.2 | async-start | bytes 1048576 | tf_op jit(solution)/shard_map/all_to_all | solution.py:228
  62.7 8.4 %collective-permute-start.5 = (bf16[256,256]{1,0:T(8,128)(2,1)S(1)}, bf16[256,256]{1,0:T(8,128)(2,1)S(1)}, u32[]{:S(2)}, u32[]{:S(2)}) collective-permute-start(bf16[256,256]{1,0:T(8,128)(2,1)S(1)} %get-tuple-element.35.cur_ref), channel_id=1, source_target_pairs={{16,0},{20,4},{24,8},{28,12},{32,16},{36,20},{40,24},{44,28},{48,3... | collective-permute-start | bytes 393224 | tf_op jit(solution)/shard_map/ppermute | solution.py:27
  71.1 8.3 %collective-permute-start.6 = (bf16[2,256,256]{2,1,0:T(8,128)(2,1)S(1)}, bf16[2,256,256]{2,1,0:T(8,128)(2,1)S(1)}, u32[]{:S(2)}, u32[]{:S(2)}) collective-permute-start(bf16[2,256,256]{2,1,0:T(8,128)(2,1)S(1)} %shard_map.65), channel_id=1, source_target_pairs={{8,0},{12,4},{16,8},{20,12},{24,16},{28,20},{32,24},{36,28},{40,32... | collective-permute-start | bytes 786440 | tf_op jit(solution)/shard_map/ppermute | solution.py:27
  74.8 2.0 %copy-start.1 = (bf16[7,1024,256]{2,1,0:T(8,128)(2,1)S(1)}, bf16[7,1024,256]{2,1,0:T(8,128)(2,1)}, u32[]{:S(2)}) copy-start(bf16[7,1024,256]{2,1,0:T(8,128)(2,1)} %copy-done) | copy-start | bytes 11010052
  79.4 4.2 %collective-permute-start.7 = (bf16[6,256,256]{2,1,0:T(8,128)(2,1)S(1)}, bf16[6,256,256]{2,1,0:T(8,128)(2,1)S(1)}, u32[]{:S(2)}, u32[]{:S(2)}) collective-permute-start(bf16[6,256,256]{2,1,0:T(8,128)(2,1)S(1)} %shard_map.66), channel_id=1, source_target_pairs={{0,4},{4,0},{8,12},{12,8},{16,20},{20,16},{24,28},{28,24},{32,36},... | collective-permute-start | bytes 2359304 | tf_op jit(solution)/shard_map/ppermute | solution.py:32
  83.7 13.6 %collective-permute-start.8 = (bf16[2,256,256]{2,1,0:T(8,128)(2,1)S(1)}, bf16[2,256,256]{2,1,0:T(8,128)(2,1)S(1)}, u32[]{:S(2)}, u32[]{:S(2)}) collective-permute-start(bf16[2,256,256]{2,1,0:T(8,128)(2,1)S(1)} %get-tuple-element.37), channel_id=1, source_target_pairs={{0,8},{4,12},{8,16},{12,20},{16,24},{20,28},{24,32},{28,36},{32,40... | collective-permute-start | bytes 786440 | tf_op jit(solution)/shard_map/ppermute | solution.py:27
  87.0 13.1 %all-to-all-start.3 = ((bf16[4,256,256]{2,1,0:T(8,128)(2,1)}), bf16[4,256,256]{2,1,0:T(8,128)(2,1)S(1)}, u32[]{:S(2)}, u32[]{:S(2)}) async-start(bf16[4,256,256]{2,1,0:T(8,128)(2,1)} %shard_map.68), calls=%async_computation.3 | async-start | bytes 1048576 | tf_op jit(solution)/shard_map/all_to_all | solution.py:239
  97.3 10.5 %collective-permute-start.9 = (bf16[256,256]{1,0:T(8,128)(2,1)S(1)}, bf16[256,256]{1,0:T(8,128)(2,1)S(1)}, u32[]{:S(2)}, u32[]{:S(2)}) collective-permute-start(bf16[256,256]{1,0:T(8,128)(2,1)S(1)} %shard_map.70), channel_id=1, source_target_pairs={{0,16},{4,20},{8,24},{12,28},{16,32},{20,36},{24,40},{28,44},{32,4... | collective-permute-start | bytes 393224 | tf_op jit(solution)/shard_map/ppermute | solution.py:27

commit v3 on v2

v3 whole, which is shorter than its diff:
```python
import jax
import jax.numpy as jnp
from jax import lax
from jax.experimental import pallas as pl
from jax.experimental.pallas import tpu as pltpu
from jax.sharding import PartitionSpec as P


ITERS = 2
EARLY = 2


step_size = 0.8

VMEM = pltpu.VMEM
HBM = pltpu.HBM
F32 = jnp.float32
BF16 = jnp.bfloat16


def spec(space=None):
    return pl.BlockSpec(memory_space=VMEM if space is None else space)


def shifted(value, by):
    length = lax.axis_size("chain")
    pairs = [(i, i + by) for i in range(length) if 0 <= i + by < length]
    return lax.ppermute(value, "chain", pairs)


def swapped(value):
    length = lax.axis_size("chain")
    return lax.ppermute(value, "chain", [(i, i ^ 1) for i in range(length)])


def is_odd():
    return lax.rem(lax.axis_index("chain"), 2) == 1


def soft_limit(values, limit):
    return jnp.maximum(values - limit, 0.0) + jnp.minimum(values + limit, 0.0)


def send_copies(cur_ref, copies_ref, sems):
    copies = [
        pltpu.make_async_copy(cur_ref, copies_ref.at[s], sems.at[s])
        for s in range(copies_ref.shape[0])
    ]
    for copy in copies:
        copy.start()
    return copies


def begin_kernel(warm_ref, est_ref, cur_ref, copies_ref, held, in_sems, out_sems):
    parts, rows, _ = held.shape
    loads = [
        pltpu.make_async_copy(warm_ref.at[pl.ds(i * rows, rows), :], held.at[i], in_sems.at[i])
        for i in range(parts)
    ]
    for load in loads:
        load.start()
    for i, load in enumerate(loads):
        load.wait()
        est = held[i].T
        est_ref[:, i * rows : (i + 1) * rows] = est
        cur_ref[:, i * rows : (i + 1) * rows] = est.astype(BF16)
    for copy in send_copies(cur_ref, copies_ref, out_sems):
        copy.wait()


def pair_kernel(cur_ref, far_ref, out_ref):
    out_ref[0] = cur_ref[...]
    out_ref[1] = far_ref[...]


def load_kernel(tiles_ref, far_ref, held, sem):
    del far_ref
    copy = pltpu.make_async_copy(tiles_ref.at[pl.ds(0, EARLY)], held, sem)
    copy.start()
    copy.wait()


def backward_kernel(
    widths_ref, tiles_ref, early_ref, block_ref, first_ref, even_ref, lent_ref, late_ref, sems
):
    late = late_ref.shape[0]
    copies = [
        pltpu.make_async_copy(tiles_ref.at[EARLY + i], late_ref.at[i], sems.at[i])
        for i in range(late)
    ]
    for copy in copies:
        copy.start()
    block = jnp.concatenate([block_ref[s] for s in range(block_ref.shape[0])], axis=1)
    for j in range(EARLY + late):
        if j >= EARLY:
            copies[j - EARLY].wait()
        tile = early_ref[j] if j < EARLY else late_ref[j - EARLY]
        total = jnp.dot(block, tile, preferred_element_type=F32)
        total = jnp.where(j <= widths_ref[0], total, 0.0)
        if j == 0:
            first_ref[...] = total
        elif j % 2 == 0:
            even_ref[j // 2 - 1] = total.astype(BF16)
        else:
            lent_ref[3 + j // 2] = total.astype(BF16)


def lend_kernel(lent_ref, cur_ref, near_ref, far_ref, out_ref):
    del lent_ref

    @pl.when(is_odd())
    def _():
        out_ref[0] = cur_ref[...]
        out_ref[1] = near_ref[0]
        out_ref[2] = far_ref[...]

    @pl.when(jnp.logical_not(is_odd()))
    def _():
        out_ref[0] = near_ref[0]
        out_ref[1] = far_ref[...]
        out_ref[2] = near_ref[1]


def forward_product(widths_ref, early_ref, late_ref, values, offsets, s):
    strip = early_ref.shape[2]
    rows = pl.ds(s * strip, strip)
    left = jnp.concatenate(
        [jnp.where(j <= widths_ref[0], v, jnp.zeros_like(v)) for j, v in zip(offsets, values)],
        axis=1,
    )
    right = jnp.concatenate(
        [early_ref[j, rows, :] if j < EARLY else late_ref[j - EARLY, rows, :] for j in offsets],
        axis=1,
    )
    return lax.dot_general(left, right, (((1,), (1,)), ((), ())), preferred_element_type=F32)


def forward_even_kernel(widths_ref, early_ref, late_ref, cur_ref, near_ref, far_ref, total_ref):
    values = [cur_ref[...], near_ref[0], far_ref[...], near_ref[1]]
    for s in range(total_ref.shape[0]):
        total_ref[s] = forward_product(widths_ref, early_ref, late_ref, values, (0, 2, 4, 6), s)


def forward_odd_kernel(widths_ref, early_ref, late_ref, got_ref, total_ref, out_ref, parts, sems):
    values = [got_ref[0], got_ref[1], got_ref[2]]
    copies = []
    for s in range(out_ref.shape[0]):
        term = forward_product(widths_ref, early_ref, late_ref, values, (1, 3, 5), s)
        parts[s] = (total_ref[s] + term).astype(BF16)
        copies.append(pltpu.make_async_copy(parts.at[s], out_ref.at[s], sems.at[s]))
        copies[-1].start()
    for copy in copies:
        copy.wait()


def combine_kernel(even_ref, got_ref, pair_ref, mid_ref):
    def add(k, other):
        return (even_ref[k].astype(F32) + other.astype(F32)).astype(BF16)

    @pl.when(is_odd())
    def _():
        pair_ref[0] = add(0, got_ref[4])
        mid_ref[...] = add(1, got_ref[5])
        pair_ref[1] = even_ref[2]

    @pl.when(jnp.logical_not(is_odd()))
    def _():
        pair_ref[0] = add(0, got_ref[3])
        mid_ref[...] = add(1, got_ref[4])
        pair_ref[1] = add(2, got_ref[5])


def relay_kernel(mid_ref, near_ref, out_ref):
    out_ref[...] = (mid_ref[...].astype(F32) + near_ref[1].astype(F32)).astype(BF16)


def settle_kernel(est_ref, first_ref, got_ref, near_ref, scores_ref, out_ref):
    coupled = first_ref[...] + jnp.where(is_odd(), got_ref[3].astype(F32), 0.0)
    coupled = coupled + near_ref[0].astype(F32)
    est = est_ref[...]
    columns, traits = est.shape[0], scores_ref.shape[0]
    target = jnp.concatenate([scores_ref[...]] * (columns // traits), axis=0)
    out_ref[...] = est - step_size * (est + coupled - target)


def new_estimate(settled_ref, seg_ref, far_ref, pen_ref):
    coupled = far_ref[...].astype(F32)
    for s in range(seg_ref.shape[0]):
        coupled = coupled + seg_ref[s].astype(F32)
    return soft_limit(settled_ref[...] - step_size * coupled, pen_ref[...])


def update_kernel(settled_ref, seg_ref, far_ref, pen_ref, new_ref, cur_ref, copies_ref, sems):
    est = new_estimate(settled_ref, seg_ref, far_ref, pen_ref)
    cur_ref[...] = est.astype(BF16)
    copies = send_copies(cur_ref, copies_ref, sems)
    new_ref[...] = est
    for copy in copies:
        copy.wait()


def final_kernel(settled_ref, seg_ref, far_ref, pen_ref, out_ref):
    out_ref[...] = new_estimate(settled_ref, seg_ref, far_ref, pen_ref).T


def call(kernel, out_shape, n_in, scalars, flops, nbytes, mib, outside=(), out_outside=(), **more):
    ins = [spec(pltpu.SMEM)] * scalars + [spec()] * (n_in - scalars)
    for i in outside:
        ins[i] = spec(HBM)
    many = isinstance(out_shape, tuple)
    outs = [spec()] * (len(out_shape) if many else 1)
    for i in out_outside:
        outs[i] = spec(HBM)
    return pl.pallas_call(
        kernel,
        out_shape=out_shape,
        in_specs=ins,
        out_specs=tuple(outs) if many else outs[0],
        cost_estimate=pl.CostEstimate(flops=flops, bytes_accessed=nbytes, transcendentals=0),
        compiler_params=pltpu.CompilerParams(vmem_limit_bytes=mib << 20),
        **more,
    )


def per_device(band_tiles, widths, warm_start, scores, penalty):
    n_seg = lax.axis_size("seg")
    tiles = pltpu.with_memory_space_constraint(jnp.transpose(band_tiles[0], (1, 0, 2)), HBM)
    depth, block_len, strip = tiles.shape
    columns = warm_start.shape[1]
    scores_t = scores.T
    pen = jnp.broadcast_to((step_size * penalty)[:, None], (columns, strip))

    def shape(dtype, *lead):
        return jax.ShapeDtypeStruct((*lead, columns, strip), dtype)

    flops = 2 * depth * block_len * strip * columns
    tile_bytes = depth * block_len * strip * 2
    one = columns * strip
    seg_sems = pltpu.SemaphoreType.DMA((n_seg,))
    fresh = (shape(F32), shape(BF16), HBM((n_seg, columns, strip), BF16))
    begin = call(
        begin_kernel,
        fresh,
        1,
        0,
        one,
        8 * one,
        4,
        outside=(0,),
        out_outside=(2,),
        scratch_shapes=[VMEM((2, strip // 2, columns), F32), pltpu.SemaphoreType.DMA((2,)), seg_sems],
    )
    pair = call(pair_kernel, shape(BF16, 2), 2, 0, one, 8 * one, 2)
    load = call(
        load_kernel,
        jax.ShapeDtypeStruct((EARLY, block_len, strip), BF16),
        2,
        0,
        one,
        tile_bytes * EARLY // depth,
        4,
        outside=(0,),
        scratch_shapes=[pltpu.SemaphoreType.DMA],
    )
    backward = call(
        backward_kernel,
        (
            shape(F32),
            shape(BF16, 3),
            shape(BF16, 6),
            jax.ShapeDtypeStruct((depth - EARLY, block_len, strip), BF16),
        ),
        4,
        1,
        flops,
        tile_bytes,
        8,
        outside=(1,),
        scratch_shapes=[pltpu.SemaphoreType.DMA((depth - EARLY,))],
    )
    lend = call(lend_kernel, shape(BF16, 6), 4, 0, one, 12 * one, 4, input_output_aliases={0: 0})
    forward_even = call(forward_even_kernel, shape(F32, n_seg), 6, 1, flops * 4 // 7, tile_bytes, 8)
    forward_odd = call(
        forward_odd_kernel,
        HBM((n_seg, columns, strip), BF16),
        5,
        1,
        flops * 3 // 7,
        tile_bytes,
        8,
        out_outside=(0,),
        scratch_shapes=[VMEM((n_seg, columns, strip), BF16), seg_sems],
    )
    combine = call(combine_kernel, (shape(BF16, 2), shape(BF16)), 2, 0, one, 18 * one, 4)
    relay = call(relay_kernel, shape(BF16), 2, 0, one, 6 * one, 2)
    settle = call(settle_kernel, shape(F32), 5, 0, one, 14 * one, 4)
    update = call(
        update_kernel, fresh, 4, 0, one, 12 * one, 6, out_outside=(2,), scratch_shapes=[seg_sems]
    )
    final = call(final_kernel, jax.ShapeDtypeStruct((strip, columns), F32), 4, 0, one, 12 * one, 6)

    estimate, current, copies = begin(pltpu.with_memory_space_constraint(warm_start, HBM))
    for iteration in range(ITERS):
        far = shifted(current, -4)
        block = lax.all_to_all(copies, "seg", 0, 0)
        near = shifted(pair(current, far), -2)
        early = load(tiles, far)
        first, even, lent, late = backward(widths, tiles, early, block)
        got = swapped(lend(lent, current, near, far))
        total = forward_even(widths, early, late, current, near, far)
        back_pair, mid = combine(even, got)
        back_near = shifted(back_pair, 2)
        partial = forward_odd(widths, early, late, got, total)
        summed = lax.all_to_all(partial, "seg", 0, 0)
        back_far = shifted(relay(mid, back_near), 4)
        settled = settle(estimate, first, got, back_near, scores_t)
        if iteration < ITERS - 1:
            estimate, current, copies = update(settled, summed, back_far, pen)
        else:
            return final(settled, summed, back_far, pen)


def solution(mesh):
    in_specs = (
        P("chain", None, None, "seg"),
        P("chain"),
        P(("chain", "seg"), None),
        P(("chain", "seg"), None),
        P(),
    )
    out_specs = P(("chain", "seg"), None)
    return jax.shard_map(
        per_device, mesh=mesh, in_specs=in_specs, out_specs=out_specs, check_vma=False
    )
```

time: 109 us -> 111 us (1.018)
  Pallas kernels: 12.7 us -> 18.2 us
  local copies, waits for them, and re-layouts: 3.09 us -> 0.11 us
    pallas_call x13 -> x17, Pallas kernels: 12.5 us -> 18.1 us  [the longest x2 6.42 us: per_device(): first, even, lent, late = backward(widths, tiles, early, block)]
    unnamed x10 -> x4, local copies, waits for them, and re-layouts: 3 us -> 0.01 us
  transfers between devices with their start and end apart: 14 -> 14, of which waited for: 11 -> 11; matrix products, arithmetic and copies ran while one was open for 0% -> 0% of each run, Pallas kernels for 9% -> 12%
where the time goes in v3:
time: 111 us; the launch traced here: 110 us
  starting transfers between devices  50.6 us (46%)
  waiting for transfers between devices  40.3 us (36%)
  Pallas kernels  18.2 us (16%)
    ppermute x8, waiting for transfers between devices, shifted(): return lax.ppermute(value, 'chain', pairs)  34.4 us
    ppermute x8, starting transfers between devices, shifted(): return lax.ppermute(value, 'chain', pairs)  27.5 us
    all_to_all x2, starting transfers between devices, per_device(): block = lax.all_to_all(copies, 'seg', 0, 0)  9.65 us
    all_to_all x2, starting transfers between devices, per_device(): summed = lax.all_to_all(partial, 'seg', 0, 0)  9.62 us
    pallas_call x2, Pallas kernels, per_device(): first, even, lent, late = backward(widths, tiles, early, block)  6.42 us
    ppermute x2, starting transfers between devices, swapped(): return lax.ppermute(value, 'chain', [(i, i ^ 1) for i in range(length)])  3.84 us
    ppermute x2, waiting for transfers between devices, swapped(): return lax.ppermute(value, 'chain', [(i, i ^ 1) for i in range(length)])  3.76 us
    pallas_call x2, Pallas kernels, per_device(): partial = forward_odd(widths, early, late, got, total)  2.71 us
  transfers between devices with their start and end apart: 14, of which 11 were waited for; matrix products, arithmetic and copies ran while one was open for 0% of the time, Pallas kernels for 12%

profile of v3, /device:TPU:386, one launch (start us, length us, event | category | flops | bytes accessed | tf_op | source)
XLA Modules:
  0.0 110.1 jit_solution(4291188715828242082)
XLA Ops:
  0.0 2.0 %shard_map.55 = (f32[256,256]{1,0:T(8,128)S(1)}, bf16[256,256]{1,0:T(8,128)(2,1)S(1)}, bf16[4,256,256]{2,1,0:T(8,128)(2,1)}) custom-call(f32[256,256]{1,0:T(8,128)} %warm_ref.1), custom_call_target="tpu_custom_call" | custom-call | flops 65536 | bytes 524288 | tf_op jit(solution)/shard_map/pallas_call | solution.py:302
  2.0 4.8 %all-to-all-start = ((bf16[4,256,256]{2,1,0:T(8,128)(2,1)}), bf16[4,256,256]{2,1,0:T(8,128)(2,1)S(1)}, u32[]{:S(2)}, u32[]{:S(2)}) async-start(bf16[4,256,256]{2,1,0:T(8,128)(2,1)} %get-tuple-element.25), calls=%async_computation | async-start | bytes 1048576 | tf_op jit(solution)/shard_map/all_to_all | solution.py:305
  6.8 6.7 %collective-permute-start = (bf16[256,256]{1,0:T(8,128)(2,1)S(1)}, bf16[256,256]{1,0:T(8,128)(2,1)S(1)}, u32[]{:S(2)}, u32[]{:S(2)}) collective-permute-start(bf16[256,256]{1,0:T(8,128)(2,1)S(1)} %get-tuple-element.24.cur_ref), channel_id=1, source_target_pairs={{16,0},{20,4},{24,8},{28,12},{32,16},{36,20},{40,24},{44,28},{48,3... | collective-permute-start | bytes 393224 | tf_op jit(solution)/shard_map/ppermute | solution.py:28
  13.6 2.5 %collective-permute-done.far_ref = bf16[256,256]{1,0:T(8,128)(2,1)S(1)} collective-permute-done((bf16[256,256]{1,0:T(8,128)(2,1)S(1)}, bf16[256,256]{1,0:T(8,128)(2,1)S(1)}, u32[]{:S(2)}, u32[]{:S(2)}) %collective-permute-start) | collective-permute-done | bytes 131104 | tf_op jit(solution)/shard_map/ppermute | solution.py:28
  16.1 7.8 %collective-permute-start.1 = (bf16[2,256,256]{2,1,0:T(8,128)(2,1)S(1)}, bf16[2,256,256]{2,1,0:T(8,128)(2,1)S(1)}, u32[]{:S(2)}, u32[]{:S(2)}) collective-permute-start(bf16[2,256,256]{2,1,0:T(8,128)(2,1)S(1)} %shard_map.58), channel_id=1, source_target_pairs={{8,0},{12,4},{16,8},{20,12},{24,16},{28,20},{32,24},{36,28},{40,32... | collective-permute-start | bytes 786440 | tf_op jit(solution)/shard_map/ppermute | solution.py:28
  24.5 1.2 %shard_map.56.early_ref = bf16[2,1024,256]{2,1,0:T(8,128)(2,1)S(1)} custom-call(bf16[7,1024,256]{2,1,0:T(8,128)(2,1)} %bitcast.6, bf16[256,256]{1,0:T(8,128)(2,1)S(1)} %collective-permute-done.far_ref), custom_call_target="tpu_custom_call" | custom-call | flops 65536 | bytes 1048576 | tf_op jit(solution)/shard_map/pallas_call | solution.py:307
  25.8 0.0 all-to-all-done.block_ref
  25.8 3.2 %shard_map.57 = (f32[256,256]{1,0:T(8,128)S(1)}, bf16[3,256,256]{2,1,0:T(8,128)(2,1)S(1)}, bf16[6,256,256]{2,1,0:T(8,128)(2,1)S(1)}, bf16[5,1024,256]{2,1,0:T(8,128)(2,1)S(1)}) custom-call(s32[1]{0:T(128)S(6)} %copy.10.widths_ref, bf16[7,1024,256]{2,1,0:T(8,128)(2,1)} %bitcast.7, bf16[2,1024,256]{2,1,0:T(8,128)(2,1)S(1)} %shard_map.56.early_ref, ...), custom_call_target="tpu_custom_call" | custom-call | flops 939524096 | bytes 3670016 | tf_op jit(solution)/shard_map/pallas_call | solution.py:308
  29.0 0.0 collective-permute-done.1.near_ref
  29.1 1.9 %collective-permute-start.2 = (bf16[6,256,256]{2,1,0:T(8,128)(2,1)S(1)}, bf16[6,256,256]{2,1,0:T(8,128)(2,1)S(1)}, u32[]{:S(2)}, u32[]{:S(2)}) collective-permute-start(bf16[6,256,256]{2,1,0:T(8,128)(2,1)S(1)} %shard_map.59), channel_id=1, source_target_pairs={{0,4},{4,0},{8,12},{12,8},{16,20},{20,16},{24,28},{28,24},{32,36},... | collective-permute-start | bytes 2359304 | tf_op jit(solution)/shard_map/ppermute | solution.py:33
  31.0 2.3 %collective-permute-done.2.got_ref = bf16[6,256,256]{2,1,0:T(8,128)(2,1)S(1)} collective-permute-done((bf16[6,256,256]{2,1,0:T(8,128)(2,1)S(1)}, bf16[6,256,256]{2,1,0:T(8,128)(2,1)S(1)}, u32[]{:S(2)}, u32[]{:S(2)}) %collective-permute-start.2) | collective-permute-done | bytes 786464 | tf_op jit(solution)/shard_map/ppermute | solution.py:33
  33.2 0.8 shard_map.60
  34.0 1.9 %collective-permute-start.3 = (bf16[2,256,256]{2,1,0:T(8,128)(2,1)}, bf16[2,256,256]{2,1,0:T(8,128)(2,1)S(1)}, u32[]{:S(2)}, u32[]{:S(2)}) collective-permute-start(bf16[2,256,256]{2,1,0:T(8,128)(2,1)} %get-tuple-element.29), channel_id=1, source_target_pairs={{0,8},{4,12},{8,16},{12,20},{16,24},{20,28},{24,32},{28,36},{32,40... | collective-permute-start | bytes 786440 | tf_op jit(solution)/shard_map/ppermute | solution.py:28
  36.0 0.7 shard_map.62.total_ref
  36.7 0.0 copy-start.1
  36.7 0.0 copy-start
  36.7 1.4 %shard_map.63 = bf16[4,256,256]{2,1,0:T(8,128)(2,1)} custom-call(s32[1]{0:T(128)S(6)} %copy.10.widths_ref, bf16[2,1024,256]{2,1,0:T(8,128)(2,1)S(1)} %shard_map.56.early_ref, bf16[5,1024,256]{2,1,0:T(8,128)(2,1)S(1)} %get-tuple-element.30.late_ref, bf16[6,256,256]{2,1,0:T(8,128)(2,1)S(1)} %collective-permute-done.2.got_ref, ...), custom_call_target="tpu_custom_call" | custom-call | flops 402653184 | bytes 3670016 | tf_op jit(solution)/shard_map/pallas_call | solution.py:313
  38.1 4.8 %all-to-all-start.1 = ((bf16[4,256,256]{2,1,0:T(8,128)(2,1)}), bf16[4,256,256]{2,1,0:T(8,128)(2,1)S(1)}, u32[]{:S(2)}, u32[]{:S(2)}) async-start(bf16[4,256,256]{2,1,0:T(8,128)(2,1)} %shard_map.63), calls=%async_computation.1 | async-start | bytes 1048576 | tf_op jit(solution)/shard_map/all_to_all | solution.py:314
  42.9 4.9 %collective-permute-done.3.near_ref = bf16[2,256,256]{2,1,0:T(8,128)(2,1)S(1)} collective-permute-done((bf16[2,256,256]{2,1,0:T(8,128)(2,1)}, bf16[2,256,256]{2,1,0:T(8,128)(2,1)S(1)}, u32[]{:S(2)}, u32[]{:S(2)}) %collective-permute-start.3) | collective-permute-done | bytes 262176 | tf_op jit(solution)/shard_map/ppermute | solution.py:28
  47.8 1.9 %collective-permute-start.4 = (bf16[256,256]{1,0:T(8,128)(2,1)S(1)}, bf16[256,256]{1,0:T(8,128)(2,1)S(1)}, u32[]{:S(2)}, u32[]{:S(2)}) collective-permute-start(bf16[256,256]{1,0:T(8,128)(2,1)S(1)} %shard_map.64), channel_id=1, source_target_pairs={{0,16},{4,20},{8,24},{12,28},{16,32},{20,36},{24,40},{28,44},{32,4... | collective-permute-start | bytes 393224 | tf_op jit(solution)/shard_map/ppermute | solution.py:28
  49.7 0.0 copy-done.1
  49.8 0.0 copy-done
  49.8 0.1 shard_map.61.settled_ref
  49.9 1.3 %all-to-all-done.1.seg_ref = bf16[4,256,256]{2,1,0:T(8,128)(2,1)S(1)} async-done(((bf16[4,256,256]{2,1,0:T(8,128)(2,1)}), bf16[4,256,256]{2,1,0:T(8,128)(2,1)S(1)}, u32[]{:S(2)}, u32[]{:S(2)}) %all-to-all-start.1) | async-done | bytes 524320 | tf_op jit(solution)/shard_map/all_to_all | solution.py:314
  51.2 7.1 %collective-permute-done.4.far_ref = bf16[256,256]{1,0:T(8,128)(2,1)S(1)} collective-permute-done((bf16[256,256]{1,0:T(8,128)(2,1)S(1)}, bf16[256,256]{1,0:T(8,128)(2,1)S(1)}, u32[]{:S(2)}, u32[]{:S(2)}) %collective-permute-start.4) | collective-permute-done | bytes 131104 | tf_op jit(solution)/shard_map/ppermute | solution.py:28
  58.3 0.1 broadcast_in_dim.2.pen_ref
  58.4 1.0 shard_map.65
  59.4 4.8 %all-to-all-start.2 = ((bf16[4,256,256]{2,1,0:T(8,128)(2,1)}), bf16[4,256,256]{2,1,0:T(8,128)(2,1)S(1)}, u32[]{:S(2)}, u32[]{:S(2)}) async-start(bf16[4,256,256]{2,1,0:T(8,128)(2,1)} %get-tuple-element.34), calls=%async_computation.2 | async-start | bytes 1048576 | tf_op jit(solution)/shard_map/all_to_all | solution.py:305
  64.2 1.9 %collective-permute-start.5 = (bf16[256,256]{1,0:T(8,128)(2,1)S(1)}, bf16[256,256]{1,0:T(8,128)(2,1)S(1)}, u32[]{:S(2)}, u32[]{:S(2)}) collective-permute-start(bf16[256,256]{1,0:T(8,128)(2,1)S(1)} %get-tuple-element.33.cur_ref), channel_id=1, source_target_pairs={{16,0},{20,4},{24,8},{28,12},{32,16},{36,20},{40,24},{44,28},{48,3... | collective-permute-start | bytes 393224 | tf_op jit(solution)/shard_map/ppermute | solution.py:28
  66.1 6.4 %collective-permute-done.5.far_ref = bf16[256,256]{1,0:T(8,128)(2,1)S(1)} collective-permute-done((bf16[256,256]{1,0:T(8,128)(2,1)S(1)}, bf16[256,256]{1,0:T(8,128)(2,1)S(1)}, u32[]{:S(2)}, u32[]{:S(2)}) %collective-permute-start.5) | collective-permute-done | bytes 131104 | tf_op jit(solution)/shard_map/ppermute | solution.py:28
  72.6 3.2 %collective-permute-start.6 = (bf16[2,256,256]{2,1,0:T(8,128)(2,1)S(1)}, bf16[2,256,256]{2,1,0:T(8,128)(2,1)S(1)}, u32[]{:S(2)}, u32[]{:S(2)}) collective-permute-start(bf16[2,256,256]{2,1,0:T(8,128)(2,1)S(1)} %shard_map.68), channel_id=1, source_target_pairs={{8,0},{12,4},{16,8},{20,12},{24,16},{28,20},{32,24},{36,28},{40,32... | collective-permute-start | bytes 786440 | tf_op jit(solution)/shard_map/ppermute | solution.py:28
  75.8 1.2 %shard_map.66.early_ref = bf16[2,1024,256]{2,1,0:T(8,128)(2,1)S(1)} custom-call(bf16[7,1024,256]{2,1,0:T(8,128)(2,1)} %bitcast.8, bf16[256,256]{1,0:T(8,128)(2,1)S(1)} %collective-permute-done.5.far_ref), custom_call_target="tpu_custom_call" | custom-call | flops 65536 | bytes 1048576 | tf_op jit(solution)/shard_map/pallas_call | solution.py:307
  77.0 0.0 all-to-all-done.2.block_ref
  77.0 3.2 %shard_map.67 = (f32[256,256]{1,0:T(8,128)S(1)}, bf16[3,256,256]{2,1,0:T(8,128)(2,1)S(1)}, bf16[6,256,256]{2,1,0:T(8,128)(2,1)S(1)}, bf16[5,1024,256]{2,1,0:T(8,128)(2,1)S(1)}) custom-call(s32[1]{0:T(128)S(6)} %copy.10.widths_ref, bf16[7,1024,256]{2,1,0:T(8,128)(2,1)} %bitcast.9, bf16[2,1024,256]{2,1,0:T(8,128)(2,1)S(1)} %shard_map.66.early_ref, ...), custom_call_target="tpu_custom_call" | custom-call | flops 939524096 | bytes 3670016 | tf_op jit(solution)/shard_map/pallas_call | solution.py:308
  80.2 0.6 collective-permute-done.6.near_ref
  80.9 1.9 %collective-permute-start.7 = (bf16[6,256,256]{2,1,0:T(8,128)(2,1)S(1)}, bf16[6,256,256]{2,1,0:T(8,128)(2,1)S(1)}, u32[]{:S(2)}, u32[]{:S(2)}) collective-permute-start(bf16[6,256,256]{2,1,0:T(8,128)(2,1)S(1)} %shard_map.69), channel_id=1, source_target_pairs={{0,4},{4,0},{8,12},{12,8},{16,20},{20,16},{24,28},{28,24},{32,36},... | collective-permute-start | bytes 2359304 | tf_op jit(solution)/shard_map/ppermute | solution.py:33
  82.8 0.7 shard_map.72.total_ref
  83.5 1.5 %collective-permute-done.7.got_ref = bf16[6,256,256]{2,1,0:T(8,128)(2,1)S(1)} collective-permute-done((bf16[6,256,256]{2,1,0:T(8,128)(2,1)S(1)}, bf16[6,256,256]{2,1,0:T(8,128)(2,1)S(1)}, u32[]{:S(2)}, u32[]{:S(2)}) %collective-permute-start.7) | collective-permute-done | bytes 786464 | tf_op jit(solution)/shard_map/ppermute | solution.py:33
  85.0 0.1 shard_map.70
  85.1 2.1 %collective-permute-start.8 = (bf16[2,256,256]{2,1,0:T(8,128)(2,1)S(1)}, bf16[2,256,256]{2,1,0:T(8,128)(2,1)S(1)}, u32[]{:S(2)}, u32[]{:S(2)}) collective-permute-start(bf16[2,256,256]{2,1,0:T(8,128)(2,1)S(1)} %get-tuple-element.38), channel_id=1, source_target_pairs={{0,8},{4,12},{8,16},{12,20},{16,24},{20,28},{24,32},{28,36},{32,40... | collective-permute-start | bytes 786440 | tf_op jit(solution)/shard_map/ppermute | solution.py:28
  87.2 1.4 %shard_map.73 = bf16[4,256,256]{2,1,0:T(8,128)(2,1)} custom-call(s32[1]{0:T(128)S(6)} %copy.10.widths_ref, bf16[2,1024,256]{2,1,0:T(8,128)(2,1)S(1)} %shard_map.66.early_ref, bf16[5,1024,256]{2,1,0:T(8,128)(2,1)S(1)} %get-tuple-element.39.late_ref, bf16[6,256,256]{2,1,0:T(8,128)(2,1)S(1)} %collective-permute-done.7.got_ref, ...), custom_call_target="tpu_custom_call" | custom-call | flops 402653184 | bytes 3670016 | tf_op jit(solution)/shard_map/pallas_call | solution.py:313
  88.6 4.8 %all-to-all-start.3 = ((bf16[4,256,256]{2,1,0:T(8,128)(2,1)}), bf16[4,256,256]{2,1,0:T(8,128)(2,1)S(1)}, u32[]{:S(2)}, u32[]{:S(2)}) async-start(bf16[4,256,256]{2,1,0:T(8,128)(2,1)} %shard_map.73), calls=%async_computation.3 | async-start | bytes 1048576 | tf_op jit(solution)/shard_map/all_to_all | solution.py:314
  93.4 5.3 %collective-permute-done.8.near_ref = bf16[2,256,256]{2,1,0:T(8,128)(2,1)S(1)} collective-permute-done((bf16[2,256,256]{2,1,0:T(8,128)(2,1)S(1)}, bf16[2,256,256]{2,1,0:T(8,128)(2,1)S(1)}, u32[]{:S(2)}, u32[]{:S(2)}) %collective-permute-start.8) | collective-permute-done | bytes 262176 | tf_op jit(solution)/shard_map/ppermute | solution.py:28
  98.7 1.9 %collective-permute-start.9 = (bf16[256,256]{1,0:T(8,128)(2,1)S(1)}, bf16[256,256]{1,0:T(8,128)(2,1)S(1)}, u32[]{:S(2)}, u32[]{:S(2)}) collective-permute-start(bf16[256,256]{1,0:T(8,128)(2,1)S(1)} %shard_map.74), channel_id=1, source_target_pairs={{0,16},{4,20},{8,24},{12,28},{16,32},{20,36},{24,40},{28,44},{32,4... | collective-permute-start | bytes 393224 | tf_op jit(solution)/shard_map/ppermute | solution.py:28
  100.6 0.1 shard_map.71.settled_ref
  100.7 0.8 all-to-all-done.3.seg_ref
  101.5 7.6 %collective-permute-done.9.far_ref = bf16[256,256]{1,0:T(8,128)(2,1)S(1)} collective-permute-done((bf16[256,256]{1,0:T(8,128)(2,1)S(1)}, bf16[256,256]{1,0:T(8,128)(2,1)S(1)}, u32[]{:S(2)}, u32[]{:S(2)}) %collective-permute-start.9) | collective-permute-done | bytes 131104 | tf_op jit(solution)/shard_map/ppermute | solution.py:28
  109.2 0.9 shard_map.75
  (7 shorter events, 0.2 us)
Async XLA Ops:
  2.0 23.8 %all-to-all-start = ((bf16[4,256,256]{2,1,0:T(8,128)(2,1)}), bf16[4,256,256]{2,1,0:T(8,128)(2,1)S(1)}, u32[]{:S(2)}, u32[]{:S(2)}) async-start(bf16[4,256,256]{2,1,0:T(8,128)(2,1)} %get-tuple-element.25), calls=%async_computation | async-start | bytes 1048576 | tf_op jit(solution)/shard_map/all_to_all | solution.py:305
  6.8 9.3 %collective-permute-start = (bf16[256,256]{1,0:T(8,128)(2,1)S(1)}, bf16[256,256]{1,0:T(8,128)(2,1)S(1)}, u32[]{:S(2)}, u32[]{:S(2)}) collective-permute-start(bf16[256,256]{1,0:T(8,128)(2,1)S(1)} %get-tuple-element.24.cur_ref), channel_id=1, source_target_pairs={{16,0},{20,4},{24,8},{28,12},{32,16},{36,20},{40,24},{44,28},{48,3... | collective-permute-start | bytes 393224 | tf_op jit(solution)/shard_map/ppermute | solution.py:28
  16.1 12.9 %collective-permute-start.1 = (bf16[2,256,256]{2,1,0:T(8,128)(2,1)S(1)}, bf16[2,256,256]{2,1,0:T(8,128)(2,1)S(1)}, u32[]{:S(2)}, u32[]{:S(2)}) collective-permute-start(bf16[2,256,256]{2,1,0:T(8,128)(2,1)S(1)} %shard_map.58), channel_id=1, source_target_pairs={{8,0},{12,4},{16,8},{20,12},{24,16},{28,20},{32,24},{36,28},{40,32... | collective-permute-start | bytes 786440 | tf_op jit(solution)/shard_map/ppermute | solution.py:28
  29.1 4.2 %collective-permute-start.2 = (bf16[6,256,256]{2,1,0:T(8,128)(2,1)S(1)}, bf16[6,256,256]{2,1,0:T(8,128)(2,1)S(1)}, u32[]{:S(2)}, u32[]{:S(2)}) collective-permute-start(bf16[6,256,256]{2,1,0:T(8,128)(2,1)S(1)} %shard_map.59), channel_id=1, source_target_pairs={{0,4},{4,0},{8,12},{12,8},{16,20},{20,16},{24,28},{28,24},{32,36},... | collective-permute-start | bytes 2359304 | tf_op jit(solution)/shard_map/ppermute | solution.py:33
  34.0 13.7 %collective-permute-start.3 = (bf16[2,256,256]{2,1,0:T(8,128)(2,1)}, bf16[2,256,256]{2,1,0:T(8,128)(2,1)S(1)}, u32[]{:S(2)}, u32[]{:S(2)}) collective-permute-start(bf16[2,256,256]{2,1,0:T(8,128)(2,1)} %get-tuple-element.29), channel_id=1, source_target_pairs={{0,8},{4,12},{8,16},{12,20},{16,24},{20,28},{24,32},{28,36},{32,40... | collective-permute-start | bytes 786440 | tf_op jit(solution)/shard_map/ppermute | solution.py:28
  36.7 13.0 %copy-start.1 = (f32[256]{0:T(256)S(1)}, f32[256]{0:T(256)}, u32[]{:S(2)}) copy-start(f32[256]{0:T(256)} %param.9) | copy-start | bytes 3076
  36.7 13.0 %copy-start = (f32[256,64]{0,1:T(8,128)S(1)}, f32[256,64]{0,1:T(8,128)}, u32[]{:S(2)}) copy-start(f32[256,64]{0,1:T(8,128)} %param.8) | copy-start | bytes 196612
  38.1 13.1 %all-to-all-start.1 = ((bf16[4,256,256]{2,1,0:T(8,128)(2,1)}), bf16[4,256,256]{2,1,0:T(8,128)(2,1)S(1)}, u32[]{:S(2)}, u32[]{:S(2)}) async-start(bf16[4,256,256]{2,1,0:T(8,128)(2,1)} %shard_map.63), calls=%async_computation.1 | async-start | bytes 1048576 | tf_op jit(solution)/shard_map/all_to_all | solution.py:314
  47.8 10.5 %collective-permute-start.4 = (bf16[256,256]{1,0:T(8,128)(2,1)S(1)}, bf16[256,256]{1,0:T(8,128)(2,1)S(1)}, u32[]{:S(2)}, u32[]{:S(2)}) collective-permute-start(bf16[256,256]{1,0:T(8,128)(2,1)S(1)} %shard_map.64), channel_id=1, source_target_pairs={{0,16},{4,20},{8,24},{12,28},{16,32},{20,36},{24,40},{28,44},{32,4... | collective-permute-start | bytes 393224 | tf_op jit(solution)/shard_map/ppermute | solution.py:28
  59.4 17.6 %all-to-all-start.2 = ((bf16[4,256,256]{2,1,0:T(8,128)(2,1)}), bf16[4,256,256]{2,1,0:T(8,128)(2,1)S(1)}, u32[]{:S(2)}, u32[]{:S(2)}) async-start(bf16[4,256,256]{2,1,0:T(8,128)(2,1)} %get-tuple-element.34), calls=%async_computation.2 | async-start | bytes 1048576 | tf_op jit(solution)/shard_map/all_to_all | solution.py:305
  64.2 8.4 %collective-permute-start.5 = (bf16[256,256]{1,0:T(8,128)(2,1)S(1)}, bf16[256,256]{1,0:T(8,128)(2,1)S(1)}, u32[]{:S(2)}, u32[]{:S(2)}) collective-permute-start(bf16[256,256]{1,0:T(8,128)(2,1)S(1)} %get-tuple-element.33.cur_ref), channel_id=1, source_target_pairs={{16,0},{20,4},{24,8},{28,12},{32,16},{36,20},{40,24},{44,28},{48,3... | collective-permute-start | bytes 393224 | tf_op jit(solution)/shard_map/ppermute | solution.py:28
  72.6 8.3 %collective-permute-start.6 = (bf16[2,256,256]{2,1,0:T(8,128)(2,1)S(1)}, bf16[2,256,256]{2,1,0:T(8,128)(2,1)S(1)}, u32[]{:S(2)}, u32[]{:S(2)}) collective-permute-start(bf16[2,256,256]{2,1,0:T(8,128)(2,1)S(1)} %shard_map.68), channel_id=1, source_target_pairs={{8,0},{12,4},{16,8},{20,12},{24,16},{28,20},{32,24},{36,28},{40,32... | collective-permute-start | bytes 786440 | tf_op jit(solution)/shard_map/ppermute | solution.py:28
  80.9 4.2 %collective-permute-start.7 = (bf16[6,256,256]{2,1,0:T(8,128)(2,1)S(1)}, bf16[6,256,256]{2,1,0:T(8,128)(2,1)S(1)}, u32[]{:S(2)}, u32[]{:S(2)}) collective-permute-start(bf16[6,256,256]{2,1,0:T(8,128)(2,1)S(1)} %shard_map.69), channel_id=1, source_target_pairs={{0,4},{4,0},{8,12},{12,8},{16,20},{20,16},{24,28},{28,24},{32,36},... | collective-permute-start | bytes 2359304 | tf_op jit(solution)/shard_map/ppermute | solution.py:33
  85.1 13.5 %collective-permute-start.8 = (bf16[2,256,256]{2,1,0:T(8,128)(2,1)S(1)}, bf16[2,256,256]{2,1,0:T(8,128)(2,1)S(1)}, u32[]{:S(2)}, u32[]{:S(2)}) collective-permute-start(bf16[2,256,256]{2,1,0:T(8,128)(2,1)S(1)} %get-tuple-element.38), channel_id=1, source_target_pairs={{0,8},{4,12},{8,16},{12,20},{16,24},{20,28},{24,32},{28,36},{32,40... | collective-permute-start | bytes 786440 | tf_op jit(solution)/shard_map/ppermute | solution.py:28
  88.6 12.9 %all-to-all-start.3 = ((bf16[4,256,256]{2,1,0:T(8,128)(2,1)}), bf16[4,256,256]{2,1,0:T(8,128)(2,1)S(1)}, u32[]{:S(2)}, u32[]{:S(2)}) async-start(bf16[4,256,256]{2,1,0:T(8,128)(2,1)} %shard_map.73), calls=%async_computation.3 | async-start | bytes 1048576 | tf_op jit(solution)/shard_map/all_to_all | solution.py:314
  98.7 10.5 %collective-permute-start.9 = (bf16[256,256]{1,0:T(8,128)(2,1)S(1)}, bf16[256,256]{1,0:T(8,128)(2,1)S(1)}, u32[]{:S(2)}, u32[]{:S(2)}) collective-permute-start(bf16[256,256]{1,0:T(8,128)(2,1)S(1)} %shard_map.74), channel_id=1, source_target_pairs={{0,16},{4,20},{8,24},{12,28},{16,32},{20,36},{24,40},{28,44},{32,4... | collective-permute-start | bytes 393224 | tf_op jit(solution)/shard_map/ppermute | solution.py:28

commit v4 on v3

--- a/solution.py
+++ b/solution.py
@@ -51,7 +51,7 @@
     return copies
 
 
-def begin_kernel(warm_ref, est_ref, cur_ref, copies_ref, held, in_sems, out_sems):
+def begin_kernel(warm_ref, est_ref, cur_ref, held, in_sems):
     parts, rows, _ = held.shape
     loads = [
         pltpu.make_async_copy(warm_ref.at[pl.ds(i * rows, rows), :], held.at[i], in_sems.at[i])
@@ -64,7 +64,10 @@
         est = held[i].T
         est_ref[:, i * rows : (i + 1) * rows] = est
         cur_ref[:, i * rows : (i + 1) * rows] = est.astype(BF16)
-    for copy in send_copies(cur_ref, copies_ref, out_sems):
+
+
+def spread_kernel(cur_ref, copies_ref, sems):
+    for copy in send_copies(cur_ref, copies_ref, sems):
         copy.wait()
 
 
@@ -159,14 +162,14 @@
 
     @pl.when(is_odd())
     def _():
-        pair_ref[0] = add(0, got_ref[4])
-        mid_ref[...] = add(1, got_ref[5])
+        mid_ref[...] = add(0, got_ref[4])
+        pair_ref[0] = add(1, got_ref[5])
         pair_ref[1] = even_ref[2]
 
     @pl.when(jnp.logical_not(is_odd()))
     def _():
-        pair_ref[0] = add(0, got_ref[3])
-        mid_ref[...] = add(1, got_ref[4])
+        mid_ref[...] = add(0, got_ref[3])
+        pair_ref[0] = add(1, got_ref[4])
         pair_ref[1] = add(2, got_ref[5])
 
 
@@ -190,13 +193,10 @@
     return soft_limit(settled_ref[...] - step_size * coupled, pen_ref[...])
 
 
-def update_kernel(settled_ref, seg_ref, far_ref, pen_ref, new_ref, cur_ref, copies_ref, sems):
+def update_kernel(settled_ref, seg_ref, far_ref, pen_ref, new_ref, cur_ref):
     est = new_estimate(settled_ref, seg_ref, far_ref, pen_ref)
     cur_ref[...] = est.astype(BF16)
-    copies = send_copies(cur_ref, copies_ref, sems)
     new_ref[...] = est
-    for copy in copies:
-        copy.wait()
 
 
 def final_kernel(settled_ref, seg_ref, far_ref, pen_ref, out_ref):
@@ -237,7 +237,7 @@
     tile_bytes = depth * block_len * strip * 2
     one = columns * strip
     seg_sems = pltpu.SemaphoreType.DMA((n_seg,))
-    fresh = (shape(F32), shape(BF16), HBM((n_seg, columns, strip), BF16))
+    fresh = (shape(F32), shape(BF16))
     begin = call(
         begin_kernel,
         fresh,
@@ -247,8 +247,18 @@
         8 * one,
         4,
         outside=(0,),
-        out_outside=(2,),
-        scratch_shapes=[VMEM((2, strip // 2, columns), F32), pltpu.SemaphoreType.DMA((2,)), seg_sems],
+        scratch_shapes=[VMEM((2, strip // 2, columns), F32), pltpu.SemaphoreType.DMA((2,))],
+    )
+    spread = call(
+        spread_kernel,
+        HBM((n_seg, columns, strip), BF16),
+        1,
+        0,
+        one,
+        10 * one,
+        2,
+        out_outside=(0,),
+        scratch_shapes=[seg_sems],
     )
     pair = call(pair_kernel, shape(BF16, 2), 2, 0, one, 8 * one, 2)
     load = call(
@@ -294,14 +304,13 @@
     combine = call(combine_kernel, (shape(BF16, 2), shape(BF16)), 2, 0, one, 18 * one, 4)
     relay = call(relay_kernel, shape(BF16), 2, 0, one, 6 * one, 2)
     settle = call(settle_kernel, shape(F32), 5, 0, one, 14 * one, 4)
-    update = call(
-        update_kernel, fresh, 4, 0, one, 12 * one, 6, out_outside=(2,), scratch_shapes=[seg_sems]
-    )
+    update = call(update_kernel, fresh, 4, 0, one, 12 * one, 6)
     final = call(final_kernel, jax.ShapeDtypeStruct((strip, columns), F32), 4, 0, one, 12 * one, 6)
 
-    estimate, current, copies = begin(pltpu.with_memory_space_constraint(warm_start, HBM))
+    estimate, current = begin(pltpu.with_memory_space_constraint(warm_start, HBM))
     for iteration in range(ITERS):
         far = shifted(current, -4)
+        copies = spread(current)
         block = lax.all_to_all(copies, "seg", 0, 0)
         near = shifted(pair(current, far), -2)
         early = load(tiles, far)
@@ -309,15 +318,15 @@
         got = swapped(lend(lent, current, near, far))
         total = forward_even(widths, early, late, current, near, far)
         back_pair, mid = combine(even, got)
-        back_near = shifted(back_pair, 2)
+        back_first = shifted(back_pair, 4)
         partial = forward_odd(widths, early, late, got, total)
         summed = lax.all_to_all(partial, "seg", 0, 0)
-        back_far = shifted(relay(mid, back_near), 4)
-        settled = settle(estimate, first, got, back_near, scores_t)
+        back_last = shifted(relay(mid, back_first), 2)
+        settled = settle(estimate, first, got, back_first, scores_t)
         if iteration < ITERS - 1:
-            estimate, current, copies = update(settled, summed, back_far, pen)
+            estimate, current = update(settled, summed, back_last, pen)
         else:
-            return final(settled, summed, back_far, pen)
+            return final(settled, summed, back_last, pen)
 
 
 def solution(mesh):

time: 111 us -> 111 us (level)
    pallas_call x6 -> x8, Pallas kernels: 2.15 us -> 2.99 us  [the longest x2 1.68 us: per_device(): copies = spread(current)]
  transfers between devices with their start and end apart: 14 -> 14, of which waited for: 11 -> 10; matrix products, arithmetic and copies ran while one was open for 0% -> 0% of each run, Pallas kernels for 12% -> 12%
where the time goes in v4:
time: 111 us; the launch traced here: 110 us
  starting transfers between devices  51.5 us (46%)
  waiting for transfers between devices  39.3 us (35%)
  Pallas kernels  18.2 us (16%)
    ppermute x8, waiting for transfers between devices, shifted(): return lax.ppermute(value, 'chain', pairs)  34.6 us
    ppermute x8, starting transfers between devices, shifted(): return lax.ppermute(value, 'chain', pairs)  28.4 us
    all_to_all x2, starting transfers between devices, per_device(): block = lax.all_to_all(copies, 'seg', 0, 0)  9.65 us
    all_to_all x2, starting transfers between devices, per_device(): summed = lax.all_to_all(partial, 'seg', 0, 0)  9.62 us
    pallas_call x2, Pallas kernels, per_device(): first, even, lent, late = backward(widths, tiles, early, block)  6.42 us
    ppermute x2, starting transfers between devices, swapped(): return lax.ppermute(value, 'chain', [(i, i ^ 1) for i in range(length)])  3.84 us
    ppermute x2, waiting for transfers between devices, swapped(): return lax.ppermute(value, 'chain', [(i, i ^ 1) for i in range(length)])  3.76 us
    pallas_call x2, Pallas kernels, per_device(): partial = forward_odd(widths, early, late, got, total)  2.71 us
  transfers between devices with their start and end apart: 14, of which 10 were waited for; matrix products, arithmetic and copies ran while one was open for 0% of the time, Pallas kernels for 12%

profile of v4, /device:TPU:386, one launch (start us, length us, event | category | flops | bytes accessed | tf_op | source)
XLA Modules:
  0.0 110.1 jit_solution(11019200903602765302)
XLA Ops:
  0.0 1.1 %shard_map.55 = (f32[256,256]{1,0:T(8,128)S(1)}, bf16[256,256]{1,0:T(8,128)(2,1)S(1)}) custom-call(f32[256,256]{1,0:T(8,128)} %warm_ref.1), custom_call_target="tpu_custom_call" | custom-call | flops 65536 | bytes 524288 | tf_op jit(solution)/shard_map/pallas_call | solution.py:310
  1.1 0.8 shard_map.57
  2.0 4.8 %all-to-all-start = ((bf16[4,256,256]{2,1,0:T(8,128)(2,1)}), bf16[4,256,256]{2,1,0:T(8,128)(2,1)S(1)}, u32[]{:S(2)}, u32[]{:S(2)}) async-start(bf16[4,256,256]{2,1,0:T(8,128)(2,1)} %shard_map.57), calls=%async_computation | async-start | bytes 1048576 | tf_op jit(solution)/shard_map/all_to_all | solution.py:314
  6.8 6.7 %collective-permute-start = (bf16[256,256]{1,0:T(8,128)(2,1)S(1)}, bf16[256,256]{1,0:T(8,128)(2,1)S(1)}, u32[]{:S(2)}, u32[]{:S(2)}) collective-permute-start(bf16[256,256]{1,0:T(8,128)(2,1)S(1)} %get-tuple-element.22.cur_ref), channel_id=1, source_target_pairs={{16,0},{20,4},{24,8},{28,12},{32,16},{36,20},{40,24},{44,28},{48,3... | collective-permute-start | bytes 393224 | tf_op jit(solution)/shard_map/ppermute | solution.py:28
  13.6 2.5 %collective-permute-done.far_ref = bf16[256,256]{1,0:T(8,128)(2,1)S(1)} collective-permute-done((bf16[256,256]{1,0:T(8,128)(2,1)S(1)}, bf16[256,256]{1,0:T(8,128)(2,1)S(1)}, u32[]{:S(2)}, u32[]{:S(2)}) %collective-permute-start) | collective-permute-done | bytes 131104 | tf_op jit(solution)/shard_map/ppermute | solution.py:28
  16.1 7.8 %collective-permute-start.1 = (bf16[2,256,256]{2,1,0:T(8,128)(2,1)S(1)}, bf16[2,256,256]{2,1,0:T(8,128)(2,1)S(1)}, u32[]{:S(2)}, u32[]{:S(2)}) collective-permute-start(bf16[2,256,256]{2,1,0:T(8,128)(2,1)S(1)} %shard_map.59), channel_id=1, source_target_pairs={{8,0},{12,4},{16,8},{20,12},{24,16},{28,20},{32,24},{36,28},{40,32... | collective-permute-start | bytes 786440 | tf_op jit(solution)/shard_map/ppermute | solution.py:28
  24.5 1.2 %shard_map.56.early_ref = bf16[2,1024,256]{2,1,0:T(8,128)(2,1)S(1)} custom-call(bf16[7,1024,256]{2,1,0:T(8,128)(2,1)} %bitcast.6, bf16[256,256]{1,0:T(8,128)(2,1)S(1)} %collective-permute-done.far_ref), custom_call_target="tpu_custom_call" | custom-call | flops 65536 | bytes 1048576 | tf_op jit(solution)/shard_map/pallas_call | solution.py:316
  25.8 0.0 all-to-all-done.block_ref
  25.8 3.2 %shard_map.58 = (f32[256,256]{1,0:T(8,128)S(1)}, bf16[3,256,256]{2,1,0:T(8,128)(2,1)S(1)}, bf16[6,256,256]{2,1,0:T(8,128)(2,1)S(1)}, bf16[5,1024,256]{2,1,0:T(8,128)(2,1)S(1)}) custom-call(s32[1]{0:T(128)S(6)} %copy.10.widths_ref, bf16[7,1024,256]{2,1,0:T(8,128)(2,1)} %bitcast.7, bf16[2,1024,256]{2,1,0:T(8,128)(2,1)S(1)} %shard_map.56.early_ref, ...), custom_call_target="tpu_custom_call" | custom-call | flops 939524096 | bytes 3670016 | tf_op jit(solution)/shard_map/pallas_call | solution.py:317
  29.0 0.0 collective-permute-done.1.near_ref
  29.1 1.9 %collective-permute-start.2 = (bf16[6,256,256]{2,1,0:T(8,128)(2,1)S(1)}, bf16[6,256,256]{2,1,0:T(8,128)(2,1)S(1)}, u32[]{:S(2)}, u32[]{:S(2)}) collective-permute-start(bf16[6,256,256]{2,1,0:T(8,128)(2,1)S(1)} %shard_map.60), channel_id=1, source_target_pairs={{0,4},{4,0},{8,12},{12,8},{16,20},{20,16},{24,28},{28,24},{32,36},... | collective-permute-start | bytes 2359304 | tf_op jit(solution)/shard_map/ppermute | solution.py:33
  31.0 2.3 %collective-permute-done.2.got_ref = bf16[6,256,256]{2,1,0:T(8,128)(2,1)S(1)} collective-permute-done((bf16[6,256,256]{2,1,0:T(8,128)(2,1)S(1)}, bf16[6,256,256]{2,1,0:T(8,128)(2,1)S(1)}, u32[]{:S(2)}, u32[]{:S(2)}) %collective-permute-start.2) | collective-permute-done | bytes 786464 | tf_op jit(solution)/shard_map/ppermute | solution.py:33
  33.3 0.8 shard_map.61
  34.0 1.9 %collective-permute-start.3 = (bf16[2,256,256]{2,1,0:T(8,128)(2,1)}, bf16[2,256,256]{2,1,0:T(8,128)(2,1)S(1)}, u32[]{:S(2)}, u32[]{:S(2)}) collective-permute-start(bf16[2,256,256]{2,1,0:T(8,128)(2,1)} %get-tuple-element.26), channel_id=1, source_target_pairs={{0,16},{4,20},{8,24},{12,28},{16,32},{20,36},{24,40},{28,44},{32,4... | collective-permute-start | bytes 786440 | tf_op jit(solution)/shard_map/ppermute | solution.py:28
  36.0 0.7 shard_map.63.total_ref
  36.7 0.0 copy-start.1
  36.7 0.0 copy-start
  36.7 1.4 %shard_map.64 = bf16[4,256,256]{2,1,0:T(8,128)(2,1)} custom-call(s32[1]{0:T(128)S(6)} %copy.10.widths_ref, bf16[2,1024,256]{2,1,0:T(8,128)(2,1)S(1)} %shard_map.56.early_ref, bf16[5,1024,256]{2,1,0:T(8,128)(2,1)S(1)} %get-tuple-element.27.late_ref, bf16[6,256,256]{2,1,0:T(8,128)(2,1)S(1)} %collective-permute-done.2.got_ref, ...), custom_call_target="tpu_custom_call" | custom-call | flops 402653184 | bytes 3670016 | tf_op jit(solution)/shard_map/pallas_call | solution.py:322
  38.1 4.8 %all-to-all-start.1 = ((bf16[4,256,256]{2,1,0:T(8,128)(2,1)}), bf16[4,256,256]{2,1,0:T(8,128)(2,1)S(1)}, u32[]{:S(2)}, u32[]{:S(2)}) async-start(bf16[4,256,256]{2,1,0:T(8,128)(2,1)} %shard_map.64), calls=%async_computation.1 | async-start | bytes 1048576 | tf_op jit(solution)/shard_map/all_to_all | solution.py:323
  42.9 5.2 %collective-permute-done.3.near_ref = bf16[2,256,256]{2,1,0:T(8,128)(2,1)S(1)} collective-permute-done((bf16[2,256,256]{2,1,0:T(8,128)(2,1)}, bf16[2,256,256]{2,1,0:T(8,128)(2,1)S(1)}, u32[]{:S(2)}, u32[]{:S(2)}) %collective-permute-start.3) | collective-permute-done | bytes 262176 | tf_op jit(solution)/shard_map/ppermute | solution.py:28
  48.1 1.9 %collective-permute-start.4 = (bf16[256,256]{1,0:T(8,128)(2,1)S(1)}, bf16[256,256]{1,0:T(8,128)(2,1)S(1)}, u32[]{:S(2)}, u32[]{:S(2)}) collective-permute-start(bf16[256,256]{1,0:T(8,128)(2,1)S(1)} %shard_map.65), channel_id=1, source_target_pairs={{0,8},{4,12},{8,16},{12,20},{16,24},{20,28},{24,32},{28,36},{32,40... | collective-permute-start | bytes 393224 | tf_op jit(solution)/shard_map/ppermute | solution.py:28
  50.0 0.0 copy-done.1
  50.1 0.0 copy-done
  50.1 0.1 shard_map.62.settled_ref
  50.2 1.0 all-to-all-done.1.seg_ref
  51.2 7.1 %collective-permute-done.4.far_ref = bf16[256,256]{1,0:T(8,128)(2,1)S(1)} collective-permute-done((bf16[256,256]{1,0:T(8,128)(2,1)S(1)}, bf16[256,256]{1,0:T(8,128)(2,1)S(1)}, u32[]{:S(2)}, u32[]{:S(2)}) %collective-permute-start.4) | collective-permute-done | bytes 131104 | tf_op jit(solution)/shard_map/ppermute | solution.py:28
  58.3 0.1 broadcast_in_dim.2.pen_ref
  58.4 0.1 shard_map.66
  58.5 0.8 shard_map.68
  59.4 4.8 %all-to-all-start.2 = ((bf16[4,256,256]{2,1,0:T(8,128)(2,1)}), bf16[4,256,256]{2,1,0:T(8,128)(2,1)S(1)}, u32[]{:S(2)}, u32[]{:S(2)}) async-start(bf16[4,256,256]{2,1,0:T(8,128)(2,1)} %shard_map.68), calls=%async_computation.2 | async-start | bytes 1048576 | tf_op jit(solution)/shard_map/all_to_all | solution.py:314
  64.2 1.9 %collective-permute-start.5 = (bf16[256,256]{1,0:T(8,128)(2,1)S(1)}, bf16[256,256]{1,0:T(8,128)(2,1)S(1)}, u32[]{:S(2)}, u32[]{:S(2)}) collective-permute-start(bf16[256,256]{1,0:T(8,128)(2,1)S(1)} %get-tuple-element.30.cur_ref), channel_id=1, source_target_pairs={{16,0},{20,4},{24,8},{28,12},{32,16},{36,20},{40,24},{44,28},{48,3... | collective-permute-start | bytes 393224 | tf_op jit(solution)/shard_map/ppermute | solution.py:28
  66.1 6.4 %collective-permute-done.5.far_ref = bf16[256,256]{1,0:T(8,128)(2,1)S(1)} collective-permute-done((bf16[256,256]{1,0:T(8,128)(2,1)S(1)}, bf16[256,256]{1,0:T(8,128)(2,1)S(1)}, u32[]{:S(2)}, u32[]{:S(2)}) %collective-permute-start.5) | collective-permute-done | bytes 131104 | tf_op jit(solution)/shard_map/ppermute | solution.py:28
  72.6 3.7 %collective-permute-start.6 = (bf16[2,256,256]{2,1,0:T(8,128)(2,1)S(1)}, bf16[2,256,256]{2,1,0:T(8,128)(2,1)S(1)}, u32[]{:S(2)}, u32[]{:S(2)}) collective-permute-start(bf16[2,256,256]{2,1,0:T(8,128)(2,1)S(1)} %shard_map.70), channel_id=1, source_target_pairs={{8,0},{12,4},{16,8},{20,12},{24,16},{28,20},{32,24},{36,28},{40,32... | collective-permute-start | bytes 786440 | tf_op jit(solution)/shard_map/ppermute | solution.py:28
  76.3 1.2 %shard_map.67.early_ref = bf16[2,1024,256]{2,1,0:T(8,128)(2,1)S(1)} custom-call(bf16[7,1024,256]{2,1,0:T(8,128)(2,1)} %bitcast.8, bf16[256,256]{1,0:T(8,128)(2,1)S(1)} %collective-permute-done.5.far_ref), custom_call_target="tpu_custom_call" | custom-call | flops 65536 | bytes 1048576 | tf_op jit(solution)/shard_map/pallas_call | solution.py:316
  77.5 0.0 all-to-all-done.2.block_ref
  77.5 3.2 %shard_map.69 = (f32[256,256]{1,0:T(8,128)S(1)}, bf16[3,256,256]{2,1,0:T(8,128)(2,1)S(1)}, bf16[6,256,256]{2,1,0:T(8,128)(2,1)S(1)}, bf16[5,1024,256]{2,1,0:T(8,128)(2,1)S(1)}) custom-call(s32[1]{0:T(128)S(6)} %copy.10.widths_ref, bf16[7,1024,256]{2,1,0:T(8,128)(2,1)} %bitcast.9, bf16[2,1024,256]{2,1,0:T(8,128)(2,1)S(1)} %shard_map.67.early_ref, ...), custom_call_target="tpu_custom_call" | custom-call | flops 939524096 | bytes 3670016 | tf_op jit(solution)/shard_map/pallas_call | solution.py:317
  80.8 0.1 collective-permute-done.6.near_ref
  80.9 1.9 %collective-permute-start.7 = (bf16[6,256,256]{2,1,0:T(8,128)(2,1)S(1)}, bf16[6,256,256]{2,1,0:T(8,128)(2,1)S(1)}, u32[]{:S(2)}, u32[]{:S(2)}) collective-permute-start(bf16[6,256,256]{2,1,0:T(8,128)(2,1)S(1)} %shard_map.71), channel_id=1, source_target_pairs={{0,4},{4,0},{8,12},{12,8},{16,20},{20,16},{24,28},{28,24},{32,36},... | collective-permute-start | bytes 2359304 | tf_op jit(solution)/shard_map/ppermute | solution.py:33
  82.8 0.7 shard_map.74.total_ref
  83.5 1.5 %collective-permute-done.7.got_ref = bf16[6,256,256]{2,1,0:T(8,128)(2,1)S(1)} collective-permute-done((bf16[6,256,256]{2,1,0:T(8,128)(2,1)S(1)}, bf16[6,256,256]{2,1,0:T(8,128)(2,1)S(1)}, u32[]{:S(2)}, u32[]{:S(2)}) %collective-permute-start.7) | collective-permute-done | bytes 786464 | tf_op jit(solution)/shard_map/ppermute | solution.py:33
  85.1 0.1 shard_map.72
  85.2 1.9 %collective-permute-start.8 = (bf16[2,256,256]{2,1,0:T(8,128)(2,1)S(1)}, bf16[2,256,256]{2,1,0:T(8,128)(2,1)S(1)}, u32[]{:S(2)}, u32[]{:S(2)}) collective-permute-start(bf16[2,256,256]{2,1,0:T(8,128)(2,1)S(1)} %get-tuple-element.34), channel_id=1, source_target_pairs={{0,16},{4,20},{8,24},{12,28},{16,32},{20,36},{24,40},{28,44},{32,4... | collective-permute-start | bytes 786440 | tf_op jit(solution)/shard_map/ppermute | solution.py:28
  87.1 1.4 %shard_map.75 = bf16[4,256,256]{2,1,0:T(8,128)(2,1)} custom-call(s32[1]{0:T(128)S(6)} %copy.10.widths_ref, bf16[2,1024,256]{2,1,0:T(8,128)(2,1)S(1)} %shard_map.67.early_ref, bf16[5,1024,256]{2,1,0:T(8,128)(2,1)S(1)} %get-tuple-element.35.late_ref, bf16[6,256,256]{2,1,0:T(8,128)(2,1)S(1)} %collective-permute-done.7.got_ref, ...), custom_call_target="tpu_custom_call" | custom-call | flops 402653184 | bytes 3670016 | tf_op jit(solution)/shard_map/pallas_call | solution.py:322
  88.4 4.8 %all-to-all-start.3 = ((bf16[4,256,256]{2,1,0:T(8,128)(2,1)}), bf16[4,256,256]{2,1,0:T(8,128)(2,1)S(1)}, u32[]{:S(2)}, u32[]{:S(2)}) async-start(bf16[4,256,256]{2,1,0:T(8,128)(2,1)} %shard_map.75), calls=%async_computation.3 | async-start | bytes 1048576 | tf_op jit(solution)/shard_map/all_to_all | solution.py:323
  93.3 5.7 %collective-permute-done.8.near_ref = bf16[2,256,256]{2,1,0:T(8,128)(2,1)S(1)} collective-permute-done((bf16[2,256,256]{2,1,0:T(8,128)(2,1)S(1)}, bf16[2,256,256]{2,1,0:T(8,128)(2,1)S(1)}, u32[]{:S(2)}, u32[]{:S(2)}) %collective-permute-start.8) | collective-permute-done | bytes 262176 | tf_op jit(solution)/shard_map/ppermute | solution.py:28
  99.0 2.5 %collective-permute-start.9 = (bf16[256,256]{1,0:T(8,128)(2,1)S(1)}, bf16[256,256]{1,0:T(8,128)(2,1)S(1)}, u32[]{:S(2)}, u32[]{:S(2)}) collective-permute-start(bf16[256,256]{1,0:T(8,128)(2,1)S(1)} %shard_map.76), channel_id=1, source_target_pairs={{0,8},{4,12},{8,16},{12,20},{16,24},{20,28},{24,32},{28,36},{32,40... | collective-permute-start | bytes 393224 | tf_op jit(solution)/shard_map/ppermute | solution.py:28
  101.5 0.1 shard_map.73.settled_ref
  101.6 0.0 all-to-all-done.3.seg_ref
  101.7 7.5 %collective-permute-done.9.far_ref = bf16[256,256]{1,0:T(8,128)(2,1)S(1)} collective-permute-done((bf16[256,256]{1,0:T(8,128)(2,1)S(1)}, bf16[256,256]{1,0:T(8,128)(2,1)S(1)}, u32[]{:S(2)}, u32[]{:S(2)}) %collective-permute-start.9) | collective-permute-done | bytes 131104 | tf_op jit(solution)/shard_map/ppermute | solution.py:28
  109.2 0.9 shard_map.77
  (7 shorter events, 0.2 us)
Async XLA Ops:
  2.0 23.8 %all-to-all-start = ((bf16[4,256,256]{2,1,0:T(8,128)(2,1)}), bf16[4,256,256]{2,1,0:T(8,128)(2,1)S(1)}, u32[]{:S(2)}, u32[]{:S(2)}) async-start(bf16[4,256,256]{2,1,0:T(8,128)(2,1)} %shard_map.57), calls=%async_computation | async-start | bytes 1048576 | tf_op jit(solution)/shard_map/all_to_all | solution.py:314
  6.8 9.3 %collective-permute-start = (bf16[256,256]{1,0:T(8,128)(2,1)S(1)}, bf16[256,256]{1,0:T(8,128)(2,1)S(1)}, u32[]{:S(2)}, u32[]{:S(2)}) collective-permute-start(bf16[256,256]{1,0:T(8,128)(2,1)S(1)} %get-tuple-element.22.cur_ref), channel_id=1, source_target_pairs={{16,0},{20,4},{24,8},{28,12},{32,16},{36,20},{40,24},{44,28},{48,3... | collective-permute-start | bytes 393224 | tf_op jit(solution)/shard_map/ppermute | solution.py:28
  16.1 12.9 %collective-permute-start.1 = (bf16[2,256,256]{2,1,0:T(8,128)(2,1)S(1)}, bf16[2,256,256]{2,1,0:T(8,128)(2,1)S(1)}, u32[]{:S(2)}, u32[]{:S(2)}) collective-permute-start(bf16[2,256,256]{2,1,0:T(8,128)(2,1)S(1)} %shard_map.59), channel_id=1, source_target_pairs={{8,0},{12,4},{16,8},{20,12},{24,16},{28,20},{32,24},{36,28},{40,32... | collective-permute-start | bytes 786440 | tf_op jit(solution)/shard_map/ppermute | solution.py:28
  29.1 4.2 %collective-permute-start.2 = (bf16[6,256,256]{2,1,0:T(8,128)(2,1)S(1)}, bf16[6,256,256]{2,1,0:T(8,128)(2,1)S(1)}, u32[]{:S(2)}, u32[]{:S(2)}) collective-permute-start(bf16[6,256,256]{2,1,0:T(8,128)(2,1)S(1)} %shard_map.60), channel_id=1, source_target_pairs={{0,4},{4,0},{8,12},{12,8},{16,20},{20,16},{24,28},{28,24},{32,36},... | collective-permute-start | bytes 2359304 | tf_op jit(solution)/shard_map/ppermute | solution.py:33
  34.0 14.0 %collective-permute-start.3 = (bf16[2,256,256]{2,1,0:T(8,128)(2,1)}, bf16[2,256,256]{2,1,0:T(8,128)(2,1)S(1)}, u32[]{:S(2)}, u32[]{:S(2)}) collective-permute-start(bf16[2,256,256]{2,1,0:T(8,128)(2,1)} %get-tuple-element.26), channel_id=1, source_target_pairs={{0,16},{4,20},{8,24},{12,28},{16,32},{20,36},{24,40},{28,44},{32,4... | collective-permute-start | bytes 786440 | tf_op jit(solution)/shard_map/ppermute | solution.py:28
  36.7 13.3 %copy-start.1 = (f32[256]{0:T(256)S(1)}, f32[256]{0:T(256)}, u32[]{:S(2)}) copy-start(f32[256]{0:T(256)} %param.9) | copy-start | bytes 3076
  36.7 13.3 %copy-start = (f32[256,64]{0,1:T(8,128)S(1)}, f32[256,64]{0,1:T(8,128)}, u32[]{:S(2)}) copy-start(f32[256,64]{0,1:T(8,128)} %param.8) | copy-start | bytes 196612
  38.1 13.1 %all-to-all-start.1 = ((bf16[4,256,256]{2,1,0:T(8,128)(2,1)}), bf16[4,256,256]{2,1,0:T(8,128)(2,1)S(1)}, u32[]{:S(2)}, u32[]{:S(2)}) async-start(bf16[4,256,256]{2,1,0:T(8,128)(2,1)} %shard_map.64), calls=%async_computation.1 | async-start | bytes 1048576 | tf_op jit(solution)/shard_map/all_to_all | solution.py:323
  48.1 10.2 %collective-permute-start.4 = (bf16[256,256]{1,0:T(8,128)(2,1)S(1)}, bf16[256,256]{1,0:T(8,128)(2,1)S(1)}, u32[]{:S(2)}, u32[]{:S(2)}) collective-permute-start(bf16[256,256]{1,0:T(8,128)(2,1)S(1)} %shard_map.65), channel_id=1, source_target_pairs={{0,8},{4,12},{8,16},{12,20},{16,24},{20,28},{24,32},{28,36},{32,40... | collective-permute-start | bytes 393224 | tf_op jit(solution)/shard_map/ppermute | solution.py:28
  59.4 18.1 %all-to-all-start.2 = ((bf16[4,256,256]{2,1,0:T(8,128)(2,1)}), bf16[4,256,256]{2,1,0:T(8,128)(2,1)S(1)}, u32[]{:S(2)}, u32[]{:S(2)}) async-start(bf16[4,256,256]{2,1,0:T(8,128)(2,1)} %shard_map.68), calls=%async_computation.2 | async-start | bytes 1048576 | tf_op jit(solution)/shard_map/all_to_all | solution.py:314
  64.2 8.4 %collective-permute-start.5 = (bf16[256,256]{1,0:T(8,128)(2,1)S(1)}, bf16[256,256]{1,0:T(8,128)(2,1)S(1)}, u32[]{:S(2)}, u32[]{:S(2)}) collective-permute-start(bf16[256,256]{1,0:T(8,128)(2,1)S(1)} %get-tuple-element.30.cur_ref), channel_id=1, source_target_pairs={{16,0},{20,4},{24,8},{28,12},{32,16},{36,20},{40,24},{44,28},{48,3... | collective-permute-start | bytes 393224 | tf_op jit(solution)/shard_map/ppermute | solution.py:28
  72.6 8.3 %collective-permute-start.6 = (bf16[2,256,256]{2,1,0:T(8,128)(2,1)S(1)}, bf16[2,256,256]{2,1,0:T(8,128)(2,1)S(1)}, u32[]{:S(2)}, u32[]{:S(2)}) collective-permute-start(bf16[2,256,256]{2,1,0:T(8,128)(2,1)S(1)} %shard_map.70), channel_id=1, source_target_pairs={{8,0},{12,4},{16,8},{20,12},{24,16},{28,20},{32,24},{36,28},{40,32... | collective-permute-start | bytes 786440 | tf_op jit(solution)/shard_map/ppermute | solution.py:28
  80.9 4.2 %collective-permute-start.7 = (bf16[6,256,256]{2,1,0:T(8,128)(2,1)S(1)}, bf16[6,256,256]{2,1,0:T(8,128)(2,1)S(1)}, u32[]{:S(2)}, u32[]{:S(2)}) collective-permute-start(bf16[6,256,256]{2,1,0:T(8,128)(2,1)S(1)} %shard_map.71), channel_id=1, source_target_pairs={{0,4},{4,0},{8,12},{12,8},{16,20},{20,16},{24,28},{28,24},{32,36},... | collective-permute-start | bytes 2359304 | tf_op jit(solution)/shard_map/ppermute | solution.py:33
  85.2 13.8 %collective-permute-start.8 = (bf16[2,256,256]{2,1,0:T(8,128)(2,1)S(1)}, bf16[2,256,256]{2,1,0:T(8,128)(2,1)S(1)}, u32[]{:S(2)}, u32[]{:S(2)}) collective-permute-start(bf16[2,256,256]{2,1,0:T(8,128)(2,1)S(1)} %get-tuple-element.34), channel_id=1, source_target_pairs={{0,16},{4,20},{8,24},{12,28},{16,32},{20,36},{24,40},{28,44},{32,4... | collective-permute-start | bytes 786440 | tf_op jit(solution)/shard_map/ppermute | solution.py:28
  88.4 13.2 %all-to-all-start.3 = ((bf16[4,256,256]{2,1,0:T(8,128)(2,1)}), bf16[4,256,256]{2,1,0:T(8,128)(2,1)S(1)}, u32[]{:S(2)}, u32[]{:S(2)}) async-start(bf16[4,256,256]{2,1,0:T(8,128)(2,1)} %shard_map.75), calls=%async_computation.3 | async-start | bytes 1048576 | tf_op jit(solution)/shard_map/all_to_all | solution.py:323
  99.0 10.2 %collective-permute-start.9 = (bf16[256,256]{1,0:T(8,128)(2,1)S(1)}, bf16[256,256]{1,0:T(8,128)(2,1)S(1)}, u32[]{:S(2)}, u32[]{:S(2)}) collective-permute-start(bf16[256,256]{1,0:T(8,128)(2,1)S(1)} %shard_map.76), channel_id=1, source_target_pairs={{0,8},{4,12},{8,16},{12,20},{16,24},{20,28},{24,32},{28,36},{32,40... | collective-permute-start | bytes 393224 | tf_op jit(solution)/shard_map/ppermute | solution.py:28
